TPU v7x, 32 devices: a whole 2x2x4 slice. The times are simulated.
32 devices in a mesh: seq: 8 (over z, y), head: 4 (over x, core).
Axes of the slice: x: 2, y: 2, z: 4, core: 2. Of those that a mesh axis runs over, the one named last changes fastest.
Arguments:
- mixer_input: bfloat16 [16384, 5120], P('seq', 'head'), may hold values from -6 to 6
- write_map: bfloat16 [16384, 128], P('seq', 'head'), may hold values from -0.5 to 0.5
- read_map: bfloat16 [16384, 128], P('seq', 'head'), may hold values from -6 to 6
- step_size: float32 [80, 16384], P('head', 'seq'), may hold values from 0 to 0.5
- log_decay: float32 [80, 16384], P('head', 'seq'), may hold values from -3 to 0
- skip_gain: float32 [80], P('head'), may hold values from 0.5 to 1.5
- level_table: float32 [7, 8], replicated, may hold values from 0.5 to 2
- level_index: int32 [7, 16384], P(None, 'seq'), may hold values from 0 to 7
Outputs:
- mixer_output: bfloat16 [16384, 5120], P('seq', 'head')
All inputs are finite; a program needn't handle non-finite values.
Results may differ from a plain program's by a relative error of at most 0.0043.
Values may be sent and summed in bfloat16 or wider, within the bound.
No kernel may reach another device: no remote copies, remote signals or barrier semaphores. Data moves between devices by JAX's collectives and lax.ppermute only.
A program may use at most 256 MiB of HBM per device.

v0:
```python
import jax
import jax.numpy as jnp
from jax import lax
from jax.sharding import PartitionSpec as P

BLOCK = 256


def from_partner(x, axis, stride):
    return lax.ppermute(x, axis, [(i, i ^ 1 << stride) for i in range(lax.axis_size(axis))])


def pick_row(source, where_at):
    return lax.dynamic_index_in_dim(source, where_at, 0, keepdims=False)


def tree_merge(lower_state, lower_total, upper_state, upper_total):
    merged = jnp.exp(upper_total)[..., None, None] * lower_state + upper_state
    return (merged, lower_total + upper_total)


def pair_merge(state_rows, total_rows):
    paired_state = state_rows.reshape((-1, 2) + state_rows.shape[1:])
    paired_total = total_rows.reshape((-1, 2) + total_rows.shape[1:])
    return tree_merge(
        paired_state[:, 0], paired_total[:, 0], paired_state[:, 1], paired_total[:, 1]
    )


def on_device(
    mixer_input, write_map, read_map, step_size, log_decay, skip_gain, level_table, level_index
):
    token_count = mixer_input.shape[0]
    head_count = log_decay.shape[0]
    head_width = mixer_input.shape[1] // head_count
    block_count = token_count // BLOCK
    local_bits = block_count.bit_length() - 1
    device_bits = lax.axis_size("seq").bit_length() - 1
    level_count = level_table.shape[0]
    my_rank = lax.axis_index("seq")
    write_rows, read_rows = (
        lax.all_gather(write_map, "head", axis=1, tiled=True),
        lax.all_gather(read_map, "head", axis=1, tiled=True),
    )
    state_width = write_rows.shape[1]
    level_weight = jnp.zeros(level_index.shape, jnp.float32)
    for entry in range(level_table.shape[1]):
        level_weight = level_weight + jnp.where(
            level_index == entry, level_table[:, entry : entry + 1], 0.0
        )
    decay_sum = jnp.cumsum(log_decay.reshape(head_count, block_count, BLOCK), axis=2).transpose(
        1, 0, 2
    )
    block_decay = decay_sum[:, :, -1]
    step_blocks = step_size.reshape(head_count, block_count, BLOCK).transpose(1, 0, 2)
    causal = jnp.arange(BLOCK)[:, None] >= jnp.arange(BLOCK)[None, :]

    def block_rows(block_index, source):
        return lax.dynamic_slice_in_dim(source, block_index * BLOCK, BLOCK, 0)

    def block_input(block_index):
        return block_rows(block_index, mixer_input).reshape(BLOCK, head_count, head_width)

    def intra_block(block_index):
        scores = lax.dot_general(
            block_rows(block_index, read_rows),
            block_rows(block_index, write_rows),
            (((1,), (1,)), ((), ())),
            preferred_element_type=jnp.float32,
        )
        sums_here = pick_row(decay_sum, block_index)
        gap = jnp.where(causal[None], sums_here[:, :, None] - sums_here[:, None, :], -jnp.inf)
        mixing = (scores[None] * jnp.exp(gap)).astype(jnp.bfloat16)
        inputs = (
            block_input(block_index) * pick_row(step_blocks, block_index).T[:, :, None]
        ).astype(jnp.bfloat16)
        return jnp.einsum("hts,shp->thp", mixing, inputs, preferred_element_type=jnp.float32)

    def state_block(block_index):
        sums_here = pick_row(decay_sum, block_index)
        factor = pick_row(step_blocks, block_index) * jnp.exp(sums_here[:, -1:] - sums_here)
        end_inputs = (block_input(block_index) * factor.T[:, :, None]).astype(jnp.bfloat16)
        return jnp.einsum(
            "sn,shp->hnp",
            block_rows(block_index, write_rows),
            end_inputs,
            preferred_element_type=jnp.float32,
        )

    block_ids = jnp.arange(block_count, dtype=jnp.int32)
    trees = [lax.map(state_block, block_ids)]
    totals = [block_decay]
    for bit_pos in range(local_bits):
        merged_state, merged_total = pair_merge(trees[-1], totals[-1])
        trees.append(merged_state)
        totals.append(merged_total)
    own_state = trees[-1][0]
    own_total = totals[-1][0]
    flags = []
    for section_bit in range(device_bits):
        flags.append((my_rank >> section_bit & 1).astype(jnp.float32))
    buckets = []
    bucket_totals = []
    mine_state, mine_total = (own_state, own_total)
    for section_bit in range(device_bits):
        other_state, other_total = from_partner((mine_state, mine_total), "seq", section_bit)
        buckets.append(other_state)
        bucket_totals.append(other_total)
        if section_bit + 1 < device_bits:
            upper = flags[section_bit] > 0.5
            mine_state, mine_total = tree_merge(
                jnp.where(upper, other_state, mine_state),
                jnp.where(upper, other_total, mine_total),
                jnp.where(upper, mine_state, other_state),
                jnp.where(upper, mine_total, other_total),
            )

    def read_block(block_index):
        running = jnp.zeros((head_count,), jnp.float32)
        states = []
        for bit_pos in range(local_bits):
            shifted = block_index >> bit_pos
            bit_flag = (shifted & 1).astype(jnp.float32)
            bucket_at = jnp.maximum(shifted - 1, 0)
            states.append(
                (bit_flag * jnp.exp(running))[:, None, None] * pick_row(trees[bit_pos], bucket_at)
            )
            running = running + bit_flag * pick_row(totals[bit_pos], bucket_at)
        for section_bit in range(device_bits):
            states.append(
                (flags[section_bit] * jnp.exp(running))[:, None, None] * buckets[section_bit]
            )
            running = running + flags[section_bit] * bucket_totals[section_bit]
        stacked = jnp.stack(states, axis=1).reshape(
            head_count, (level_count - 1) * state_width, head_width
        )
        weights_here = lax.dynamic_slice_in_dim(level_weight, block_index * BLOCK, BLOCK, 1)
        read_here = block_rows(block_index, read_rows).astype(jnp.float32)
        queries = (weights_here[1:].T[:, :, None] * read_here[:, None, :]).reshape(
            BLOCK, (level_count - 1) * state_width
        )
        inter_part = jnp.einsum(
            "tk,hkp->thp",
            queries,
            stacked,
            precision=lax.Precision.HIGHEST,
            preferred_element_type=jnp.float32,
        )
        intra_part = intra_block(block_index)
        result = (
            weights_here[0][:, None, None] * intra_part
            + jnp.exp(pick_row(decay_sum, block_index)).T[:, :, None] * inter_part
            + skip_gain[None, :, None] * block_input(block_index)
        )
        return result.astype(jnp.bfloat16)

    mixed = lax.map(read_block, block_ids)
    return mixed.reshape(token_count, head_count * head_width)


def solution(mesh):
    placed = (
        P("seq", "head"),
        P("seq", "head"),
        P("seq", "head"),
        P("head", "seq"),
        P("head", "seq"),
        P("head"),
        P(),
        P(None, "seq"),
    )
    return jax.shard_map(
        on_device, mesh=mesh, in_specs=placed, out_specs=P("seq", "head"), check_vma=False
    )
```

profile of v0, /device:TPU:0, one launch (start us, length us, event | category | flops | bytes accessed | tf_op | source)
XLA Modules:
  0.0 432.0 jit_solution(9415984456963590949)
XLA Ops:
  1.1 11.3 %reduce-window.6 = f32[20,8,2,128]{3,1,2,0:T(8,128)S(1)} reduce-window(f32[20,8,2,128]{3,1,2,0:T(8,128)S(1)} %copy.60, f32[]{:T(128)} %constant.130.clone.1), window={size=1x1x1x128 pad=0_0x0_0x0_0x127_0}, to_apply=%region_0.1 | reduce-window | flops 5201920 | bytes 327684 | tf_op jit(solution)/shard_map/reduce-window
  13.6 8.0 %copy.71 = bf16[2048,1280]{0,1:T(8,128)(2,1)} copy(bf16[2048,1280]{1,0:T(8,128)(2,1)} %param.12) | data formatting | bytes 10485760
  21.6 8.6 %all_gather.7 = bf16[2048,128]{0,1:T(8,128)(2,1)S(1)} all-gather(bf16[2048,32]{0,1:T(8,128)(2,1)S(1)} %copy-done.6), channel_id=1, replica_groups=mesh['seq'=8,'head'=4] {'head'}, dimensions={1}, use_global_device_ids=true | all-gather | bytes 655360 | tf_op jit(solution)/shard_map/all_gather | solution.py:42
  33.0 61.9 %while.24 = (s32[]{:T(128)}, f32[8,20,128,64]{2,3,1,0:T(8,128)}, s32[8]{0:T(128)S(1)}, bf16[2048,1280]{0,1:T(8,128)(2,1)}, f32[8,20,256]{2,0,1:T(8,128)}, /*inde...) while((s32[]{:T(128)}, f32[8,20,128,64]{2,3,1,0:T(8,128)}, ...), condition=%wide.region_3.4_spmd, body=%wide.region_2.3_spmd.sunk | while | flops 84879368 | bytes 2974669 | solution.py:91
  77.4 2.1 fusion.80
  94.9 5.8 %fusion.59 = (f32[4,1,20,128,64]{3,4,2,1,0:T(8,128)}, f32[4,1,20,128,64]{3,4,2,1,0:T(8,128)}) fusion(f32[4,2,20,128,64]{3,4,2,1,0:T(8,128)} %bitcast.244), kind=kLoop, calls=%fused_computation.118 | loop fusion | bytes 10485760 | tf_op jit(solution)/shard_map/slice | solution.py:26
  100.9 2.8 fusion.47
  107.3 15.0 %collective-permute-done.1 = f32[20]{0:T(128)S(1)} collective-permute-done((f32[20]{0:T(128)S(1)}, f32[20]{0:T(128)S(1)}, u32[]{:S(2)}, u32[]{:S(2)}) %collective-permute-start.1) | collective-permute-done | bytes 112 | tf_op jit(solution)/shard_map/ppermute | solution.py:10
  125.5 4.3 %fusion.46 = f32[4,20,128,64]{2,3,1,0:T(8,128)} fusion(f32[4,20]{1,0:T(4,128)S(1)} %bitcast.263, f32[4,2,20,128,64]{3,4,2,1,0:T(8,128)} %bitcast.245), kind=kLoop, calls=%fused_computation.80 | loop fusion | flops 1310720 | bytes 7864640 | tf_op jit(solution)/shard_map/add | solution.py:18
  130.3 8.5 %collective-permute-done.3 = f32[20]{0:T(128)S(1)} collective-permute-done((f32[20]{0:T(128)S(1)}, f32[20]{0:T(128)S(1)}, u32[]{:S(2)}, u32[]{:S(2)}) %collective-permute-start.3) | collective-permute-done | bytes 112 | tf_op jit(solution)/shard_map/ppermute | solution.py:10
  138.9 2.7 collective-permute-start.4
  141.9 7.2 %all_gather.6 = bf16[2048,128]{0,1:T(8,128)(2,1)} all-gather(bf16[2048,32]{0,1:T(8,128)(2,1)S(1)} %copy-done.7), channel_id=1, replica_groups=mesh['seq'=8,'head'=4] {'head'}, dimensions={1}, use_global_device_ids=true | all-gather | bytes 655360 | tf_op jit(solution)/shard_map/all_gather | solution.py:43
  149.9 19.3 %collective-permute-done.4 = f32[20,128,64]{1,2,0:T(8,128)} collective-permute-done((f32[20,128,64]{1,2,0:T(8,128)S(1)}, f32[20,128,64]{1,2,0:T(8,128)}, u32[]{:S(2)}, u32[]{:S(2)}) %collective-permute-start.4) | collective-permute-done | bytes 655392 | tf_op jit(solution)/shard_map/ppermute | solution.py:10
  169.2 244.2 %while.25 = (s32[]{:T(128)}, bf16[8,256,20,64]{1,3,2,0:T(8,128)(2,1)}, s32[8]{0:T(128)S(1)}, f32[7,2048]{1,0:T(8,128)}, bf16[2048,1280]{0,1:T(8,128)(2,1)}, /*in...) while((s32[]{:T(128)}, ...), condition=%wide.region_5.6_spmd.clone, body=%wide.region_4.5_spmd.clone.sunk | while | flops 3214246144 | bytes 19449572 | solution.py:157
  175.9 2.1 fusion.88
  193.2 6.4 %fusion.92 = bf16[8,256,20,64]{1,3,2,0:T(8,128)(2,1)} fusion(bf16[8,256,20,64]{1,3,2,0:T(8,128)(2,1)} %get-tuple-element.944, s32[]{:T(128)} %get-tuple-element.943, bf16[256,20,64]{0,2,1:T(8,128)(2,1)S(1)} %bitcast.242, f32[256,20,64]{0,2,1:T(8,128)S(1)} %fusion.86, f32[20,6,128,64]{2,3,1,0:T(8,128)} %fusion.91, f32[20]{0:T(128)S(1)} %get-tuple-element.998, ...), kind=kOutput, calls=%fused_computation.33.clone.1 | convolution fusion | flops 3022061568 | bytes 6711888 | tf_op jit(solution)/shard_map/while/body/eval_jaxpr/tk,hkp->thp/dot_general | solution.py:142
  206.4 2.1 fusion.88
  223.7 6.4 %fusion.92 = bf16[8,256,20,64]{1,3,2,0:T(8,128)(2,1)} fusion(bf16[8,256,20,64]{1,3,2,0:T(8,128)(2,1)} %get-tuple-element.944, s32[]{:T(128)} %get-tuple-element.943, bf16[256,20,64]{0,2,1:T(8,128)(2,1)S(1)} %bitcast.242, f32[256,20,64]{0,2,1:T(8,128)S(1)} %fusion.86, f32[20,6,128,64]{2,3,1,0:T(8,128)} %fusion.91, f32[20]{0:T(128)S(1)} %get-tuple-element.998, ...), kind=kOutput, calls=%fused_computation.33.clone.1 | convolution fusion | flops 3022061568 | bytes 6711888 | tf_op jit(solution)/shard_map/while/body/eval_jaxpr/tk,hkp->thp/dot_general | solution.py:142
  236.9 2.1 fusion.88
  254.2 6.4 %fusion.92 = bf16[8,256,20,64]{1,3,2,0:T(8,128)(2,1)} fusion(bf16[8,256,20,64]{1,3,2,0:T(8,128)(2,1)} %get-tuple-element.944, s32[]{:T(128)} %get-tuple-element.943, bf16[256,20,64]{0,2,1:T(8,128)(2,1)S(1)} %bitcast.242, f32[256,20,64]{0,2,1:T(8,128)S(1)} %fusion.86, f32[20,6,128,64]{2,3,1,0:T(8,128)} %fusion.91, f32[20]{0:T(128)S(1)} %get-tuple-element.998, ...), kind=kOutput, calls=%fused_computation.33.clone.1 | convolution fusion | flops 3022061568 | bytes 6711888 | tf_op jit(solution)/shard_map/while/body/eval_jaxpr/tk,hkp->thp/dot_general | solution.py:142
  267.4 2.1 fusion.88
  284.7 6.4 %fusion.92 = bf16[8,256,20,64]{1,3,2,0:T(8,128)(2,1)} fusion(bf16[8,256,20,64]{1,3,2,0:T(8,128)(2,1)} %get-tuple-element.944, s32[]{:T(128)} %get-tuple-element.943, bf16[256,20,64]{0,2,1:T(8,128)(2,1)S(1)} %bitcast.242, f32[256,20,64]{0,2,1:T(8,128)S(1)} %fusion.86, f32[20,6,128,64]{2,3,1,0:T(8,128)} %fusion.91, f32[20]{0:T(128)S(1)} %get-tuple-element.998, ...), kind=kOutput, calls=%fused_computation.33.clone.1 | convolution fusion | flops 3022061568 | bytes 6711888 | tf_op jit(solution)/shard_map/while/body/eval_jaxpr/tk,hkp->thp/dot_general | solution.py:142
  297.9 2.1 fusion.88
  315.2 6.4 %fusion.92 = bf16[8,256,20,64]{1,3,2,0:T(8,128)(2,1)} fusion(bf16[8,256,20,64]{1,3,2,0:T(8,128)(2,1)} %get-tuple-element.944, s32[]{:T(128)} %get-tuple-element.943, bf16[256,20,64]{0,2,1:T(8,128)(2,1)S(1)} %bitcast.242, f32[256,20,64]{0,2,1:T(8,128)S(1)} %fusion.86, f32[20,6,128,64]{2,3,1,0:T(8,128)} %fusion.91, f32[20]{0:T(128)S(1)} %get-tuple-element.998, ...), kind=kOutput, calls=%fused_computation.33.clone.1 | convolution fusion | flops 3022061568 | bytes 6711888 | tf_op jit(solution)/shard_map/while/body/eval_jaxpr/tk,hkp->thp/dot_general | solution.py:142
  328.4 2.1 fusion.88
  345.7 6.4 %fusion.92 = bf16[8,256,20,64]{1,3,2,0:T(8,128)(2,1)} fusion(bf16[8,256,20,64]{1,3,2,0:T(8,128)(2,1)} %get-tuple-element.944, s32[]{:T(128)} %get-tuple-element.943, bf16[256,20,64]{0,2,1:T(8,128)(2,1)S(1)} %bitcast.242, f32[256,20,64]{0,2,1:T(8,128)S(1)} %fusion.86, f32[20,6,128,64]{2,3,1,0:T(8,128)} %fusion.91, f32[20]{0:T(128)S(1)} %get-tuple-element.998, ...), kind=kOutput, calls=%fused_computation.33.clone.1 | convolution fusion | flops 3022061568 | bytes 6711888 | tf_op jit(solution)/shard_map/while/body/eval_jaxpr/tk,hkp->thp/dot_general | solution.py:142
  376.2 6.4 %fusion.92 = bf16[8,256,20,64]{1,3,2,0:T(8,128)(2,1)} fusion(bf16[8,256,20,64]{1,3,2,0:T(8,128)(2,1)} %get-tuple-element.944, s32[]{:T(128)} %get-tuple-element.943, bf16[256,20,64]{0,2,1:T(8,128)(2,1)S(1)} %bitcast.242, f32[256,20,64]{0,2,1:T(8,128)S(1)} %fusion.86, f32[20,6,128,64]{2,3,1,0:T(8,128)} %fusion.91, f32[20]{0:T(128)S(1)} %get-tuple-element.998, ...), kind=kOutput, calls=%fused_computation.33.clone.1 | convolution fusion | flops 3022061568 | bytes 6711888 | tf_op jit(solution)/shard_map/while/body/eval_jaxpr/tk,hkp->thp/dot_general | solution.py:142
  389.5 2.1 fusion.88
  406.8 6.4 %fusion.92 = bf16[8,256,20,64]{1,3,2,0:T(8,128)(2,1)} fusion(bf16[8,256,20,64]{1,3,2,0:T(8,128)(2,1)} %get-tuple-element.944, s32[]{:T(128)} %get-tuple-element.943, bf16[256,20,64]{0,2,1:T(8,128)(2,1)S(1)} %bitcast.242, f32[256,20,64]{0,2,1:T(8,128)S(1)} %fusion.86, f32[20,6,128,64]{2,3,1,0:T(8,128)} %fusion.91, f32[20]{0:T(128)S(1)} %get-tuple-element.998, ...), kind=kOutput, calls=%fused_computation.33.clone.1 | convolution fusion | flops 3022061568 | bytes 6711888 | tf_op jit(solution)/shard_map/while/body/eval_jaxpr/tk,hkp->thp/dot_general | solution.py:142
  413.4 6.2 %copy.76 = bf16[8,256,20,64]{1,0,3,2:T(8,128)(2,1)S(1)} copy(bf16[8,256,20,64]{1,3,2,0:T(8,128)(2,1)} %get-tuple-element.405) | data formatting | bytes 10485760 | tf_op jit(solution)/shard_map/while | solution.py:157
  419.6 4.6 %copy.87 = bf16[160,8,8,256]{3,1,2,0:T(8,128)(2,1)} copy(bf16[160,8,8,256]{3,2,1,0:T(8,128)(2,1)S(1)} %bitcast.246) | data formatting | bytes 10485760
  424.1 7.9 %copy.77 = bf16[2048,1280]{1,0:T(8,128)(2,1)} copy(bf16[2048,1280]{0,1:T(8,128)(2,1)} %bitcast.247) | data formatting | bytes 10485760 | tf_op jit(solution)/shard_map/reshape | solution.py:158
  (451 shorter events, 194.6 us)
Async XLA Ops:
  13.6 17.7 %copy-start.5 = (f32[20,2048]{1,0:T(8,128)S(1)}, f32[20,2048]{1,0:T(8,128)}, u32[]{:S(2)}) copy-start(f32[20,2048]{1,0:T(8,128)} %param.15) | copy-start | bytes 491524
  105.2 17.1 %collective-permute-start = (f32[20,128,64]{1,2,0:T(8,128)S(1)}, f32[20,128,64]{1,2,0:T(8,128)S(1)}, u32[]{:S(2)}, u32[]{:S(2)}) collective-permute-start(f32[20,128,64]{1,2,0:T(8,128)S(1)} %fusion.50), channel_id=1, source_target_pairs={{0,4},{4,0},{8,12},{12,8},{16,20},{20,16},{24,28},{28,24},{1,5},{5... | collective-permute-start | bytes 1966088 | tf_op jit(solution)/shard_map/ppermute | solution.py:10
  106.7 15.6 %collective-permute-start.1 = (f32[20]{0:T(128)S(1)}, f32[20]{0:T(128)S(1)}, u32[]{:S(2)}, u32[]{:S(2)}) collective-permute-start(f32[20]{0:T(128)S(1)} %get-tuple-element.667), channel_id=1, source_target_pairs={{0,4},{4,0},{8,12},{12,8},{16,20},{20,16},{24,28},{28,24},{1,5},{5... | collective-permute-start | bytes 248 | tf_op jit(solution)/shard_map/ppermute | solution.py:10
  107.3 16.9 %copy-start.1 = (f32[2,2,20,128,64]{3,4,2,1,0:T(8,128)S(1)}, f32[2,2,20,128,64]{3,4,2,1,0:T(8,128)}, u32[]{:S(2)}) copy-start(f32[2,2,20,128,64]{3,4,2,1,0:T(8,128)} %copy-done) | copy-start | bytes 7864324
  122.5 16.2 %collective-permute-start.2 = (f32[20,128,64]{1,2,0:T(8,128)S(1)}, f32[20,128,64]{1,2,0:T(8,128)S(1)}, u32[]{:S(2)}, u32[]{:S(2)}) collective-permute-start(f32[20,128,64]{1,2,0:T(8,128)S(1)} %select_add_fusion.1), channel_id=1, source_target_pairs={{0,8},{4,12},{8,0},{12,4},{16,24},{20,28},{24,16},{28,20},{1,9},{5... | collective-permute-start | bytes 1966088 | tf_op jit(solution)/shard_map/ppermute | solution.py:10
  125.5 16.2 %copy-start.3 = (f32[7,8]{1,0:T(8,128)S(1)}, f32[7,8]{1,0:T(8,128)}, u32[]{:S(2)}) copy-start(f32[7,8]{1,0:T(8,128)} %param.18) | copy-start | bytes 676
  125.5 16.5 %copy-start.7 = (bf16[2048,32]{0,1:T(8,128)(2,1)S(1)}, bf16[2048,32]{0,1:T(8,128)(2,1)}, u32[]{:S(2)}) copy-start(bf16[2048,32]{0,1:T(8,128)(2,1)} %param.14) | copy-start | bytes 393220
  129.8 19.3 %copy-start.8 = (s32[7,2048]{1,0:T(8,128)S(1)}, s32[7,2048]{1,0:T(8,128)}, u32[]{:S(2)}) copy-start(s32[7,2048]{1,0:T(8,128)} %param.19) | copy-start | bytes 172036
  129.8 39.3 %copy-start.4 = (f32[20]{0:T(128)S(1)}, f32[20]{0:T(128)}, u32[]{:S(2)}) copy-start(f32[20]{0:T(128)} %param.17) | copy-start | bytes 244
  129.8 8.9 %collective-permute-start.3 = (f32[20]{0:T(128)S(1)}, f32[20]{0:T(128)S(1)}, u32[]{:S(2)}, u32[]{:S(2)}) collective-permute-start(f32[20]{0:T(128)S(1)} %get-tuple-element.665), channel_id=1, source_target_pairs={{0,8},{4,12},{8,0},{12,4},{16,24},{20,28},{24,16},{28,20},{1,9},{5... | collective-permute-start | bytes 248 | tf_op jit(solution)/shard_map/ppermute | solution.py:10
  138.9 30.2 %collective-permute-start.4 = (f32[20,128,64]{1,2,0:T(8,128)S(1)}, f32[20,128,64]{1,2,0:T(8,128)}, u32[]{:S(2)}, u32[]{:S(2)}) collective-permute-start(f32[20,128,64]{1,2,0:T(8,128)S(1)} %select_add_fusion), channel_id=1, source_target_pairs={{0,16},{4,20},{8,24},{12,28},{16,0},{20,4},{24,8},{28,12},{1,17},{... | collective-permute-start | bytes 1966088 | tf_op jit(solution)/shard_map/ppermute | solution.py:10
  169.2 9.9 %copy-start.9 = (f32[4,20]{1,0:T(4,128)}, f32[4,20]{1,0:T(4,128)S(1)}, u32[]{:S(2)}) copy-start(f32[4,20]{1,0:T(4,128)S(1)} %get-tuple-element.987) | copy-start | bytes 964 | tf_op jit(solution)/shard_map/while
  169.2 9.9 %copy-start.11 = (f32[2,20]{1,0:T(2,128)}, f32[2,20]{1,0:T(2,128)S(1)}, u32[]{:S(2)}) copy-start(f32[2,20]{1,0:T(2,128)S(1)} %get-tuple-element.990) | copy-start | bytes 484 | tf_op jit(solution)/shard_map/while
  169.2 9.9 %copy-start.13 = (f32[20]{0:T(128)}, f32[20]{0:T(128)S(1)}, u32[]{:S(2)}) copy-start(f32[20]{0:T(128)S(1)} %get-tuple-element.996) | copy-start | bytes 244 | tf_op jit(solution)/shard_map/while
  199.7 9.9 %copy-start.9 = (f32[4,20]{1,0:T(4,128)}, f32[4,20]{1,0:T(4,128)S(1)}, u32[]{:S(2)}) copy-start(f32[4,20]{1,0:T(4,128)S(1)} %get-tuple-element.987) | copy-start | bytes 964 | tf_op jit(solution)/shard_map/while
  199.7 9.9 %copy-start.11 = (f32[2,20]{1,0:T(2,128)}, f32[2,20]{1,0:T(2,128)S(1)}, u32[]{:S(2)}) copy-start(f32[2,20]{1,0:T(2,128)S(1)} %get-tuple-element.990) | copy-start | bytes 484 | tf_op jit(solution)/shard_map/while
  199.7 9.9 %copy-start.13 = (f32[20]{0:T(128)}, f32[20]{0:T(128)S(1)}, u32[]{:S(2)}) copy-start(f32[20]{0:T(128)S(1)} %get-tuple-element.996) | copy-start | bytes 244 | tf_op jit(solution)/shard_map/while
  230.2 9.9 %copy-start.9 = (f32[4,20]{1,0:T(4,128)}, f32[4,20]{1,0:T(4,128)S(1)}, u32[]{:S(2)}) copy-start(f32[4,20]{1,0:T(4,128)S(1)} %get-tuple-element.987) | copy-start | bytes 964 | tf_op jit(solution)/shard_map/while
  230.2 9.9 %copy-start.11 = (f32[2,20]{1,0:T(2,128)}, f32[2,20]{1,0:T(2,128)S(1)}, u32[]{:S(2)}) copy-start(f32[2,20]{1,0:T(2,128)S(1)} %get-tuple-element.990) | copy-start | bytes 484 | tf_op jit(solution)/shard_map/while
  230.2 9.9 %copy-start.13 = (f32[20]{0:T(128)}, f32[20]{0:T(128)S(1)}, u32[]{:S(2)}) copy-start(f32[20]{0:T(128)S(1)} %get-tuple-element.996) | copy-start | bytes 244 | tf_op jit(solution)/shard_map/while
  260.7 9.9 %copy-start.9 = (f32[4,20]{1,0:T(4,128)}, f32[4,20]{1,0:T(4,128)S(1)}, u32[]{:S(2)}) copy-start(f32[4,20]{1,0:T(4,128)S(1)} %get-tuple-element.987) | copy-start | bytes 964 | tf_op jit(solution)/shard_map/while
  260.7 9.9 %copy-start.11 = (f32[2,20]{1,0:T(2,128)}, f32[2,20]{1,0:T(2,128)S(1)}, u32[]{:S(2)}) copy-start(f32[2,20]{1,0:T(2,128)S(1)} %get-tuple-element.990) | copy-start | bytes 484 | tf_op jit(solution)/shard_map/while
  260.7 9.9 %copy-start.13 = (f32[20]{0:T(128)}, f32[20]{0:T(128)S(1)}, u32[]{:S(2)}) copy-start(f32[20]{0:T(128)S(1)} %get-tuple-element.996) | copy-start | bytes 244 | tf_op jit(solution)/shard_map/while
  291.2 9.9 %copy-start.9 = (f32[4,20]{1,0:T(4,128)}, f32[4,20]{1,0:T(4,128)S(1)}, u32[]{:S(2)}) copy-start(f32[4,20]{1,0:T(4,128)S(1)} %get-tuple-element.987) | copy-start | bytes 964 | tf_op jit(solution)/shard_map/while
  291.2 9.9 %copy-start.11 = (f32[2,20]{1,0:T(2,128)}, f32[2,20]{1,0:T(2,128)S(1)}, u32[]{:S(2)}) copy-start(f32[2,20]{1,0:T(2,128)S(1)} %get-tuple-element.990) | copy-start | bytes 484 | tf_op jit(solution)/shard_map/while
  321.7 9.9 %copy-start.9 = (f32[4,20]{1,0:T(4,128)}, f32[4,20]{1,0:T(4,128)S(1)}, u32[]{:S(2)}) copy-start(f32[4,20]{1,0:T(4,128)S(1)} %get-tuple-element.987) | copy-start | bytes 964 | tf_op jit(solution)/shard_map/while
  321.7 9.9 %copy-start.11 = (f32[2,20]{1,0:T(2,128)}, f32[2,20]{1,0:T(2,128)S(1)}, u32[]{:S(2)}) copy-start(f32[2,20]{1,0:T(2,128)S(1)} %get-tuple-element.990) | copy-start | bytes 484 | tf_op jit(solution)/shard_map/while
  352.2 9.9 %copy-start.9 = (f32[4,20]{1,0:T(4,128)}, f32[4,20]{1,0:T(4,128)S(1)}, u32[]{:S(2)}) copy-start(f32[4,20]{1,0:T(4,128)S(1)} %get-tuple-element.987) | copy-start | bytes 964 | tf_op jit(solution)/shard_map/while
  352.2 9.9 %copy-start.11 = (f32[2,20]{1,0:T(2,128)}, f32[2,20]{1,0:T(2,128)S(1)}, u32[]{:S(2)}) copy-start(f32[2,20]{1,0:T(2,128)S(1)} %get-tuple-element.990) | copy-start | bytes 484 | tf_op jit(solution)/shard_map/while
  352.2 9.9 %copy-start.13 = (f32[20]{0:T(128)}, f32[20]{0:T(128)S(1)}, u32[]{:S(2)}) copy-start(f32[20]{0:T(128)S(1)} %get-tuple-element.996) | copy-start | bytes 244 | tf_op jit(solution)/shard_map/while
  382.7 9.9 %copy-start.9 = (f32[4,20]{1,0:T(4,128)}, f32[4,20]{1,0:T(4,128)S(1)}, u32[]{:S(2)}) copy-start(f32[4,20]{1,0:T(4,128)S(1)} %get-tuple-element.987) | copy-start | bytes 964 | tf_op jit(solution)/shard_map/while
  382.7 9.9 %copy-start.11 = (f32[2,20]{1,0:T(2,128)}, f32[2,20]{1,0:T(2,128)S(1)}, u32[]{:S(2)}) copy-start(f32[2,20]{1,0:T(2,128)S(1)} %get-tuple-element.990) | copy-start | bytes 484 | tf_op jit(solution)/shard_map/while
  (53 other events, 330.0 us)
where the time goes:
time: 438 us; the launch traced here: 432 us
  local copies, waits for them, and re-layouts  116 us (26%)
  other arithmetic  106 us (24%)
  matrix products  88 us (20%)
  loops' own time  56.8 us (13%)
  waiting for transfers between devices  42.8 us (10%)
  blocking collectives  15.8 us (4%)
  starting transfers between devices  6.78 us (2%)
    while x40, other arithmetic  65.8 us
    dot_general x8, matrix products, read_block(): jnp.einsum('tk,hkp->thp', queries, stacked, precision=lax.Precision.HIGHE...  51.5 us
    ppermute x5, waiting for transfers between devices, from_partner(): lax.ppermute(x, axis, [(i, i ^ 1 << stride) for i in range(lax.axis_size(...  42.8 us
    another operation x1, loops' own time, on_device(): mixed = lax.map(read_block, block_ids)  36.5 us
    dynamic_slice x32, local copies, waits for them, and re-layouts, block_rows(): return lax.dynamic_slice_in_dim(source, block_index * BLOCK, BLOCK, 0)  25.9 us
    another operation x1, loops' own time, on_device(): trees = [lax.map(state_block, block_ids)]  20.3 us
    dynamic_slice x48, local copies, waits for them, and re-layouts, pick_row(): return lax.dynamic_index_in_dim(source, where_at, 0, keepdims=False)  18.4 us
    another operation x8, other arithmetic, read_block(): jnp.stack(states, axis=1)  16.6 us
  transfers between devices with their start and end apart: 5, of which 3 were waited for; matrix products, arithmetic and copies ran while one was open for 2% of the time, Pallas kernels for 0%

commit v1 on v0

v1 whole, which is shorter than its diff:
```python
import functools

import jax
import jax.numpy as jnp
from jax import lax
from jax.experimental import pallas as pl
from jax.experimental.pallas import tpu as pltpu
from jax.sharding import PartitionSpec as P

BLOCK = 256
HALF = BLOCK // 2
LANES = 128
LOG2E = 1.4426950408889634
F32 = jnp.float32
BF16 = jnp.bfloat16
NT = (((1,), (1,)), ((), ()))
NN = (((1,), (0,)), ((), ()))
TN = (((0,), (0,)), ((), ()))


def dot(a, b, dims=NN):
    return lax.dot_general(a, b, dims, preferred_element_type=F32)


def three(a):
    high = a.astype(BF16)
    rest = a - high.astype(F32)
    middle = rest.astype(BF16)
    return high, middle, (rest - middle.astype(F32)).astype(BF16)


def exact_left(mask, a):
    high, middle, low = three(a)
    return (dot(mask, low, NT) + dot(mask, middle, NT)) + dot(mask, high, NT)


def exact_right(a, mask):
    high, middle, low = three(a)
    return (dot(low, mask, NT) + dot(middle, mask, NT)) + dot(high, mask, NT)


def spread(padded, heads, width, per_head):
    row = lax.broadcasted_iota(jnp.int32, (2 * padded, width), 0)
    lane = lax.broadcasted_iota(jnp.int32, (2 * padded, width), 1)
    row = jnp.where(row >= padded, row - padded, row)
    own = (row * per_head <= lane) & (lane < (row + 1) * per_head) & (row < heads)
    return own.astype(F32).astype(BF16)


def pair_up(value, padded):
    lane = lax.broadcasted_iota(jnp.int32, value.shape, 1)
    high = value.astype(BF16).astype(F32)
    return jnp.where(lane < padded, high, value - high).astype(BF16)


def prep_kernel(
    heads, padded, width, log_decay, step_size, level_index, level_table,
    cum_t, cum_h, f_step, f_end, f_off, f_cum, f_run, f_total, weight_t, weight_h, rows,
    decay_two, step_two, sums,
):
    tokens = log_decay.shape[1]
    blocks = tokens // BLOCK
    per_head = width // heads
    decay_two[...] = jnp.zeros_like(decay_two)
    step_two[...] = jnp.zeros_like(step_two)
    for base in (0, padded):
        decay_two[base : base + heads, :] = log_decay[...]
        step_two[base : base + heads, :] = step_size[...]
    t_at = lax.broadcasted_iota(jnp.int32, (BLOCK, BLOCK), 0)
    s_at = lax.broadcasted_iota(jnp.int32, (BLOCK, BLOCK), 1)
    lower = (t_at >= s_at).astype(F32).astype(BF16)
    same = (t_at == s_at).astype(F32).astype(BF16)
    weight = jnp.zeros(level_index.shape, F32)
    index = level_index[...]
    for entry in range(level_table.shape[1]):
        weight = weight + jnp.where(index == entry, level_table[:, entry : entry + 1], 0.0)
    weight_h[...] = weight
    for c in range(blocks):
        at = slice(c * BLOCK, (c + 1) * BLOCK)
        sums[at, :] = exact_left(lower, decay_two[:, at])
        cum_h[:, at] = exact_right(decay_two[0:padded, at], lower) * LOG2E
        weight_t[at, :] = exact_left(same, weight_h[:, at])
    before = [jnp.zeros((1, 2 * padded), F32)]
    ends = []
    for c in range(blocks):
        ends.append(sums[(c + 1) * BLOCK - 1 : (c + 1) * BLOCK, :])
        before.append(before[-1] + ends[-1])
    total = before[-1]
    after = [jnp.zeros((1, 2 * padded), F32)]
    for c in reversed(range(blocks)):
        after.append(after[-1] + ends[c])
    after = after[::-1]
    for c in range(blocks):
        at = slice(c * BLOCK, (c + 1) * BLOCK)
        cum = sums[at, :]
        step = exact_left(same, step_two[:, at])
        cum_t[at, :] = cum * LOG2E
        f_step[at, :] = pair_up(step, padded)
        to_end = jnp.exp(ends[c] - cum)
        f_end[at, :] = pair_up(step * to_end, padded)
        f_total[at, :] = pair_up(step * jnp.exp((ends[c] - cum) + after[c + 1]), padded)
        f_cum[at, :] = pair_up(jnp.exp(cum), padded)
        f_run[at, :] = pair_up(jnp.exp(cum + before[c]), padded)
        middle = sums[c * BLOCK + HALF - 1 : c * BLOCK + HALF, :]
        first = cum[:HALF]
        f_off[c * BLOCK : c * BLOCK + HALF, :] = pair_up(
            step[:HALF] * jnp.exp(middle - first), padded
        )
        f_off[c * BLOCK + HALF : (c + 1) * BLOCK, :] = pair_up(jnp.exp(cum[HALF:] - middle), padded)
    where = lax.broadcasted_iota(jnp.int32, (rows.shape[0], 2 * padded), 0)
    table = jnp.zeros((rows.shape[0], 2 * padded), F32)
    for c in range(blocks):
        table = jnp.where(where == c, ends[c], table)
    table = jnp.where(where == blocks, total, table)
    rows[...] = dot(pair_up(jnp.exp(table), padded), spread(padded, heads, width, per_head))


def state_kernel(heads, padded, tile, mixer, factor, write_t, rows, mine, mine_exp, payload):
    width = mixer.shape[1]
    state = write_t.shape[0]
    blocks = pl.num_programs(0)
    c = pl.program_id(0)
    wide = spread(padded, heads, width, width // heads)

    @pl.when(c == 0)
    def _():
        mine[...] = jnp.zeros_like(mine)

    for left in range(0, width, tile):
        at = slice(left, left + tile)
        scaled = (mixer[:, at].astype(F32) * dot(factor[...], wide[:, at])).astype(BF16)
        mine[:, at] += dot(write_t[...], scaled)

    @pl.when(c == blocks - 1)
    def _():
        row_count = payload.shape[0] - state
        total = rows[blocks_row(rows) : blocks_row(rows) + 1, :]
        payload[0:state, :] = mine[...].astype(BF16)
        payload[state:, :] = exp_rows(total, row_count)
        mine_exp[...] = jnp.broadcast_to(total, mine_exp.shape)


def blocks_row(rows):
    return rows.shape[0] - 8


def exp_rows(total, count):
    where = lax.broadcasted_iota(jnp.int32, (count, total.shape[1]), 0)
    high = total.astype(BF16).astype(F32)
    return jnp.where(where == 0, high, jnp.where(where == 1, total - high, 0.0)).astype(BF16)


def merge_kernel(flags, bit, received, mine, mine_exp, merged, merged_exp, payload):
    state = mine.shape[0]
    extra = received[state:, :].astype(F32)
    other_exp = extra[0:1] + extra[1:2]
    own_exp = mine_exp[0:1, :]
    upper = (jnp.zeros((1, mine.shape[1]), jnp.int32) + flags[bit]) > 0
    own_scale = jnp.where(upper, 1.0, other_exp)
    other_scale = jnp.where(upper, own_exp, 1.0)
    new = own_scale * mine[...] + other_scale * received[0:state, :].astype(F32)
    merged[...] = new
    total = own_exp * other_exp
    merged_exp[...] = jnp.broadcast_to(total, merged_exp.shape)
    payload[0:state, :] = new.astype(BF16)
    payload[state:, :] = exp_rows(total, payload.shape[0] - state)


def local_kernel(
    heads, padded, tile, bits, first, mixer, write_t, read_t, cum_t, cum_h, f_step, f_end, f_off,
    f_cum, weight_t, weight_h, rows, skip, slots_in, base, slots, scores, inter, fresh,
):
    width = mixer.shape[1]
    per_head = width // heads
    g = pl.program_id(0)
    c = first + g
    wide = spread(padded, heads, width, per_head)

    @pl.when(g == 0)
    def _():
        slots[...] = slots_in[...]

    for bit in range(bits):

        @pl.when((c >> bit) & 1 == 1)
        def _(bit=bit):
            query = (read_t[...].astype(F32) * weight_h[bit + 1 : bit + 2, :]).astype(BF16)
            part = dot(query, slots[bit].astype(BF16), TN)
            if bit == 0:
                inter[...] = part
            else:

                @pl.when(c & ((1 << bit) - 1) == 0)
                def _():
                    inter[...] = part

                @pl.when(c & ((1 << bit) - 1) != 0)
                def _():
                    inter[...] += part

    @pl.when(c == 0)
    def _():
        inter[...] = jnp.zeros_like(inter)

    t_at = lax.broadcasted_iota(jnp.int32, (BLOCK, BLOCK), 0)
    s_at = lax.broadcasted_iota(jnp.int32, (BLOCK, BLOCK), 1)
    weighted = dot(read_t[...], write_t[...], TN) * weight_t[:, 0:1]
    scores[...] = jnp.where(t_at >= s_at, weighted, 0.0)
    off_scores = scores[HALF:, :HALF].astype(BF16)
    lane = lax.broadcasted_iota(jnp.int32, (HALF, LANES), 1)
    heads_here = LANES // per_head
    for left in range(0, width, tile):
        at = slice(left, left + tile)
        mixer_f = mixer[:, at].astype(F32)
        inputs = (mixer_f * dot(f_step[...], wide[:, at])).astype(BF16)
        off = dot(f_off[...], wide[:, at])
        off_inputs = (mixer_f[:HALF] * off[:HALF]).astype(BF16)
        off_part = dot(off_scores, off_inputs) * off[HALF:]
        rest = inter[:, at] * dot(f_cum[...], wide[:, at]) + skip[:, at] * mixer_f
        end_inputs = (mixer_f * dot(f_end[...], wide[:, at])).astype(BF16)
        fresh[:, at] = dot(write_t[...], end_inputs)
        for inner in range(0, tile, LANES):
            lanes = slice(inner, inner + LANES)
            out = slice(left + inner, left + inner + LANES)
            head = (left + inner) // per_head
            for half in range(2):
                rows_at = slice(half * HALF, (half + 1) * HALF)
                here = inputs[rows_at, lanes].astype(F32)
                left_side = []
                right_side = []
                for k in range(heads_here):
                    gap = cum_t[rows_at, head + k : head + k + 1] - cum_h[head + k : head + k + 1, rows_at]
                    mixing = scores[rows_at, rows_at] * jnp.exp2(jnp.minimum(gap, 0.0))
                    left_side.append(mixing.astype(BF16))
                    own = (lane >= k * per_head) & (lane < (k + 1) * per_head)
                    right_side.append(jnp.where(own, here, 0.0).astype(BF16))
                part = dot(jnp.concatenate(left_side, 1), jnp.concatenate(right_side, 0))
                part = part + rest[rows_at, lanes]
                if half == 1:
                    part = part + off_part[:, lanes]
                base[rows_at, out] = part

    shrink = rows[pl.ds(c, 1), :]
    for bit in range(bits):
        below = (1 << bit) - 1

        @pl.when(((c >> bit) & 1 == 1) & (c & below == below))
        def _(bit=bit):
            fresh[...] += shrink * slots[bit]

        @pl.when(((c >> bit) & 1 == 1) & (c & below != below))
        def _(bit=bit):
            slots[bit] = shrink * slots[bit]

        @pl.when(((c >> bit) & 1 == 0) & (c & below == below))
        def _(bit=bit):
            slots[bit] = fresh[...]


def final_kernel(padded, heads, tile, local_bits, bits, flags, base, read_t, weight_h, factor, *rest):
    received = rest[:bits]
    out, buckets = rest[bits], rest[bits + 1]
    width = base.shape[1]
    state = read_t.shape[0]
    wide = spread(padded, heads, width, width // heads)

    @pl.when(pl.program_id(0) == 0)
    def _():
        running = jnp.ones((1, width), F32)
        for bit in range(bits):
            upper = (jnp.zeros((1, width), jnp.int32) + flags[bit]) > 0
            extra = received[bit][state:, :].astype(F32)
            scale = jnp.where(upper, running, 0.0)
            buckets[bit * state : (bit + 1) * state, :] = (
                received[bit][0:state, :].astype(F32) * scale
            ).astype(BF16)
            running = jnp.where(upper, running * (extra[0:1] + extra[1:2]), running)

    read_f = read_t[...].astype(F32)
    queries = jnp.concatenate(
        [
            (read_f * weight_h[local_bits + 1 + bit : local_bits + 2 + bit, :]).astype(BF16)
            for bit in range(bits)
        ],
        0,
    )
    for left in range(0, width, tile):
        at = slice(left, left + tile)
        part = dot(queries, buckets[:, at], TN)
        out[:, at] = (base[:, at] + part * dot(factor[...], wide[:, at])).astype(BF16)


def gather_columns(mine, axis):
    pieces = mine
    size = lax.axis_size(axis)
    stride = size // 2
    while stride:
        other = lax.ppermute(pieces, axis, [(i, i ^ stride) for i in range(size)])
        pieces = jnp.concatenate([pieces, other], 0)
        stride //= 2
    return pieces


def cost(flops, bytes_accessed):
    return pl.CostEstimate(flops=flops, bytes_accessed=bytes_accessed, transcendentals=0)


def on_device(
    mixer_input, write_map, read_map, step_size, log_decay, skip_gain, level_table, level_index
):
    tokens, width = mixer_input.shape
    heads = log_decay.shape[0]
    per_head = width // heads
    blocks = tokens // BLOCK
    local_bits = blocks.bit_length() - 1
    ranks = lax.axis_size("seq")
    device_bits = ranks.bit_length() - 1
    levels = level_table.shape[0]
    padded = -(-heads // 32) * 32
    tile = 256
    rank = lax.axis_index("seq")
    flags = (rank >> jnp.arange(device_bits, dtype=jnp.int32)) & 1

    write_t = gather_columns(write_map.T, "head")
    read_t = gather_columns(read_map.T, "head")
    state = write_t.shape[0]

    sds = jax.ShapeDtypeStruct
    narrow = sds((tokens, 2 * padded), BF16)
    row_count = -(-blocks // 8) * 8 + 8
    (
        cum_t, cum_h, f_step, f_end, f_off, f_cum, f_run, f_total, weight_t, weight_h, rows
    ) = pl.pallas_call(
        functools.partial(prep_kernel, heads, padded, width),
        out_shape=(
            sds((tokens, 2 * padded), F32), sds((padded, tokens), F32),
            narrow, narrow, narrow, narrow, narrow, narrow,
            sds((tokens, levels), F32), sds((levels, tokens), F32), sds((row_count, width), F32),
        ),
        scratch_shapes=[
            pltpu.VMEM((2 * padded, tokens), F32),
            pltpu.VMEM((2 * padded, tokens), F32),
            pltpu.VMEM((tokens, 2 * padded), F32),
        ],
        name="prep",
    )(log_decay, step_size, level_index, level_table)

    by_token = lambda columns: pl.BlockSpec((BLOCK, columns), lambda g: (g, 0))
    by_lane = lambda count: pl.BlockSpec((count, BLOCK), lambda g: (0, g))
    whole = lambda shape: pl.BlockSpec(shape, lambda g: (0,) * len(shape))
    payload_rows = state + 8
    mine, mine_exp, payload = pl.pallas_call(
        functools.partial(state_kernel, heads, padded, tile),
        grid=(blocks,),
        in_specs=[by_token(width), by_token(2 * padded), by_lane(state), whole((row_count, width))],
        out_specs=(whole((state, width)), whole((8, width)), whole((payload_rows, width))),
        out_shape=(
            sds((state, width), F32), sds((8, width), F32), sds((payload_rows, width), BF16)
        ),
        cost_estimate=cost(2 * tokens * width * state, tokens * width * 2),
        name="state",
    )(mixer_input, f_total, write_t, rows)

    skip_row = jnp.repeat(skip_gain, per_head)[None, :]

    def local(first, count, slots):
        shift = lambda columns: pl.BlockSpec((BLOCK, columns), lambda g: (g + first, 0))
        shift_lane = lambda n: pl.BlockSpec((n, BLOCK), lambda g: (0, g + first))
        return pl.pallas_call(
            functools.partial(local_kernel, heads, padded, tile, local_bits, first),
            grid=(count,),
            in_specs=[
                shift(width), shift_lane(state), shift_lane(state), shift(2 * padded),
                shift_lane(padded), shift(2 * padded), shift(2 * padded), shift(2 * padded),
                shift(2 * padded), shift(levels), shift_lane(levels), whole((row_count, width)),
                whole((1, width)), whole((local_bits, state, width)),
            ],
            out_specs=(by_token(width), whole((local_bits, state, width))),
            out_shape=(
                sds((count * BLOCK, width), F32), sds((local_bits, state, width), F32)
            ),
            scratch_shapes=[
                pltpu.VMEM((BLOCK, BLOCK), F32),
                pltpu.VMEM((BLOCK, width), F32),
                pltpu.VMEM((state, width), F32),
            ],
            cost_estimate=cost(count * BLOCK * width * 2 * 3000, count * BLOCK * width * 8),
            name="local",
        )(
            mixer_input, write_t, read_t, cum_t, cum_h, f_step, f_end, f_off, f_cum, weight_t,
            weight_h, rows, skip_row, slots,
        )

    slots = jnp.zeros((local_bits, state, width), F32)
    base, slots = local(0, blocks, slots)

    received = []
    for bit in range(device_bits):
        other = lax.ppermute(payload, "seq", [(i, i ^ 1 << bit) for i in range(ranks)])
        received.append(other)
        if bit + 1 < device_bits:
            mine, mine_exp, payload = pl.pallas_call(
                lambda f, *refs, bit=bit: merge_kernel(f, bit, *refs),
                in_specs=[pl.BlockSpec(memory_space=pltpu.SMEM)]
                + [pl.BlockSpec(memory_space=pltpu.VMEM)] * 3,
                out_shape=(
                    sds((state, width), F32), sds((8, width), F32), sds((payload_rows, width), BF16)
                ),
                cost_estimate=cost(4 * state * width, state * width * 12),
                name="merge",
            )(flags, other, mine, mine_exp)

    return pl.pallas_call(
        functools.partial(final_kernel, padded, heads, tile, local_bits, device_bits),
        grid=(blocks,),
        in_specs=[
            pl.BlockSpec(memory_space=pltpu.SMEM), by_token(width), by_lane(state),
            by_lane(levels), by_token(2 * padded),
        ]
        + [whole((payload_rows, width))] * device_bits,
        out_specs=by_token(width),
        out_shape=sds((tokens, width), BF16),
        scratch_shapes=[pltpu.VMEM((device_bits * state, width), BF16)],
        cost_estimate=cost(2 * tokens * width * state * device_bits, tokens * width * 6),
        name="final",
    )(flags, base, read_t, weight_h, f_run, *received)


def solution(mesh):
    placed = (
        P("seq", "head"),
        P("seq", "head"),
        P("seq", "head"),
        P("head", "seq"),
        P("head", "seq"),
        P("head"),
        P(),
        P(None, "seq"),
    )
    return jax.shard_map(
        on_device, mesh=mesh, in_specs=placed, out_specs=P("seq", "head"), check_vma=False
    )
```

time: 438 us -> 104 us (0.24); the launches traced: 432 us -> 104 us
  local copies, waits for them, and re-layouts: 116 us -> 4.41 us
  other arithmetic: 106 us -> 4.02 us
  matrix products: 88 us -> 0 us
  Pallas kernels: 0 us -> 66.3 us
  loops' own time: 56.8 us -> 0 us
  waiting for transfers between devices: 42.8 us -> 18.4 us
  blocking collectives: 15.8 us -> 0 us
    dot_general x32 -> x0, matrix products: 88 us -> none  [the longest x8 51.5 us: read_block(): jnp.einsum('tk,hkp->thp', queries, stacked, precision=lax.Precision.HIGHE...]
    pallas_call x0 -> x6, Pallas kernels: none -> 66.3 us  [the longest x1 31.4 us: local(): pl.pallas_call(functools.partial(local_kernel, heads, padded, tile, local...]
    while x40 -> x0, other arithmetic: 65.8 us -> none
    another operation x2 -> x0, loops' own time: 56.8 us -> none  [the longest x1 36.5 us: on_device(): mixed = lax.map(read_block, block_ids)]
    dynamic_slice x96 -> x0, local copies, waits for them, and re-layouts: 54.6 us -> none  [the longest x32 25.9 us: block_rows(): return lax.dynamic_slice_in_dim(source, block_index * BLOCK, BLOCK, 0)]
    another operation x10 -> x0, other arithmetic: 27.9 us -> none  [the longest x8 16.6 us: read_block(): jnp.stack(states, axis=1)]
    ppermute x5 -> x7, waiting for transfers between devices: 42.8 us -> 18.4 us  [the longest x3 14.7 us: on_device(): lax.ppermute(payload, 'seq', [(i, i ^ 1 << bit) for i in range(ranks)])]
    all_gather x2 -> x0, blocking collectives: 15.8 us -> none  [the longest x1 8.63 us: on_device(): lax.all_gather(write_map, 'head', axis=1, tiled=True)]
  transfers between devices with their start and end apart: 5 -> 7, of which waited for: 3 -> 3; matrix products, arithmetic and copies ran while one was open for 2% -> 5% of each run, Pallas kernels for 0% -> 51%
where the time goes in v1:
time: 104 us
  Pallas kernels  66.3 us (64%)
  waiting for transfers between devices  18.4 us (18%)
  starting transfers between devices  10.6 us (10%)
  local copies, waits for them, and re-layouts  4.41 us (4%)
  other arithmetic  4.02 us (4%)
    pallas_call x1, Pallas kernels, local(): pl.pallas_call(functools.partial(local_kernel, heads, padded, tile, local...  31.4 us
    ppermute x3, waiting for transfers between devices, on_device(): lax.ppermute(payload, 'seq', [(i, i ^ 1 << bit) for i in range(ranks)])  14.7 us
    pallas_call x1, Pallas kernels, on_device(): pl.pallas_call(functools.partial(state_kernel, heads, padded, tile), grid...  12.6 us
    pallas_call x1, Pallas kernels, on_device(): pl.pallas_call(functools.partial(final_kernel, padded, heads, tile, local...  11.6 us
    pallas_call x1, Pallas kernels, on_device(): pl.pallas_call(functools.partial(prep_kernel, heads, padded, width), out_...  6.17 us
    ppermute x3, starting transfers between devices, on_device(): lax.ppermute(payload, 'seq', [(i, i ^ 1 << bit) for i in range(ranks)])  5.69 us
    ppermute x4, starting transfers between devices, gather_columns(): other = lax.ppermute(pieces, axis, [(i, i ^ stride) for i in range(size)])  4.92 us
    pallas_call x2, Pallas kernels, on_device(): pl.pallas_call(lambda f, *refs, bit=bit: merge_kernel(f, bit, *refs), in_...  4.5 us
  transfers between devices with their start and end apart: 7, of which 3 were waited for; matrix products, arithmetic and copies ran while one was open for 5% of the time, Pallas kernels for 51%

profile of v1, /device:TPU:0, one launch (start us, length us, event | category | flops | bytes accessed | tf_op | source)
XLA Modules:
  0.0 103.8 jit_solution(12557148426920915054)
XLA Ops:
  0.0 3.0 %collective-permute-start = (bf16[32,2048]{1,0:T(8,128)(2,1)}, bf16[32,2048]{1,0:T(8,128)(2,1)S(1)}, u32[]{:S(2)}, u32[]{:S(2)}) collective-permute-start(bf16[32,2048]{1,0:T(8,128)(2,1)} %bitcast.2), channel_id=1, source_target_pairs={{0,2},{1,3},{2,0},{3,1},{4,6},{5,7},{6,4},{7,5},{8,10},{9,11},{10,... | collective-permute-start | bytes 393224 | tf_op jit(solution)/shard_map/ppermute | solution.py:298
  3.0 3.7 %collective-permute-done = bf16[32,2048]{1,0:T(8,128)(2,1)S(1)} collective-permute-done((bf16[32,2048]{1,0:T(8,128)(2,1)}, bf16[32,2048]{1,0:T(8,128)(2,1)S(1)}, u32[]{:S(2)}, u32[]{:S(2)}) %collective-permute-start) | collective-permute-done | bytes 131104 | tf_op jit(solution)/shard_map/ppermute | solution.py:298
  6.7 0.9 pad_maximum_fusion.2
  7.6 0.1 collective-permute-start.1
  7.7 1.8 %collective-permute-start.2 = (bf16[32,2048]{1,0:T(8,128)(2,1)}, bf16[32,2048]{1,0:T(8,128)(2,1)S(1)}, u32[]{:S(2)}, u32[]{:S(2)}) collective-permute-start(bf16[32,2048]{1,0:T(8,128)(2,1)} %bitcast.5), channel_id=1, source_target_pairs={{0,2},{1,3},{2,0},{3,1},{4,6},{5,7},{6,4},{7,5},{8,10},{9,11},{10,... | collective-permute-start | bytes 393224 | tf_op jit(solution)/shard_map/ppermute | solution.py:298
  9.5 6.2 %prep.1 = (f32[2048,64]{1,0:T(8,128)}, f32[32,2048]{1,0:T(8,128)}, bf16[2048,64]{1,0:T(8,128)(2,1)}, bf16[2048,64]{1,0:T(8,128)(2,1)}, bf16[2048,64]{1,0:T(8,128...) custom-call(f32[20,2048]{1,0:T(8,128)} %log_decay.1, ...), custom_call_target="tpu_custom_call" | custom-call | tf_op jit(solution)/shard_map/prep/pallas_call | solution.py:333
  15.7 0.0 collective-permute-done.1
  15.7 1.7 %pad_maximum_fusion.write_t = bf16[128,2048]{1,0:T(8,128)(2,1)} fusion(bf16[64,2048]{1,0:T(8,128)(2,1)S(1)} %collective-permute-done.1, bf16[32,2048]{1,0:T(8,128)(2,1)S(1)} %collective-permute-done, bf16[32,2048]{1,0:T(8,128)(2,1)} %bitcast.4), kind=kLoop, calls=%fused_computation | loop fusion | flops 1572864 | bytes 1048576 | tf_op jit(solution)/shard_map/concatenate | solution.py:299
  17.4 12.6 %state.1 = (f32[128,1280]{1,0:T(8,128)}, f32[8,1280]{1,0:T(8,128)}, bf16[136,1280]{1,0:T(8,128)(2,1)}) custom-call(bf16[2048,1280]{1,0:T(8,128)(2,1)} %mixer.3, bf16[2048,64]{1,0:T(8,128)(2,1)} %get-tuple-element.35.factor, bf16[128,2048]{1,0:T(8,128)(2,1)} %pad_maximum_fusion.write_t, f32[16,1280]{1,0:T(8,128)} %get-tuple-element.32.rows), custom_call_target="tpu_custom_call" | custom-call | flops 671088640 | bytes 5242880 | tf_op jit(solution)/shard_map/state/pallas_call | solution.py:352
  30.0 1.5 %collective-permute-start.4 = (bf16[136,1280]{1,0:T(8,128)(2,1)}, bf16[136,1280]{1,0:T(8,128)(2,1)S(1)}, u32[]{:S(2)}, u32[]{:S(2)}) collective-permute-start(bf16[136,1280]{1,0:T(8,128)(2,1)} %get-tuple-element.36), channel_id=1, source_target_pairs={{0,4},{4,0},{8,12},{12,8},{16,20},{20,16},{24,28},{28,24},{1,5},{5... | collective-permute-start | bytes 1044488 | tf_op jit(solution)/shard_map/ppermute | solution.py:399
  31.6 0.0 collective-permute-done.2
  31.6 0.0 copy-done.2
  31.6 0.1 collective-permute-start.3
  31.7 0.5 shift-right-arithmetic_and_fusion.f.flags
  32.2 8.3 %collective-permute-done.4.refs_0_.rest_0_ = bf16[136,1280]{1,0:T(8,128)(2,1)S(1)} collective-permute-done((bf16[136,1280]{1,0:T(8,128)(2,1)}, bf16[136,1280]{1,0:T(8,128)(2,1)S(1)}, u32[]{:S(2)}, u32[]{:S(2)}) %collective-permute-start.4) | collective-permute-done | bytes 348192 | tf_op jit(solution)/shard_map/ppermute | solution.py:399
  40.5 0.7 copy-done
  41.2 2.3 %merge.2 = (f32[128,1280]{1,0:T(8,128)}, f32[8,1280]{1,0:T(8,128)}, bf16[136,1280]{1,0:T(8,128)(2,1)}) custom-call(s32[3]{0:T(128)} %shift-right-arithmetic_and_fusion.f.flags, bf16[136,1280]{1,0:T(8,128)(2,1)} %copy-done, f32[128,1280]{1,0:T(8,128)} %get-tuple-element.37.refs_1_, f32[8,1280]{1,0:T(8,128)} %get-tuple-element.38.refs_2_), custom_call_target="tpu_custom_call" | custom-call | flops 655360 | bytes 1966080 | tf_op jit(solution)/shard_map/merge/pallas_call | solution.py:402
  43.5 1.6 %collective-permute-start.5 = (bf16[136,1280]{1,0:T(8,128)(2,1)}, bf16[136,1280]{1,0:T(8,128)(2,1)S(1)}, u32[]{:S(2)}, u32[]{:S(2)}) collective-permute-start(bf16[136,1280]{1,0:T(8,128)(2,1)} %get-tuple-element.39), channel_id=1, source_target_pairs={{0,8},{4,12},{8,0},{12,4},{16,24},{20,28},{24,16},{28,20},{1,9},{5... | collective-permute-start | bytes 1044488 | tf_op jit(solution)/shard_map/ppermute | solution.py:399
  45.0 0.1 broadcast_in_dim.6
  45.1 0.7 broadcast_in_dim_reshape.3.skip
  45.8 0.0 collective-permute-done.3
  45.8 0.8 pad_maximum_fusion.1.read_t
  46.6 6.4 %collective-permute-done.5.refs_0_.rest_1_ = bf16[136,1280]{1,0:T(8,128)(2,1)S(1)} collective-permute-done((bf16[136,1280]{1,0:T(8,128)(2,1)}, bf16[136,1280]{1,0:T(8,128)(2,1)S(1)}, u32[]{:S(2)}, u32[]{:S(2)}) %collective-permute-start.5) | collective-permute-done | bytes 348192 | tf_op jit(solution)/shard_map/ppermute | solution.py:399
  53.0 0.8 copy-done.1
  53.8 2.2 %merge.3 = (f32[128,1280]{1,0:T(8,128)}, f32[8,1280]{1,0:T(8,128)}, bf16[136,1280]{1,0:T(8,128)(2,1)}) custom-call(s32[3]{0:T(128)} %shift-right-arithmetic_and_fusion.f.flags, bf16[136,1280]{1,0:T(8,128)(2,1)} %copy-done.1, f32[128,1280]{1,0:T(8,128)} %get-tuple-element.40.refs_1_, f32[8,1280]{1,0:T(8,128)} %get-tuple-element.41.refs_2_), custom_call_target="tpu_custom_call" | custom-call | flops 655360 | bytes 1966080 | tf_op jit(solution)/shard_map/merge/pallas_call | solution.py:402
  56.0 2.6 %collective-permute-start.6 = (bf16[136,1280]{1,0:T(8,128)(2,1)}, bf16[136,1280]{1,0:T(8,128)(2,1)S(1)}, u32[]{:S(2)}, u32[]{:S(2)}) collective-permute-start(bf16[136,1280]{1,0:T(8,128)(2,1)} %get-tuple-element.42), channel_id=1, source_target_pairs={{0,16},{4,20},{8,24},{12,28},{16,0},{20,4},{24,8},{28,12},{1,17},{... | collective-permute-start | bytes 1044488 | tf_op jit(solution)/shard_map/ppermute | solution.py:399
  58.6 1.4 %broadcast_in_dim.7.slots_in = f32[3,128,1280]{2,1,0:T(8,128)} broadcast(f32[]{:T(128)} %constant.9.clone.1), dimensions={} | broadcast | bytes 1966084 | tf_op jit(solution)/shard_map/broadcast_in_dim | solution.py:394
  60.0 31.4 %local.1 = (f32[2048,1280]{1,0:T(8,128)}, f32[3,128,1280]{2,1,0:T(8,128)}) custom-call(bf16[2048,1280]{1,0:T(8,128)(2,1)} %mixer.3, bf16[128,2048]{1,0:T(8,128)(2,1)} %pad_maximum_fusion.write_t, bf16[128,2048]{1,0:T(8,128)(2,1)} %pad_maximum_fusion.1.read_t, f32[2048,64]{1,0:T(8,128)} %get-tuple-element.24.cum_t, f32[32,2048]{1,0:T(8,128)} %get-tuple-element.25.cum_h, ...), custom_call_target="tpu_custom_call" | custom-call | flops 15728640000 | bytes 20971520 | tf_op jit(solution)/shard_map/local/pallas_call | solution.py:369
  91.5 0.0 collective-permute-done.6.rest_2_
  91.5 0.0 copy-start.3
  91.5 0.7 copy-done.3
  92.2 11.6 %final.1 = bf16[2048,1280]{1,0:T(8,128)(2,1)} custom-call(s32[3]{0:T(128)} %shift-right-arithmetic_and_fusion.f.flags, f32[2048,1280]{1,0:T(8,128)} %get-tuple-element.33.base, bf16[128,2048]{1,0:T(8,128)(2,1)} %pad_maximum_fusion.1.read_t, f32[7,2048]{1,0:T(8,128)} %get-tuple-element.31.weight_h, bf16[2048,64]{1,0:T(8,128)(2,1)} %get-tuple-element.34.factor, ...), custom_call_target="tpu_custom_call" | custom-call | flops 2013265920 | bytes 15728640 | tf_op jit(solution)/shard_map/final/pallas_call | solution.py:413
  (6 shorter events, 0.0 us)
Async XLA Ops:
  0.0 31.6 %copy-start.2 = (bf16[2048,32]{0,1:T(8,128)(2,1)S(1)}, bf16[2048,32]{0,1:T(8,128)(2,1)}, u32[]{:S(2)}) copy-start(bf16[2048,32]{0,1:T(8,128)(2,1)} %param.10) | copy-start | bytes 393220
  0.0 45.0 %copy-start.4 = (f32[20]{0:T(128)S(1)}, f32[20]{0:T(128)}, u32[]{:S(2)}) copy-start(f32[20]{0:T(128)} %param.13) | copy-start | bytes 244
  0.0 6.7 %collective-permute-start = (bf16[32,2048]{1,0:T(8,128)(2,1)}, bf16[32,2048]{1,0:T(8,128)(2,1)S(1)}, u32[]{:S(2)}, u32[]{:S(2)}) collective-permute-start(bf16[32,2048]{1,0:T(8,128)(2,1)} %bitcast.2), channel_id=1, source_target_pairs={{0,2},{1,3},{2,0},{3,1},{4,6},{5,7},{6,4},{7,5},{8,10},{9,11},{10,... | collective-permute-start | bytes 393224 | tf_op jit(solution)/shard_map/ppermute | solution.py:298
  7.6 8.1 %collective-permute-start.1 = (bf16[64,2048]{1,0:T(8,128)(2,1)S(1)}, bf16[64,2048]{1,0:T(8,128)(2,1)S(1)}, u32[]{:S(2)}, u32[]{:S(2)}) collective-permute-start(bf16[64,2048]{1,0:T(8,128)(2,1)S(1)} %pad_maximum_fusion.2), channel_id=1, source_target_pairs={{0,1},{1,0},{2,3},{3,2},{4,5},{5,4},{6,7},{7,6},{8,9},{9,8},{10,11... | collective-permute-start | bytes 786440 | tf_op jit(solution)/shard_map/ppermute | solution.py:298
  7.7 23.9 %collective-permute-start.2 = (bf16[32,2048]{1,0:T(8,128)(2,1)}, bf16[32,2048]{1,0:T(8,128)(2,1)S(1)}, u32[]{:S(2)}, u32[]{:S(2)}) collective-permute-start(bf16[32,2048]{1,0:T(8,128)(2,1)} %bitcast.5), channel_id=1, source_target_pairs={{0,2},{1,3},{2,0},{3,1},{4,6},{5,7},{6,4},{7,5},{8,10},{9,11},{10,... | collective-permute-start | bytes 393224 | tf_op jit(solution)/shard_map/ppermute | solution.py:298
  30.0 10.4 %collective-permute-start.4 = (bf16[136,1280]{1,0:T(8,128)(2,1)}, bf16[136,1280]{1,0:T(8,128)(2,1)S(1)}, u32[]{:S(2)}, u32[]{:S(2)}) collective-permute-start(bf16[136,1280]{1,0:T(8,128)(2,1)} %get-tuple-element.36), channel_id=1, source_target_pairs={{0,4},{4,0},{8,12},{12,8},{16,20},{20,16},{24,28},{28,24},{1,5},{5... | collective-permute-start | bytes 1044488 | tf_op jit(solution)/shard_map/ppermute | solution.py:399
  31.6 14.2 %collective-permute-start.3 = (bf16[64,2048]{1,0:T(8,128)(2,1)S(1)}, bf16[64,2048]{1,0:T(8,128)(2,1)S(1)}, u32[]{:S(2)}, u32[]{:S(2)}) collective-permute-start(bf16[64,2048]{1,0:T(8,128)(2,1)S(1)} %pad_maximum_fusion.3), channel_id=1, source_target_pairs={{0,1},{1,0},{2,3},{3,2},{4,5},{5,4},{6,7},{7,6},{8,9},{9,8},{10,11... | collective-permute-start | bytes 786440 | tf_op jit(solution)/shard_map/ppermute | solution.py:298
  40.4 0.7 copy-start
  43.5 9.6 %collective-permute-start.5 = (bf16[136,1280]{1,0:T(8,128)(2,1)}, bf16[136,1280]{1,0:T(8,128)(2,1)S(1)}, u32[]{:S(2)}, u32[]{:S(2)}) collective-permute-start(bf16[136,1280]{1,0:T(8,128)(2,1)} %get-tuple-element.39), channel_id=1, source_target_pairs={{0,8},{4,12},{8,0},{12,4},{16,24},{20,28},{24,16},{28,20},{1,9},{5... | collective-permute-start | bytes 1044488 | tf_op jit(solution)/shard_map/ppermute | solution.py:399
  53.0 0.8 copy-start.1
  56.0 35.5 %collective-permute-start.6 = (bf16[136,1280]{1,0:T(8,128)(2,1)}, bf16[136,1280]{1,0:T(8,128)(2,1)S(1)}, u32[]{:S(2)}, u32[]{:S(2)}) collective-permute-start(bf16[136,1280]{1,0:T(8,128)(2,1)} %get-tuple-element.42), channel_id=1, source_target_pairs={{0,16},{4,20},{8,24},{12,28},{16,0},{20,4},{24,8},{28,12},{1,17},{... | collective-permute-start | bytes 1044488 | tf_op jit(solution)/shard_map/ppermute | solution.py:399
  91.5 0.7 copy-start.3

commit v2 on v0

v2 whole, which is shorter than its diff:
```python
import functools

import jax
import jax.numpy as jnp
from jax import lax
from jax.experimental import pallas as pl
from jax.experimental.pallas import tpu as pltpu
from jax.sharding import PartitionSpec as P

BLOCK = 256
HALF = BLOCK // 2
LANES = 128
LOG2E = 1.4426950408889634
F32 = jnp.float32
BF16 = jnp.bfloat16
NT = (((1,), (1,)), ((), ()))
NN = (((1,), (0,)), ((), ()))
TN = (((0,), (0,)), ((), ()))
VMEM_SPEC = pl.BlockSpec(memory_space=pltpu.VMEM)
SMEM_SPEC = pl.BlockSpec(memory_space=pltpu.SMEM)
ANY_SPEC = pl.BlockSpec(memory_space=pl.ANY)


def dot(a, b, dims=NN):
    return lax.dot_general(a, b, dims, preferred_element_type=F32)


def three(a):
    high = a.astype(BF16)
    rest = a - high.astype(F32)
    middle = rest.astype(BF16)
    return high, middle, (rest - middle.astype(F32)).astype(BF16)


def two(a):
    high = a.astype(BF16).astype(F32)
    return high, a - high


def iota(shape, dim):
    return lax.broadcasted_iota(jnp.int32, shape, dim)


def as_bf16(mask):
    return mask.astype(F32).astype(BF16)


def spread(first_row, padded, heads, width):
    per_head = width // heads
    row = iota((4 * padded, width), 0) - first_row
    lane = iota((4 * padded, width), 1)
    inside = (row >= 0) & (row < 2 * padded)
    row = jnp.where(row >= padded, row - padded, row)
    own = (row * per_head <= lane) & (lane < (row + 1) * per_head) & (row < heads)
    return as_bf16(own & inside)


class Rows:
    def __init__(self, blocks):
        halves = 2 * blocks
        self.after, self.run = 0, halves
        self.middle, self.upper, self.decay = 2 * halves, 2 * halves + blocks, 2 * halves + 2 * blocks
        self.total = 2 * halves + 3 * blocks
        self.count = -(-(self.total + 1) // 16) * 16

    def ranges(self, tokens):
        halves = tokens // HALF
        low, high = [], []
        for a in range(halves):
            low.append((a + 1) * HALF), high.append(tokens)
        for a in range(halves):
            low.append(0), high.append(a * HALF)
        for c in range(halves // 2):
            low.append(c * BLOCK), high.append(c * BLOCK + HALF)
        for c in range(halves // 2):
            low.append(c * BLOCK + HALF), high.append((c + 1) * BLOCK)
        for c in range(halves // 2):
            low.append(c * BLOCK), high.append((c + 1) * BLOCK)
        low.append(0), high.append(tokens)
        pad = self.count - len(low)
        return jnp.array([low + [0] * pad, high + [0] * pad], jnp.int32).T


def prep_kernel(
    heads, padded, log_decay, step_size, level_index, level_table, ranges,
    factors, columns, cum_h, weight_h, rows, decay, steps, packed,
):
    tokens = log_decay.shape[1]
    width = rows.shape[1]
    blocks = tokens // BLOCK
    decay[...] = jnp.zeros_like(decay)
    steps[...] = jnp.zeros_like(steps)
    decay[0:heads, :] = log_decay[...]
    steps[0:heads, :] = step_size[...]
    lower = as_bf16(iota((BLOCK, BLOCK), 0) >= iota((BLOCK, BLOCK), 1))
    levels = level_index.shape[0]
    weight = jnp.zeros(level_index.shape, F32)
    index = level_index[...]
    for entry in range(level_table.shape[1]):
        weight = weight + jnp.where(index == entry, level_table[:, entry : entry + 1], 0.0)
    weight_h[...] = weight
    packed[...] = jnp.zeros_like(packed)
    for c in range(blocks):
        at = slice(c * BLOCK, (c + 1) * BLOCK)
        high, middle, low = three(decay[:, at])
        cum = (dot(low, lower, NT) + dot(middle, lower, NT)) + dot(high, lower, NT)
        step = steps[:, at]
        mid = cum[:, HALF - 1 : HALF]
        end = cum[:, BLOCK - 1 : BLOCK]
        first = iota((padded, BLOCK), 1) < HALF
        column = two(step * jnp.exp(jnp.where(first, mid, end) - cum))
        row = two(jnp.exp(cum - jnp.where(first, 0.0, mid)))
        four = jnp.concatenate([column[0], column[1], row[0], row[1]], 0)
        factors[at, :] = four.T.astype(BF16)
        scaled = cum * LOG2E
        cum_h[:, at] = scaled - jnp.log2(step)
        packed[0:padded, :] = scaled
        packed[padded : padded + levels, :] = weight_h[:, at]
        columns[at, :] = packed[...].T
    token = iota((rows.shape[0], tokens), 1)
    chosen = as_bf16((token >= ranges[:, 0:1]) & (token < ranges[:, 1:2]))
    high, middle, low = three(decay[...])
    sums = (dot(chosen, low, NT) + dot(chosen, middle, NT)) + dot(chosen, high, NT)
    high, low = two(jnp.exp(sums))
    per_head = width // heads
    head = iota((padded, width), 0) * per_head
    lane = iota((padded, width), 1)
    own = as_bf16((head <= lane) & (lane < head + per_head))
    rows[...] = dot(high.astype(BF16), own) + dot(low.astype(BF16), own)


def scale_kernel(heads, padded, layout, mixer, factors, rows, scaled, to_total):
    tokens, width = mixer.shape
    wide = spread(0, padded, heads, width)

    def step(a, carry):
        at = pl.ds(pl.multiple_of(a * HALF, HALF), HALF)
        row = rows[pl.ds(layout.after + a, 1), :]
        value = mixer[at, :].astype(F32) * dot(factors[at, :], wide)
        scaled[at, :] = value.astype(BF16)
        to_total[at, :] = (value * row).astype(BF16)
        return carry

    lax.fori_loop(0, tokens // HALF, step, 0)


def exp_rows(total, count):
    where = iota((count, total.shape[1]), 0)
    high = total.astype(BF16).astype(F32)
    return jnp.where(where == 0, high, jnp.where(where == 1, total - high, 0.0)).astype(BF16)


def state_kernel(layout, to_total, write_t, rows, mine, mine_exp, payload):
    state = write_t.shape[0]
    new = dot(write_t[...], to_total[...])
    mine[...] = new
    payload[0:state, :] = new.astype(BF16)
    total = rows[layout.total : layout.total + 1, :]
    payload[state:, :] = exp_rows(total, payload.shape[0] - state)
    mine_exp[...] = jnp.broadcast_to(total, mine_exp.shape)


def merge_kernel(bit, flags, received, mine, mine_exp, after, merged, merged_exp, payload):
    state = mine.shape[0]
    extra = received[state:, :].astype(F32)
    other_exp = extra[0:1] + extra[1:2]
    own_exp = mine_exp[0:1, :]
    upper = (jnp.zeros((1, mine.shape[1]), jnp.int32) + flags[bit]) > 0
    own_scale = jnp.where(upper, 1.0, other_exp)
    other_scale = jnp.where(upper, own_exp, 1.0)
    new = own_scale * mine[...] + other_scale * received[0:state, :].astype(F32)
    merged[...] = new
    total = own_exp * other_exp
    merged_exp[...] = jnp.broadcast_to(total, merged_exp.shape)
    payload[0:state, :] = new.astype(BF16)
    payload[state:, :] = exp_rows(total, payload.shape[0] - state)


def local_kernel(
    heads, padded, bits, first, count, layout, tile,
    mixer, scaled, write_t, read_t, factors, columns, cum_h, weight_h, rows, skip, slots_in, after,
    base, reach, slots, scores, inter, fresh,
):
    width = mixer.shape[1]
    per_head = width // heads
    heads_here = LANES // per_head
    wide = spread(2 * padded, padded, heads, width)
    if first == 0:
        slots[...] = jnp.zeros_like(slots)
    else:
        slots[...] = slots_in[...]

    def block(g, carry):
        c = first + g
        at = pl.ds(pl.multiple_of(c * BLOCK, BLOCK), BLOCK)
        out_at = pl.ds(pl.multiple_of(g * BLOCK, BLOCK), BLOCK)
        read = read_t[:, at]
        write = write_t[:, at]

        inter[...] = jnp.zeros_like(inter)
        for bit in range(bits):

            @pl.when((c >> bit) & 1 == 1)
            def _(bit=bit):
                query = (read.astype(F32) * weight_h[bit + 1 : bit + 2, at]).astype(BF16)
                inter[...] += dot(query, slots[bit].astype(BF16), TN)

        weighted = dot(read, write, TN) * columns[at, padded : padded + 1]
        causal = iota((HALF, HALF), 0) >= iota((HALF, HALF), 1)
        off_scores = weighted[HALF:, :HALF].astype(BF16)
        scores[0] = jnp.where(causal, weighted[:HALF, :HALF], 0.0)
        scores[1] = jnp.where(causal, weighted[HALF:, HALF:], 0.0)
        lane = iota((HALF, LANES), 1)
        own = [as_bf16((lane >= k * per_head) & (lane < (k + 1) * per_head)) for k in range(heads_here)]
        middle = rows[pl.ds(layout.middle + c, 1), :]
        for half in range(2):
            half_at = pl.ds(pl.multiple_of(c * BLOCK + half * HALF, HALF), HALF)
            put_at = pl.ds(pl.multiple_of(g * BLOCK + half * HALF, HALF), HALF)
            first_at = pl.ds(pl.multiple_of(c * BLOCK, HALF), HALF)
            row_at = slice(half * HALF, (half + 1) * HALF)
            run = rows[pl.ds(layout.run + 2 * c + half, 1), :]
            for left in range(0, width, tile):
                lanes = slice(left, left + tile)
                near = dot(factors[half_at, :], wide[:, lanes])
                reach[put_at, lanes] = near * run[:, lanes]
                if half == 0:
                    rest = near * inter[row_at, lanes]
                else:
                    off = dot(off_scores, scaled[first_at, lanes])
                    rest = near * (off + middle[:, lanes] * inter[row_at, lanes])
                for inner in range(left, left + tile, LANES):
                    here = slice(inner, inner + LANES)
                    head = inner // per_head
                    value = mixer[half_at, here]
                    left_side = []
                    for k in range(heads_here):
                        gap = columns[half_at, head + k : head + k + 1] - cum_h[head + k : head + k + 1, half_at]
                        mixing = scores[half] * jnp.exp2(jnp.minimum(gap, 0.0))
                        left_side.append(mixing.astype(BF16))
                    part = dot(
                        jnp.concatenate(left_side, 1),
                        jnp.concatenate([value * mask for mask in own], 0),
                    )
                    base[put_at, here] = (
                        part + rest[:, inner - left : inner - left + LANES]
                        + skip[:, here] * value.astype(F32)
                    )

        upper = rows[pl.ds(layout.upper + c, 1), :]
        start = pl.multiple_of(c * BLOCK, HALF)
        fresh[...] = upper * dot(
            write_t[:, pl.ds(start, HALF)], scaled[pl.ds(start, HALF), :]
        ) + dot(write_t[:, pl.ds(start + HALF, HALF)], scaled[pl.ds(start + HALF, HALF), :])
        shrink = rows[pl.ds(layout.decay + c, 1), :]
        for bit in range(bits):
            below = (1 << bit) - 1

            @pl.when(((c >> bit) & 1 == 1) & (c & below == below))
            def _(bit=bit):
                fresh[...] += shrink * slots[bit]

            @pl.when(((c >> bit) & 1 == 1) & (c & below != below))
            def _(bit=bit):
                slots[bit] = shrink * slots[bit]

            @pl.when(((c >> bit) & 1 == 0) & (c & below == below))
            def _(bit=bit):
                slots[bit] = fresh[...]

        return carry

    lax.fori_loop(0, count, block, 0)


def final_kernel(starts, local_bits, bits, flags, read_t, weight_h, *rest):
    pieces = len(starts) - 1
    received, rest = rest[:bits], rest[bits:]
    bases, reaches, rest = rest[:pieces], rest[pieces : 2 * pieces], rest[2 * pieces :]
    out, buckets, ready, sems = rest
    width = out.shape[1]
    state = read_t.shape[0]
    running = jnp.ones((1, width), F32)
    for bit in range(bits):
        upper = (jnp.zeros((1, width), jnp.int32) + flags[bit]) > 0
        extra = received[bit][state:, :].astype(F32)
        scale = jnp.where(upper, running, 0.0)
        buckets[bit * state : (bit + 1) * state, :] = (
            received[bit][0:state, :].astype(F32) * scale
        ).astype(BF16)
        running = jnp.where(upper, running * (extra[0:1] + extra[1:2]), running)

    def copy(c, at):
        return pltpu.make_async_copy(ready.at[c], out.at[pl.ds(at, BLOCK), :], sems.at[c])

    for piece in range(pieces):

        def block(g, carry, piece=piece):
            c = starts[piece] + g
            at = pl.multiple_of(c * BLOCK, BLOCK)
            from_at = pl.ds(pl.multiple_of(g * BLOCK, BLOCK), BLOCK)
            read_f = read_t[:, pl.ds(at, BLOCK)].astype(F32)
            queries = jnp.concatenate(
                [
                    (read_f * weight_h[local_bits + 1 + bit : local_bits + 2 + bit, pl.ds(at, BLOCK)]).astype(BF16)
                    for bit in range(bits)
                ],
                0,
            )
            part = dot(queries, buckets[...], TN)
            ready[c] = (bases[piece][from_at, :] + part * reaches[piece][from_at, :]).astype(BF16)
            copy(c, at).start()
            return carry

        lax.fori_loop(0, starts[piece + 1] - starts[piece], block, 0)
    for c in range(starts[-1]):
        copy(c, c * BLOCK).wait()


def gather_columns(mine, axis):
    pieces = mine
    size = lax.axis_size(axis)
    stride = size // 2
    while stride:
        other = lax.ppermute(pieces, axis, [(i, i ^ stride) for i in range(size)])
        pieces = jnp.concatenate([pieces, other], 0)
        stride //= 2
    return pieces


def cost(flops, bytes_accessed):
    return pl.CostEstimate(flops=flops, bytes_accessed=bytes_accessed, transcendentals=0)


def grant(mebibytes):
    return pltpu.CompilerParams(vmem_limit_bytes=mebibytes << 20)


def on_device(
    mixer_input, write_map, read_map, step_size, log_decay, skip_gain, level_table, level_index
):
    tokens, width = mixer_input.shape
    heads = log_decay.shape[0]
    per_head = width // heads
    blocks = tokens // BLOCK
    local_bits = blocks.bit_length() - 1
    ranks = lax.axis_size("seq")
    device_bits = ranks.bit_length() - 1
    levels = level_table.shape[0]
    padded = LANES // 4
    tile = 256
    layout = Rows(blocks)
    rank = lax.axis_index("seq")
    flags = (rank >> jnp.arange(device_bits, dtype=jnp.int32)) & 1
    sds = jax.ShapeDtypeStruct

    write_t = gather_columns(write_map.T, "head")
    read_t = gather_columns(read_map.T, "head")
    state = write_t.shape[0]

    factors, columns, cum_h, weight_h, rows = pl.pallas_call(
        functools.partial(prep_kernel, heads, padded),
        in_specs=[VMEM_SPEC] * 5,
        out_specs=(VMEM_SPEC,) * 5,
        out_shape=(
            sds((tokens, LANES), BF16), sds((tokens, LANES), F32), sds((padded, tokens), F32),
            sds((levels, tokens), F32), sds((layout.count, width), F32),
        ),
        scratch_shapes=[
            pltpu.VMEM((padded, tokens), F32),
            pltpu.VMEM((padded, tokens), F32),
            pltpu.VMEM((LANES, BLOCK), F32),
        ],
        compiler_params=grant(12),
        cost_estimate=cost(2_000_000_000, 4_000_000),
        name="prep",
    )(log_decay, step_size, level_index, level_table, layout.ranges(tokens))

    scaled, to_total = pl.pallas_call(
        functools.partial(scale_kernel, heads, padded, layout),
        in_specs=[VMEM_SPEC] * 3,
        out_specs=(VMEM_SPEC,) * 2,
        out_shape=(sds((tokens, width), BF16),) * 2,
        compiler_params=grant(8),
        cost_estimate=cost(3_000_000_000, tokens * width * 6),
        name="scale",
    )(mixer_input, factors, rows)

    payload_rows = state + 8
    carried = (sds((state, width), F32), sds((8, width), F32), sds((payload_rows, width), BF16))
    mine, mine_exp, payload = pl.pallas_call(
        functools.partial(state_kernel, layout),
        in_specs=[VMEM_SPEC] * 3,
        out_specs=(VMEM_SPEC,) * 3,
        out_shape=carried,
        compiler_params=grant(8),
        cost_estimate=cost(2 * tokens * width * state, tokens * width * 2),
        name="state",
    )(to_total, write_t, rows)

    skip_row = jnp.repeat(skip_gain, per_head)[None, :]

    def local(first, count, slots, after):
        return pl.pallas_call(
            functools.partial(
                local_kernel, heads, padded, local_bits, first, count, layout, tile
            ),
            in_specs=[VMEM_SPEC] * 10 + [VMEM_SPEC, ANY_SPEC],
            out_specs=(VMEM_SPEC,) * 3,
            out_shape=(
                sds((count * BLOCK, width), F32), sds((count * BLOCK, width), F32),
                sds((local_bits, state, width), F32),
            ),
            scratch_shapes=[
                pltpu.VMEM((2, HALF, HALF), F32),
                pltpu.VMEM((BLOCK, width), F32),
                pltpu.VMEM((state, width), F32),
            ],
            compiler_params=grant(12),
            cost_estimate=cost(count * BLOCK * width * 2 * 2000, count * BLOCK * width * 8),
            name="local",
        )(
            mixer_input, scaled, write_t, read_t, factors, columns, cum_h, weight_h, rows, skip_row,
            slots, after,
        )

    shares = [1] * (device_bits - 2) + [1, 2] if device_bits > 1 else [1]
    starts = [0]
    for k, share in enumerate(shares):
        starts.append(starts[-1] + blocks * share // sum(shares))
    starts[-1] = blocks

    slots = jnp.zeros((8, LANES), F32)
    bases, reaches, received = [], [], []
    after = rows
    for bit in range(device_bits):
        other = lax.ppermute(payload, "seq", [(i, i ^ 1 << bit) for i in range(ranks)])
        if bit < len(starts) - 1 and starts[bit + 1] > starts[bit]:
            base, reach, slots = local(starts[bit], starts[bit + 1] - starts[bit], slots, after)
            bases.append(base)
            reaches.append(reach)
        received.append(other)
        if bit + 1 < device_bits:
            mine, mine_exp, payload = pl.pallas_call(
                functools.partial(merge_kernel, bit),
                in_specs=[SMEM_SPEC] + [VMEM_SPEC] * 3 + [ANY_SPEC],
                out_specs=(VMEM_SPEC,) * 3,
                out_shape=carried,
                compiler_params=grant(8),
                cost_estimate=cost(4 * state * width, state * width * 12),
                name="merge",
            )(flags, other, mine, mine_exp, slots)
            after = mine_exp

    return pl.pallas_call(
        functools.partial(final_kernel, starts, local_bits, device_bits),
        in_specs=[SMEM_SPEC] + [VMEM_SPEC] * (2 + device_bits + 2 * len(bases)),
        out_specs=ANY_SPEC,
        out_shape=sds((tokens, width), BF16),
        scratch_shapes=[
            pltpu.VMEM((device_bits * state, width), BF16),
            pltpu.VMEM((blocks, BLOCK, width), BF16),
            pltpu.SemaphoreType.DMA((blocks,)),
        ],
        compiler_params=grant(12),
        cost_estimate=cost(2 * tokens * width * state * device_bits, tokens * width * 6),
        name="final",
    )(flags, read_t, weight_h, *received, *bases, *reaches)


def solution(mesh):
    placed = (
        P("seq", "head"),
        P("seq", "head"),
        P("seq", "head"),
        P("head", "seq"),
        P("head", "seq"),
        P("head"),
        P(),
        P(None, "seq"),
    )
    return jax.shard_map(
        on_device, mesh=mesh, in_specs=placed, out_specs=P("seq", "head"), check_vma=False
    )
```

time: 438 us -> 67.9 us (0.16); the launches traced: 432 us -> 67.6 us
  other arithmetic: 106 us -> 0.12 us
  local copies, waits for them, and re-layouts: 116 us -> 14.4 us
  matrix products: 88 us -> 0 us
  loops' own time: 56.8 us -> 0 us
  Pallas kernels: 0 us -> 34.4 us
  waiting for transfers between devices: 42.8 us -> 8.41 us
  blocking collectives: 15.8 us -> 0 us
    dot_general x32 -> x0, matrix products: 88 us -> none  [the longest x8 51.5 us: read_block(): jnp.einsum('tk,hkp->thp', queries, stacked, precision=lax.Precision.HIGHE...]
    while x40 -> x0, other arithmetic: 65.8 us -> none
    another operation x2 -> x0, loops' own time: 56.8 us -> none  [the longest x1 36.5 us: on_device(): mixed = lax.map(read_block, block_ids)]
    dynamic_slice x96 -> x0, local copies, waits for them, and re-layouts: 54.6 us -> none  [the longest x32 25.9 us: block_rows(): return lax.dynamic_slice_in_dim(source, block_index * BLOCK, BLOCK, 0)]
    ppermute x5 -> x7, waiting for transfers between devices: 42.8 us -> 8.41 us  [the longest x3 7.64 us: on_device(): lax.ppermute(payload, 'seq', [(i, i ^ 1 << bit) for i in range(ranks)])]
    pallas_call x0 -> x9, Pallas kernels: none -> 34.4 us  [the longest x3 20.1 us: local(): pl.pallas_call(functools.partial(local_kernel, heads, padded, local_bits,...]
    another operation x10 -> x0, other arithmetic: 27.9 us -> none  [the longest x8 16.6 us: read_block(): jnp.stack(states, axis=1)]
    all_gather x2 -> x0, blocking collectives: 15.8 us -> none  [the longest x1 8.63 us: on_device(): lax.all_gather(write_map, 'head', axis=1, tiled=True)]
  transfers between devices with their start and end apart: 5 -> 7, of which waited for: 3 -> 4; matrix products, arithmetic and copies ran while one was open for 2% -> 0% of each run, Pallas kernels for 0% -> 39%
where the time goes in v2:
time: 67.9 us; the launch traced here: 67.6 us
  Pallas kernels  34.4 us (51%)
  local copies, waits for them, and re-layouts  14.4 us (21%)
  starting transfers between devices  10.1 us (15%)
  waiting for transfers between devices  8.41 us (12%)
    pallas_call x3, Pallas kernels, local(): pl.pallas_call(functools.partial(local_kernel, heads, padded, local_bits,...  20.1 us
    unnamed x32, local copies, waits for them, and re-layouts  14.2 us
    ppermute x3, waiting for transfers between devices, on_device(): lax.ppermute(payload, 'seq', [(i, i ^ 1 << bit) for i in range(ranks)])  7.64 us
    ppermute x3, starting transfers between devices, on_device(): lax.ppermute(payload, 'seq', [(i, i ^ 1 << bit) for i in range(ranks)])  6.49 us
    pallas_call x1, Pallas kernels, on_device(): pl.pallas_call(functools.partial(final_kernel, starts, local_bits, device...  6.04 us
    ppermute x4, starting transfers between devices, gather_columns(): other = lax.ppermute(pieces, axis, [(i, i ^ stride) for i in range(size)])  3.64 us
    pallas_call x1, Pallas kernels, on_device(): pl.pallas_call(functools.partial(scale_kernel, heads, padded, layout), in...  3.62 us
    pallas_call x2, Pallas kernels, on_device(): pl.pallas_call(functools.partial(merge_kernel, bit), in_specs=[SMEM_SPEC]...  2.15 us
  transfers between devices with their start and end apart: 7, of which 4 were waited for; matrix products, arithmetic and copies ran while one was open for 0% of the time, Pallas kernels for 39%

profile of v2, /device:TPU:0, one launch (start us, length us, event | category | flops | bytes accessed | tf_op | source)
XLA Modules:
  0.0 67.6 jit_solution(1155232497119639305)
XLA Ops:
  0.0 3.0 %collective-permute-start.2 = (bf16[32,2048]{1,0:T(8,128)(2,1)}, bf16[32,2048]{1,0:T(8,128)(2,1)S(1)}, u32[]{:S(2)}, u32[]{:S(2)}) collective-permute-start(bf16[32,2048]{1,0:T(8,128)(2,1)} %bitcast.4), channel_id=1, source_target_pairs={{0,2},{1,3},{2,0},{3,1},{4,6},{5,7},{6,4},{7,5},{8,10},{9,11},{10,... | collective-permute-start | bytes 393224 | tf_op jit(solution)/shard_map/ppermute | solution.py:324
  3.0 0.1 collective-permute-start
  3.0 1.1 %copy-done.6 = f32[20,2048]{1,0:T(8,128)S(1)} copy-done((f32[20,2048]{1,0:T(8,128)S(1)}, f32[20,2048]{1,0:T(8,128)}, u32[]{:S(2)}) %copy-start.6) | copy-done | bytes 163864
  4.1 1.2 %copy-done.7 = f32[20,2048]{1,0:T(8,128)S(1)} copy-done((f32[20,2048]{1,0:T(8,128)S(1)}, f32[20,2048]{1,0:T(8,128)}, u32[]{:S(2)}) %copy-start.7) | copy-done | bytes 163864
  5.3 0.8 %copy-done.8 = s32[7,2048]{1,0:T(8,128)S(1)} copy-done((s32[7,2048]{1,0:T(8,128)S(1)}, s32[7,2048]{1,0:T(8,128)}, u32[]{:S(2)}) %copy-start.8) | copy-done | bytes 57368
  6.1 0.7 %copy-done.9 = f32[7,8]{1,0:T(8,128)S(1)} copy-done((f32[7,8]{1,0:T(8,128)S(1)}, f32[7,8]{1,0:T(8,128)}, u32[]{:S(2)}) %copy-start.9) | copy-done | bytes 248
  6.8 0.8 %copy-done.10 = s32[64,2]{1,0:T(8,128)S(1)} copy-done((s32[64,2]{1,0:T(8,128)S(1)}, s32[64,2]{1,0:T(8,128)}, u32[]{:S(2)}) %copy-start.10) | copy-done | bytes 536
  7.6 1.7 %prep.1 = (bf16[2048,128]{1,0:T(8,128)(2,1)S(1)}, f32[2048,128]{1,0:T(8,128)S(1)}, f32[32,2048]{1,0:T(8,128)S(1)}, f32[7,2048]{1,0:T(8,128)S(1)}, f32[64,1280]{1,0:T(8,128)S(1)}) custom-call(f32[20,2048]{1,0:T(8,128)S(1)} %copy-done.6, f32[20,2048]{1,0:T(8,128)S(1)} %copy-done.7, s32[7,2048]{1,0:T(8,128)S(1)} %copy-done.8, f32[7,8]{1,0:T(8,128)S(1)} %copy-done.9, ...), custom_call_target="tpu_custom_call" | custom-call | flops 2000000000 | bytes 4000000 | tf_op jit(solution)/shard_map/prep/pallas_call | solution.py:360
  9.3 0.0 copy-start.13
  9.3 3.6 %scale.1 = (bf16[2048,1280]{1,0:T(8,128)(2,1)S(1)}, bf16[2048,1280]{1,0:T(8,128)(2,1)S(1)}) custom-call(bf16[2048,1280]{1,0:T(8,128)(2,1)S(1)} %copy-done, bf16[2048,128]{1,0:T(8,128)(2,1)S(1)} %get-tuple-element.29.factors, f32[64,1280]{1,0:T(8,128)S(1)} %get-tuple-element.30.rows.after), custom_call_target="tpu_custom_call" | custom-call | flops 3000000000 | bytes 15728640 | tf_op jit(solution)/shard_map/scale/pallas_call | solution.py:378
  12.9 2.3 %copy-done.2 = bf16[2048,1280]{1,0:T(8,128)(2,1)} copy-done((bf16[2048,1280]{1,0:T(8,128)(2,1)}, bf16[2048,1280]{1,0:T(8,128)(2,1)S(1)}, u32[]{:S(2)}) %copy-start.2) | copy-done | bytes 5242904
  15.3 2.4 %copy-done.4 = bf16[2048,1280]{1,0:T(8,128)(2,1)} copy-done((bf16[2048,1280]{1,0:T(8,128)(2,1)}, bf16[2048,1280]{1,0:T(8,128)(2,1)S(1)}, u32[]{:S(2)}) %copy-start.4) | copy-done | bytes 5242904
  17.6 0.1 collective-permute-start.3
  17.8 0.1 broadcast_in_dim.6
  17.8 0.1 broadcast_in_dim_reshape.3.skip
  17.9 0.5 collective-permute-start.1
  18.5 0.8 %collective-permute-done.3 = bf16[64,2048]{1,0:T(8,128)(2,1)S(1)} collective-permute-done((bf16[64,2048]{1,0:T(8,128)(2,1)S(1)}, bf16[64,2048]{1,0:T(8,128)(2,1)S(1)}, u32[]{:S(2)}, u32[]{:S(2)}) %collective-permute-start.3) | collective-permute-done | bytes 262176 | tf_op jit(solution)/shard_map/ppermute | solution.py:324
  19.3 2.5 %copy-done.5 = bf16[2048,1280]{1,0:T(8,128)(2,1)S(1)} copy-done((bf16[2048,1280]{1,0:T(8,128)(2,1)S(1)}, bf16[2048,1280]{1,0:T(8,128)(2,1)}, u32[]{:S(2)}) %copy-start.5) | copy-done | bytes 5242904
  21.8 0.8 %state.1 = (f32[128,1280]{1,0:T(8,128)S(1)}, f32[8,1280]{1,0:T(8,128)S(1)}, bf16[136,1280]{1,0:T(8,128)(2,1)S(1)}) custom-call(bf16[2048,1280]{1,0:T(8,128)(2,1)S(1)} %copy-done.5, bf16[128,2048]{1,0:T(8,128)(2,1)S(1)} %pad_maximum_fusion.1.write_t, f32[64,1280]{1,0:T(8,128)S(1)} %get-tuple-element.30.rows.after), custom_call_target="tpu_custom_call" | custom-call | flops 671088640 | bytes 5242880 | tf_op jit(solution)/shard_map/state/pallas_call | solution.py:390
  22.6 1.9 %collective-permute-start.4 = (bf16[136,1280]{1,0:T(8,128)(2,1)S(1)}, bf16[136,1280]{1,0:T(8,128)(2,1)S(1)}, u32[]{:S(2)}, u32[]{:S(2)}) collective-permute-start(bf16[136,1280]{1,0:T(8,128)(2,1)S(1)} %get-tuple-element.32), channel_id=1, source_target_pairs={{0,4},{4,0},{8,12},{12,8},{16,20},{20,16},{24,28},{28,24},{1,5},{5... | collective-permute-start | bytes 1044488 | tf_op jit(solution)/shard_map/ppermute | solution.py:436
  24.6 2.5 %copy-done.3 = bf16[2048,1280]{1,0:T(8,128)(2,1)S(1)} copy-done((bf16[2048,1280]{1,0:T(8,128)(2,1)S(1)}, bf16[2048,1280]{1,0:T(8,128)(2,1)}, u32[]{:S(2)}) %copy-start.3) | copy-done | bytes 5242904
  27.1 3.9 %local.3 = (f32[512,1280]{1,0:T(8,128)S(1)}, f32[512,1280]{1,0:T(8,128)S(1)}, f32[3,128,1280]{2,1,0:T(8,128)S(1)}) custom-call(bf16[2048,1280]{1,0:T(8,128)(2,1)S(1)} %copy-done.1, bf16[2048,1280]{1,0:T(8,128)(2,1)S(1)} %copy-done.3, bf16[128,2048]{1,0:T(8,128)(2,1)S(1)} %pad_maximum_fusion.1.write_t, bf16[128,2048]{1,0:T(8,128)(2,1)S(1)} %pad_maximum_fusion.read_t, ...), custom_call_target="tpu_custom_call" | custom-call | flops 2621440000 | bytes 5242880 | tf_op jit(solution)/shard_map/local/pallas_call | solution.py:403
  31.0 2.0 %collective-permute-done.4.received.rest_0_ = bf16[136,1280]{1,0:T(8,128)(2,1)S(1)} collective-permute-done((bf16[136,1280]{1,0:T(8,128)(2,1)S(1)}, bf16[136,1280]{1,0:T(8,128)(2,1)S(1)}, u32[]{:S(2)}, u32[]{:S(2)}) %collective-permute-start.4) | collective-permute-done | bytes 348192 | tf_op jit(solution)/shard_map/ppermute | solution.py:436
  33.0 0.7 merge.2
  33.7 1.9 %collective-permute-start.5 = (bf16[136,1280]{1,0:T(8,128)(2,1)S(1)}, bf16[136,1280]{1,0:T(8,128)(2,1)S(1)}, u32[]{:S(2)}, u32[]{:S(2)}) collective-permute-start(bf16[136,1280]{1,0:T(8,128)(2,1)S(1)} %get-tuple-element.39), channel_id=1, source_target_pairs={{0,8},{4,12},{8,0},{12,4},{16,24},{20,28},{24,16},{28,20},{1,9},{5... | collective-permute-start | bytes 1044488 | tf_op jit(solution)/shard_map/ppermute | solution.py:436
  35.5 4.8 %local.4 = (f32[512,1280]{1,0:T(8,128)S(1)}, f32[512,1280]{1,0:T(8,128)S(1)}, f32[3,128,1280]{2,1,0:T(8,128)S(1)}) custom-call(bf16[2048,1280]{1,0:T(8,128)(2,1)S(1)} %copy-done.1, bf16[2048,1280]{1,0:T(8,128)(2,1)S(1)} %bitcast.3, bf16[128,2048]{1,0:T(8,128)(2,1)S(1)} %pad_maximum_fusion.1.write_t, bf16[128,2048]{1,0:T(8,128)(2,1)S(1)} %pad_maximum_fusion.read_t, ...), custom_call_target="tpu_custom_call" | custom-call | flops 2621440000 | bytes 5242880 | tf_op jit(solution)/shard_map/local/pallas_call | solution.py:403
  40.3 2.8 %collective-permute-done.5.received.rest_1_ = bf16[136,1280]{1,0:T(8,128)(2,1)S(1)} collective-permute-done((bf16[136,1280]{1,0:T(8,128)(2,1)S(1)}, bf16[136,1280]{1,0:T(8,128)(2,1)S(1)}, u32[]{:S(2)}, u32[]{:S(2)}) %collective-permute-start.5) | collective-permute-done | bytes 348192 | tf_op jit(solution)/shard_map/ppermute | solution.py:436
  43.2 1.5 %merge.3 = (f32[128,1280]{1,0:T(8,128)}, f32[8,1280]{1,0:T(8,128)S(1)}, bf16[136,1280]{1,0:T(8,128)(2,1)S(1)}) custom-call(s32[3]{0:T(128)S(1)} %shift-right-arithmetic_and_fusion.flags, bf16[136,1280]{1,0:T(8,128)(2,1)S(1)} %collective-permute-done.5.received.rest_1_, f32[128,1280]{1,0:T(8,128)S(1)} %get-tuple-element.40.mine, ...), custom_call_target="tpu_custom_call" | custom-call | flops 655360 | bytes 1966080 | tf_op jit(solution)/shard_map/merge/pallas_call | solution.py:443
  44.6 2.7 %collective-permute-start.6 = (bf16[136,1280]{1,0:T(8,128)(2,1)S(1)}, bf16[136,1280]{1,0:T(8,128)(2,1)S(1)}, u32[]{:S(2)}, u32[]{:S(2)}) collective-permute-start(bf16[136,1280]{1,0:T(8,128)(2,1)S(1)} %get-tuple-element.43), channel_id=1, source_target_pairs={{0,16},{4,20},{8,24},{12,28},{16,0},{20,4},{24,8},{28,12},{1,17},{... | collective-permute-start | bytes 1044488 | tf_op jit(solution)/shard_map/ppermute | solution.py:436
  47.4 11.4 %local.5 = (f32[1024,1280]{1,0:T(8,128)S(1)}, f32[1024,1280]{1,0:T(8,128)S(1)}, f32[3,128,1280]{2,1,0:T(8,128)}) custom-call(bf16[2048,1280]{1,0:T(8,128)(2,1)S(1)} %copy-done.1, bf16[2048,1280]{1,0:T(8,128)(2,1)S(1)} %bitcast.3, bf16[128,2048]{1,0:T(8,128)(2,1)S(1)} %pad_maximum_fusion.1.write_t, bf16[128,2048]{1,0:T(8,128)(2,1)S(1)} %pad_maximum_fusion.read_t, ...), custom_call_target="tpu_custom_call" | custom-call | flops 5242880000 | bytes 10485760 | tf_op jit(solution)/shard_map/local/pallas_call | solution.py:403
  58.7 2.8 %collective-permute-done.6.rest_2_ = bf16[136,1280]{1,0:T(8,128)(2,1)S(1)} collective-permute-done((bf16[136,1280]{1,0:T(8,128)(2,1)S(1)}, bf16[136,1280]{1,0:T(8,128)(2,1)S(1)}, u32[]{:S(2)}, u32[]{:S(2)}) %collective-permute-start.6) | collective-permute-done | bytes 348192 | tf_op jit(solution)/shard_map/ppermute | solution.py:436
  61.6 6.0 %final.1 = bf16[2048,1280]{1,0:T(8,128)(2,1)} custom-call(s32[3]{0:T(128)S(1)} %shift-right-arithmetic_and_fusion.flags, bf16[128,2048]{1,0:T(8,128)(2,1)S(1)} %pad_maximum_fusion.read_t, f32[7,2048]{1,0:T(8,128)S(1)} %get-tuple-element.28.weight_h, bf16[136,1280]{1,0:T(8,128)(2,1)S(1)} %collective-permute-done.4.received.rest_0_, ...), custom_call_target="tpu_custom_call" | custom-call | flops 2013265920 | bytes 15728640 | tf_op jit(solution)/shard_map/final/pallas_call | solution.py:454
  (32 shorter events, 0.2 us)
Async XLA Ops:
  0.0 17.6 %collective-permute-start.2 = (bf16[32,2048]{1,0:T(8,128)(2,1)}, bf16[32,2048]{1,0:T(8,128)(2,1)S(1)}, u32[]{:S(2)}, u32[]{:S(2)}) collective-permute-start(bf16[32,2048]{1,0:T(8,128)(2,1)} %bitcast.4), channel_id=1, source_target_pairs={{0,2},{1,3},{2,0},{3,1},{4,6},{5,7},{6,4},{7,5},{8,10},{9,11},{10,... | collective-permute-start | bytes 393224 | tf_op jit(solution)/shard_map/ppermute | solution.py:324
  3.0 6.3 %copy-start = (bf16[2048,1280]{1,0:T(8,128)(2,1)S(1)}, bf16[2048,1280]{1,0:T(8,128)(2,1)}, u32[]{:S(2)}) copy-start(bf16[2048,1280]{1,0:T(8,128)(2,1)} %mixer.7) | copy-start | bytes 15728644
  3.0 14.9 %collective-permute-start = (bf16[32,2048]{1,0:T(8,128)(2,1)}, bf16[32,2048]{1,0:T(8,128)(2,1)S(1)}, u32[]{:S(2)}, u32[]{:S(2)}) collective-permute-start(bf16[32,2048]{1,0:T(8,128)(2,1)} %bitcast.7), channel_id=1, source_target_pairs={{0,2},{1,3},{2,0},{3,1},{4,6},{5,7},{6,4},{7,5},{8,10},{9,11},{10,... | collective-permute-start | bytes 393224 | tf_op jit(solution)/shard_map/ppermute | solution.py:324
  3.0 1.1 %copy-start.6 = (f32[20,2048]{1,0:T(8,128)S(1)}, f32[20,2048]{1,0:T(8,128)}, u32[]{:S(2)}) copy-start(f32[20,2048]{1,0:T(8,128)} %log_decay.1) | copy-start | bytes 491524
  4.1 1.2 %copy-start.7 = (f32[20,2048]{1,0:T(8,128)S(1)}, f32[20,2048]{1,0:T(8,128)}, u32[]{:S(2)}) copy-start(f32[20,2048]{1,0:T(8,128)} %step_size.1) | copy-start | bytes 491524
  5.3 0.8 %copy-start.8 = (s32[7,2048]{1,0:T(8,128)S(1)}, s32[7,2048]{1,0:T(8,128)}, u32[]{:S(2)}) copy-start(s32[7,2048]{1,0:T(8,128)} %level_index.1) | copy-start | bytes 172036
  6.1 0.7 %copy-start.9 = (f32[7,8]{1,0:T(8,128)S(1)}, f32[7,8]{1,0:T(8,128)}, u32[]{:S(2)}) copy-start(f32[7,8]{1,0:T(8,128)} %level_table.1) | copy-start | bytes 676
  6.8 0.8 %copy-start.10 = (s32[64,2]{1,0:T(8,128)S(1)}, s32[64,2]{1,0:T(8,128)}, u32[]{:S(2)}) copy-start(s32[64,2]{1,0:T(8,128)} %constant.13.ranges) | copy-start | bytes 1540
  9.3 8.4 %copy-start.11 = (bf16[2048,32]{0,1:T(8,128)(2,1)S(1)}, bf16[2048,32]{0,1:T(8,128)(2,1)}, u32[]{:S(2)}) copy-start(bf16[2048,32]{0,1:T(8,128)(2,1)} %param.10) | copy-start | bytes 393220
  9.3 8.5 %copy-start.13 = (f32[20]{0:T(128)S(1)}, f32[20]{0:T(128)}, u32[]{:S(2)}) copy-start(f32[20]{0:T(128)} %param.14) | copy-start | bytes 244
  9.3 8.6 %copy-start.12 = (bf16[2048,32]{0,1:T(8,128)(2,1)S(1)}, bf16[2048,32]{0,1:T(8,128)(2,1)}, u32[]{:S(2)}) copy-start(bf16[2048,32]{0,1:T(8,128)(2,1)} %param.11) | copy-start | bytes 393220
  12.9 2.3 %copy-start.2 = (bf16[2048,1280]{1,0:T(8,128)(2,1)}, bf16[2048,1280]{1,0:T(8,128)(2,1)S(1)}, u32[]{:S(2)}) copy-start(bf16[2048,1280]{1,0:T(8,128)(2,1)S(1)} %get-tuple-element.35.scaled) | copy-start | bytes 15728644
  15.3 2.4 %copy-start.4 = (bf16[2048,1280]{1,0:T(8,128)(2,1)}, bf16[2048,1280]{1,0:T(8,128)(2,1)S(1)}, u32[]{:S(2)}) copy-start(bf16[2048,1280]{1,0:T(8,128)(2,1)S(1)} %get-tuple-element.31.to_total) | copy-start | bytes 15728644
  17.6 1.6 %collective-permute-start.3 = (bf16[64,2048]{1,0:T(8,128)(2,1)S(1)}, bf16[64,2048]{1,0:T(8,128)(2,1)S(1)}, u32[]{:S(2)}, u32[]{:S(2)}) collective-permute-start(bf16[64,2048]{1,0:T(8,128)(2,1)S(1)} %pad_maximum_fusion.3), channel_id=1, source_target_pairs={{0,1},{1,0},{2,3},{3,2},{4,5},{5,4},{6,7},{7,6},{8,9},{9,8},{10,11... | collective-permute-start | bytes 786440 | tf_op jit(solution)/shard_map/ppermute | solution.py:324
  17.9 6.6 %collective-permute-start.1 = (bf16[64,2048]{1,0:T(8,128)(2,1)S(1)}, bf16[64,2048]{1,0:T(8,128)(2,1)S(1)}, u32[]{:S(2)}, u32[]{:S(2)}) collective-permute-start(bf16[64,2048]{1,0:T(8,128)(2,1)S(1)} %pad_maximum_fusion.2), channel_id=1, source_target_pairs={{0,1},{1,0},{2,3},{3,2},{4,5},{5,4},{6,7},{7,6},{8,9},{9,8},{10,11... | collective-permute-start | bytes 786440 | tf_op jit(solution)/shard_map/ppermute | solution.py:324
  19.3 2.5 %copy-start.5 = (bf16[2048,1280]{1,0:T(8,128)(2,1)S(1)}, bf16[2048,1280]{1,0:T(8,128)(2,1)}, u32[]{:S(2)}) copy-start(bf16[2048,1280]{1,0:T(8,128)(2,1)} %copy-done.4) | copy-start | bytes 15728644
  21.8 2.8 %copy-start.1 = (bf16[2048,1280]{1,0:T(8,128)(2,1)S(1)}, bf16[2048,1280]{1,0:T(8,128)(2,1)}, u32[]{:S(2)}) copy-start(bf16[2048,1280]{1,0:T(8,128)(2,1)} %mixer.7) | copy-start | bytes 15728644
  21.8 13.8 %slice-start = ((s8[5242880]{0:T(1024)(128)(4,1)}), s8[1048576]{0:T(1024)(128)(4,1)S(1)}, s32[]{:S(2)}) async-start(s8[5242880]{0:T(1024)(128)(4,1)} %bitcast.2), calls=%async_computation | async-start | bytes 2097152
  22.6 10.3 %collective-permute-start.4 = (bf16[136,1280]{1,0:T(8,128)(2,1)S(1)}, bf16[136,1280]{1,0:T(8,128)(2,1)S(1)}, u32[]{:S(2)}, u32[]{:S(2)}) collective-permute-start(bf16[136,1280]{1,0:T(8,128)(2,1)S(1)} %get-tuple-element.32), channel_id=1, source_target_pairs={{0,4},{4,0},{8,12},{12,8},{16,20},{20,16},{24,28},{28,24},{1,5},{5... | collective-permute-start | bytes 1044488 | tf_op jit(solution)/shard_map/ppermute | solution.py:436
  24.6 2.5 %copy-start.3 = (bf16[2048,1280]{1,0:T(8,128)(2,1)S(1)}, bf16[2048,1280]{1,0:T(8,128)(2,1)}, u32[]{:S(2)}) copy-start(bf16[2048,1280]{1,0:T(8,128)(2,1)} %copy-done.2) | copy-start | bytes 15728644
  27.1 8.4 %slice-start.1 = ((s8[5242880]{0:T(1024)(128)(4,1)}), s8[4194304]{0:T(1024)(128)(4,1)S(1)}, s32[]{:S(2)}) async-start(s8[5242880]{0:T(1024)(128)(4,1)} %bitcast.2), calls=%async_computation.1 | async-start | bytes 8388608
  33.7 9.5 %collective-permute-start.5 = (bf16[136,1280]{1,0:T(8,128)(2,1)S(1)}, bf16[136,1280]{1,0:T(8,128)(2,1)S(1)}, u32[]{:S(2)}, u32[]{:S(2)}) collective-permute-start(bf16[136,1280]{1,0:T(8,128)(2,1)S(1)} %get-tuple-element.39), channel_id=1, source_target_pairs={{0,8},{4,12},{8,0},{12,4},{16,24},{20,28},{24,16},{28,20},{1,9},{5... | collective-permute-start | bytes 1044488 | tf_op jit(solution)/shard_map/ppermute | solution.py:436
  44.6 16.9 %collective-permute-start.6 = (bf16[136,1280]{1,0:T(8,128)(2,1)S(1)}, bf16[136,1280]{1,0:T(8,128)(2,1)S(1)}, u32[]{:S(2)}, u32[]{:S(2)}) collective-permute-start(bf16[136,1280]{1,0:T(8,128)(2,1)S(1)} %get-tuple-element.43), channel_id=1, source_target_pairs={{0,16},{4,20},{8,24},{12,28},{16,0},{20,4},{24,8},{28,12},{1,17},{... | collective-permute-start | bytes 1044488 | tf_op jit(solution)/shard_map/ppermute | solution.py:436

commit v3 on v2

--- a/solution.py
+++ b/solution.py
@@ -19,6 +19,7 @@
 VMEM_SPEC = pl.BlockSpec(memory_space=pltpu.VMEM)
 SMEM_SPEC = pl.BlockSpec(memory_space=pltpu.SMEM)
 ANY_SPEC = pl.BlockSpec(memory_space=pl.ANY)
+HBM_SPEC = pl.BlockSpec(memory_space=pltpu.HBM)
 
 
 def dot(a, b, dims=NN):
@@ -61,35 +62,47 @@
         self.after, self.run = 0, halves
         self.middle, self.upper, self.decay = 2 * halves, 2 * halves + blocks, 2 * halves + 2 * blocks
         self.total = 2 * halves + 3 * blocks
-        self.count = -(-(self.total + 1) // 16) * 16
+        self.skip = self.total + 8 - self.total % 8
+        self.count = -(-(self.skip + 8) // 16) * 16
 
     def ranges(self, tokens):
         halves = tokens // HALF
-        low, high = [], []
-        for a in range(halves):
-            low.append((a + 1) * HALF), high.append(tokens)
-        for a in range(halves):
-            low.append(0), high.append(a * HALF)
-        for c in range(halves // 2):
-            low.append(c * BLOCK), high.append(c * BLOCK + HALF)
-        for c in range(halves // 2):
-            low.append(c * BLOCK + HALF), high.append((c + 1) * BLOCK)
-        for c in range(halves // 2):
-            low.append(c * BLOCK), high.append((c + 1) * BLOCK)
-        low.append(0), high.append(tokens)
-        pad = self.count - len(low)
-        return jnp.array([low + [0] * pad, high + [0] * pad], jnp.int32).T
+        blocks = halves // 2
+        k = iota((self.count, 1), 0)
+        low = (k + 1) * HALF
+        high = jnp.full_like(k, tokens)
+        low = jnp.where(k >= self.run, 0, low)
+        high = jnp.where(k >= self.run, (k - self.run) * HALF, high)
+        for first, start, size in (
+            (self.middle, 0, HALF), (self.upper, HALF, HALF), (self.decay, 0, BLOCK)
+        ):
+            here = (k - first) * BLOCK + start
+            low = jnp.where(k >= first, here, low)
+            high = jnp.where(k >= first, here + size, high)
+        low = jnp.where(k >= self.total, 0, low)
+        high = jnp.where(k == self.total, tokens, jnp.where(k > self.total, 0, high))
+        return low, high
 
 
 def prep_kernel(
-    heads, padded, log_decay, step_size, level_index, level_table, ranges,
-    factors, columns, cum_h, weight_h, rows, decay, steps, packed,
+    heads, padded, layout, log_decay_far, step_size_far, level_index_far, level_table_far, gain_far,
+    factors, columns, cum_h, weight_h, rows,
+    log_decay, step_size, level_index, level_table, gain, decay, steps, packed, sems,
 ):
+    pairs = (
+        (log_decay_far, log_decay), (step_size_far, step_size), (level_index_far, level_index),
+        (level_table_far, level_table), (gain_far, gain),
+    )
+    copies = [pltpu.make_async_copy(far, near, sems.at[n]) for n, (far, near) in enumerate(pairs)]
+    for copy in copies:
+        copy.start()
     tokens = log_decay.shape[1]
     width = rows.shape[1]
     blocks = tokens // BLOCK
     decay[...] = jnp.zeros_like(decay)
     steps[...] = jnp.zeros_like(steps)
+    for copy in copies:
+        copy.wait()
     decay[0:heads, :] = log_decay[...]
     steps[0:heads, :] = step_size[...]
     lower = as_bf16(iota((BLOCK, BLOCK), 0) >= iota((BLOCK, BLOCK), 1))
@@ -118,7 +131,8 @@
         packed[padded : padded + levels, :] = weight_h[:, at]
         columns[at, :] = packed[...].T
     token = iota((rows.shape[0], tokens), 1)
-    chosen = as_bf16((token >= ranges[:, 0:1]) & (token < ranges[:, 1:2]))
+    begin, finish = layout.ranges(tokens)
+    chosen = as_bf16((token >= begin) & (token < finish))
     high, middle, low = three(decay[...])
     sums = (dot(chosen, low, NT) + dot(chosen, middle, NT)) + dot(chosen, high, NT)
     high, low = two(jnp.exp(sums))
@@ -127,6 +141,10 @@
     lane = iota((padded, width), 1)
     own = as_bf16((head <= lane) & (lane < head + per_head))
     rows[...] = dot(high.astype(BF16), own) + dot(low.astype(BF16), own)
+    gains = jnp.broadcast_to(gain[...], (8, heads))
+    high, middle, low = three(gains)
+    own = own[:heads]
+    rows[layout.skip : layout.skip + 8, :] = (dot(low, own) + dot(middle, own)) + dot(high, own)
 
 
 def scale_kernel(heads, padded, layout, mixer, factors, rows, scaled, to_total):
@@ -160,30 +178,43 @@
     mine_exp[...] = jnp.broadcast_to(total, mine_exp.shape)
 
 
-def merge_kernel(bit, flags, received, mine, mine_exp, after, merged, merged_exp, payload):
-    state = mine.shape[0]
+def upper_half(bit, width):
+    rank = lax.axis_index("seq")
+    return ((jnp.zeros((1, width), jnp.int32) + rank) >> bit) & 1 > 0
+
+
+def merge_kernel(bit, received, mine, mine_exp, after, payload, *more):
+    state, width = mine.shape
     extra = received[state:, :].astype(F32)
     other_exp = extra[0:1] + extra[1:2]
     own_exp = mine_exp[0:1, :]
-    upper = (jnp.zeros((1, mine.shape[1]), jnp.int32) + flags[bit]) > 0
+    upper = upper_half(bit, width)
     own_scale = jnp.where(upper, 1.0, other_exp)
     other_scale = jnp.where(upper, own_exp, 1.0)
     new = own_scale * mine[...] + other_scale * received[0:state, :].astype(F32)
-    merged[...] = new
+    payload[0:state, :] = new.astype(BF16)
     total = own_exp * other_exp
-    merged_exp[...] = jnp.broadcast_to(total, merged_exp.shape)
-    payload[0:state, :] = new.astype(BF16)
     payload[state:, :] = exp_rows(total, payload.shape[0] - state)
+    if more:
+        merged, merged_exp = more
+        merged[...] = new
+        merged_exp[...] = jnp.broadcast_to(total, merged_exp.shape)
+
+
+def join_kernel(first, second, joined):
+    joined[: first.shape[0], :] = first[...]
+    joined[first.shape[0] :, :] = second[...]
 
 
 def local_kernel(
     heads, padded, bits, first, count, layout, tile,
-    mixer, scaled, write_t, read_t, factors, columns, cum_h, weight_h, rows, skip, slots_in, after,
+    mixer, scaled, write_t, read_t, factors, columns, cum_h, weight_h, rows, slots_in, after,
     base, reach, slots, scores, inter, fresh,
 ):
     width = mixer.shape[1]
     per_head = width // heads
     heads_here = LANES // per_head
+    skip = rows[layout.skip : layout.skip + 1, :]
     wide = spread(2 * padded, padded, heads, width)
     if first == 0:
         slots[...] = jnp.zeros_like(slots)
@@ -272,22 +303,51 @@
     lax.fori_loop(0, count, block, 0)
 
 
-def final_kernel(starts, local_bits, bits, flags, read_t, weight_h, *rest):
+def bucket_rows(received, bits, state, width, wanted):
+    running = jnp.ones((1, width), F32)
+    out = []
+    for bit in range(bits):
+        upper = upper_half(bit, width)
+        if bit in wanted:
+            scale = jnp.where(upper, running, 0.0)
+            out.append((received[bit][0:state, :].astype(F32) * scale).astype(BF16))
+        if bit + 1 < bits:
+            extra = received[bit][state:, :].astype(F32)
+            running = jnp.where(upper, running * (extra[0:1] + extra[1:2]), running)
+    return jnp.concatenate(out, 0) if len(out) > 1 else out[0]
+
+
+def read_levels(read_t, weight_h, at, levels):
+    read_f = read_t[:, at].astype(F32)
+    queries = [(read_f * weight_h[level : level + 1, at]).astype(BF16) for level in levels]
+    return jnp.concatenate(queries, 0) if len(queries) > 1 else queries[0]
+
+
+def middle_kernel(starts, local_bits, bits, read_t, weight_h, *rest):
+    pieces = len(starts) - 1
+    received, rest = rest[:bits], rest[bits:]
+    bases, reaches, rest = rest[:pieces], rest[pieces : 2 * pieces], rest[2 * pieces :]
+    outs, buckets = rest[:pieces], rest[pieces]
+    buckets[...] = bucket_rows(received, bits, read_t.shape[0], buckets.shape[1], range(bits))
+    for piece in range(pieces):
+
+        def block(g, carry, piece=piece):
+            at = pl.ds(pl.multiple_of((starts[piece] + g) * BLOCK, BLOCK), BLOCK)
+            here = pl.ds(pl.multiple_of(g * BLOCK, BLOCK), BLOCK)
+            levels = [local_bits + 1 + bit for bit in range(bits)]
+            part = dot(read_levels(read_t, weight_h, at, levels), buckets[...], TN)
+            outs[piece][here, :] = bases[piece][here, :] + part * reaches[piece][here, :]
+            return carry
+
+        lax.fori_loop(0, starts[piece + 1] - starts[piece], block, 0)
+
+
+def final_kernel(starts, local_bits, bits, read_t, weight_h, *rest):
     pieces = len(starts) - 1
     received, rest = rest[:bits], rest[bits:]
     bases, reaches, rest = rest[:pieces], rest[pieces : 2 * pieces], rest[2 * pieces :]
     out, buckets, ready, sems = rest
-    width = out.shape[1]
-    state = read_t.shape[0]
-    running = jnp.ones((1, width), F32)
-    for bit in range(bits):
-        upper = (jnp.zeros((1, width), jnp.int32) + flags[bit]) > 0
-        extra = received[bit][state:, :].astype(F32)
-        scale = jnp.where(upper, running, 0.0)
-        buckets[bit * state : (bit + 1) * state, :] = (
-            received[bit][0:state, :].astype(F32) * scale
-        ).astype(BF16)
-        running = jnp.where(upper, running * (extra[0:1] + extra[1:2]), running)
+    buckets[...] = bucket_rows(received, bits, read_t.shape[0], out.shape[1], [bits - 1])
 
     def copy(c, at):
         return pltpu.make_async_copy(ready.at[c], out.at[pl.ds(at, BLOCK), :], sems.at[c])
@@ -297,17 +357,10 @@
         def block(g, carry, piece=piece):
             c = starts[piece] + g
             at = pl.multiple_of(c * BLOCK, BLOCK)
-            from_at = pl.ds(pl.multiple_of(g * BLOCK, BLOCK), BLOCK)
-            read_f = read_t[:, pl.ds(at, BLOCK)].astype(F32)
-            queries = jnp.concatenate(
-                [
-                    (read_f * weight_h[local_bits + 1 + bit : local_bits + 2 + bit, pl.ds(at, BLOCK)]).astype(BF16)
-                    for bit in range(bits)
-                ],
-                0,
-            )
-            part = dot(queries, buckets[...], TN)
-            ready[c] = (bases[piece][from_at, :] + part * reaches[piece][from_at, :]).astype(BF16)
+            here = pl.ds(pl.multiple_of(g * BLOCK, BLOCK), BLOCK)
+            query = read_levels(read_t, weight_h, pl.ds(at, BLOCK), [local_bits + bits])
+            part = dot(query, buckets[...], TN)
+            ready[c] = (bases[piece][here, :] + part * reaches[piece][here, :]).astype(BF16)
             copy(c, at).start()
             return carry
 
@@ -316,15 +369,25 @@
         copy(c, c * BLOCK).wait()
 
 
-def gather_columns(mine, axis):
-    pieces = mine
+def gather_columns(mine, axis, other):
+    pieces, _ = lax.optimization_barrier((mine, other)) if other is not None else (mine, None)
     size = lax.axis_size(axis)
     stride = size // 2
+    first = None
     while stride:
         other = lax.ppermute(pieces, axis, [(i, i ^ stride) for i in range(size)])
-        pieces = jnp.concatenate([pieces, other], 0)
+        first = other if first is None else first
+        pieces = pl.pallas_call(
+            join_kernel,
+            in_specs=[VMEM_SPEC] * 2,
+            out_specs=VMEM_SPEC,
+            out_shape=jax.ShapeDtypeStruct((2 * pieces.shape[0], pieces.shape[1]), BF16),
+            compiler_params=grant(2),
+            cost_estimate=cost(0, 4 * pieces.size),
+            name="join",
+        )(pieces, other)
         stride //= 2
-    return pieces
+    return pieces, first
 
 
 def cost(flops, bytes_accessed):
@@ -349,38 +412,42 @@
     padded = LANES // 4
     tile = 256
     layout = Rows(blocks)
-    rank = lax.axis_index("seq")
-    flags = (rank >> jnp.arange(device_bits, dtype=jnp.int32)) & 1
     sds = jax.ShapeDtypeStruct
 
-    write_t = gather_columns(write_map.T, "head")
-    read_t = gather_columns(read_map.T, "head")
+    write_t, arrived = gather_columns(write_map.T, "head", None)
+    read_t, _ = gather_columns(read_map.T, "head", arrived)
     state = write_t.shape[0]
 
     factors, columns, cum_h, weight_h, rows = pl.pallas_call(
-        functools.partial(prep_kernel, heads, padded),
-        in_specs=[VMEM_SPEC] * 5,
+        functools.partial(prep_kernel, heads, padded, layout),
+        in_specs=[HBM_SPEC] * 5,
         out_specs=(VMEM_SPEC,) * 5,
         out_shape=(
             sds((tokens, LANES), BF16), sds((tokens, LANES), F32), sds((padded, tokens), F32),
             sds((levels, tokens), F32), sds((layout.count, width), F32),
         ),
         scratch_shapes=[
+            pltpu.VMEM((heads, tokens), F32),
+            pltpu.VMEM((heads, tokens), F32),
+            pltpu.VMEM(level_index.shape, jnp.int32),
+            pltpu.VMEM(level_table.shape, F32),
+            pltpu.VMEM((1, heads), F32),
             pltpu.VMEM((padded, tokens), F32),
             pltpu.VMEM((padded, tokens), F32),
             pltpu.VMEM((LANES, BLOCK), F32),
+            pltpu.SemaphoreType.DMA((5,)),
         ],
-        compiler_params=grant(12),
+        compiler_params=grant(6),
         cost_estimate=cost(2_000_000_000, 4_000_000),
         name="prep",
-    )(log_decay, step_size, level_index, level_table, layout.ranges(tokens))
+    )(log_decay, step_size, level_index, level_table, skip_gain[None, :])
 
     scaled, to_total = pl.pallas_call(
         functools.partial(scale_kernel, heads, padded, layout),
         in_specs=[VMEM_SPEC] * 3,
         out_specs=(VMEM_SPEC,) * 2,
         out_shape=(sds((tokens, width), BF16),) * 2,
-        compiler_params=grant(8),
+        compiler_params=grant(4),
         cost_estimate=cost(3_000_000_000, tokens * width * 6),
         name="scale",
     )(mixer_input, factors, rows)
@@ -392,19 +459,17 @@
         in_specs=[VMEM_SPEC] * 3,
         out_specs=(VMEM_SPEC,) * 3,
         out_shape=carried,
-        compiler_params=grant(8),
+        compiler_params=grant(4),
         cost_estimate=cost(2 * tokens * width * state, tokens * width * 2),
         name="state",
     )(to_total, write_t, rows)
-
-    skip_row = jnp.repeat(skip_gain, per_head)[None, :]
 
     def local(first, count, slots, after):
         return pl.pallas_call(
             functools.partial(
                 local_kernel, heads, padded, local_bits, first, count, layout, tile
             ),
-            in_specs=[VMEM_SPEC] * 10 + [VMEM_SPEC, ANY_SPEC],
+            in_specs=[VMEM_SPEC] * 10 + [ANY_SPEC],
             out_specs=(VMEM_SPEC,) * 3,
             out_shape=(
                 sds((count * BLOCK, width), F32), sds((count * BLOCK, width), F32),
@@ -415,11 +480,11 @@
                 pltpu.VMEM((BLOCK, width), F32),
                 pltpu.VMEM((state, width), F32),
             ],
-            compiler_params=grant(12),
+            compiler_params=grant(8),
             cost_estimate=cost(count * BLOCK * width * 2 * 2000, count * BLOCK * width * 8),
             name="local",
         )(
-            mixer_input, scaled, write_t, read_t, factors, columns, cum_h, weight_h, rows, skip_row,
+            mixer_input, scaled, write_t, read_t, factors, columns, cum_h, weight_h, rows,
             slots, after,
         )
 
@@ -440,31 +505,49 @@
             reaches.append(reach)
         received.append(other)
         if bit + 1 < device_bits:
-            mine, mine_exp, payload = pl.pallas_call(
+            last = bit + 2 == device_bits
+            shapes = (carried[2],) if last else (carried[2],) + carried[:2]
+            payload, *more = pl.pallas_call(
                 functools.partial(merge_kernel, bit),
-                in_specs=[SMEM_SPEC] + [VMEM_SPEC] * 3 + [ANY_SPEC],
-                out_specs=(VMEM_SPEC,) * 3,
-                out_shape=carried,
-                compiler_params=grant(8),
+                in_specs=[VMEM_SPEC] * 3 + [ANY_SPEC],
+                out_specs=(VMEM_SPEC,) * len(shapes),
+                out_shape=shapes,
+                compiler_params=grant(4),
                 cost_estimate=cost(4 * state * width, state * width * 12),
                 name="merge",
-            )(flags, other, mine, mine_exp, slots)
-            after = mine_exp
+            )(other, mine, mine_exp, slots)
+            if more:
+                mine, mine_exp = more
+            after = payload
+
+    if device_bits > 1:
+        count = len(bases)
+        bases = pl.pallas_call(
+            functools.partial(middle_kernel, starts, local_bits, device_bits - 1),
+            in_specs=[VMEM_SPEC] * (2 + device_bits - 1 + 2 * count),
+            out_specs=(VMEM_SPEC,) * count,
+            out_shape=tuple(sds(base.shape, F32) for base in bases),
+            input_output_aliases={2 + device_bits - 1 + k: k for k in range(count)},
+            scratch_shapes=[pltpu.VMEM(((device_bits - 1) * state, width), BF16)],
+            compiler_params=grant(4),
+            cost_estimate=cost(2 * tokens * width * state * 2, tokens * width * 6),
+            name="middle",
+        )(read_t, weight_h, *received[:-1], *bases, *reaches)
 
     return pl.pallas_call(
         functools.partial(final_kernel, starts, local_bits, device_bits),
-        in_specs=[SMEM_SPEC] + [VMEM_SPEC] * (2 + device_bits + 2 * len(bases)),
+        in_specs=[VMEM_SPEC] * (2 + device_bits + 2 * len(bases)),
         out_specs=ANY_SPEC,
         out_shape=sds((tokens, width), BF16),
         scratch_shapes=[
-            pltpu.VMEM((device_bits * state, width), BF16),
+            pltpu.VMEM((state, width), BF16),
             pltpu.VMEM((blocks, BLOCK, width), BF16),
             pltpu.SemaphoreType.DMA((blocks,)),
         ],
-        compiler_params=grant(12),
+        compiler_params=grant(8),
         cost_estimate=cost(2 * tokens * width * state * device_bits, tokens * width * 6),
         name="final",
-    )(flags, read_t, weight_h, *received, *bases, *reaches)
+    )(read_t, weight_h, *received, *bases, *reaches)
 
 
 def solution(mesh):

time: 67.9 us -> 62.5 us (0.920)
  local copies, waits for them, and re-layouts: 14.4 us -> 4.05 us
  waiting for transfers between devices: 8.41 us -> 10.8 us
  Pallas kernels: 34.4 us -> 36 us
  starting transfers between devices: 10.1 us -> 11.2 us
    unnamed x32 -> x16, local copies, waits for them, and re-layouts: 14.2 us -> 4.04 us
    ppermute x4, waiting for transfers between devices: 0.77 us -> 3.71 us  [gather_columns(): other = lax.ppermute(pieces, axis, [(i, i ^ stride) for i in range(size)])]
    pallas_call x3 -> x8, Pallas kernels: 3.8 us -> 6.56 us  [the longest x1 3.67 us: on_device(): pl.pallas_call(functools.partial(middle_kernel, starts, local_bits, devic...]
    pallas_call x1, Pallas kernels: 6.04 us -> 4.11 us  [on_device(): pl.pallas_call(functools.partial(final_kernel, starts, local_bits, device...]
    ppermute x4, starting transfers between devices: 3.64 us -> 5.32 us  [gather_columns(): other = lax.ppermute(pieces, axis, [(i, i ^ stride) for i in range(size)])]
    pallas_call x3, Pallas kernels: 20.1 us -> 20.8 us  [local(): pl.pallas_call(functools.partial(local_kernel, heads, padded, local_bits,...]
  transfers between devices with their start and end apart: 7 -> 7, of which waited for: 4 -> 3; matrix products, arithmetic and copies ran while one was open for 0% -> 0% of each run, Pallas kernels for 39% -> 51%
where the time goes in v3:
time: 62.5 us; the launch traced here: 62.2 us
  Pallas kernels  36 us (58%)
  starting transfers between devices  11.2 us (18%)
  waiting for transfers between devices  10.8 us (17%)
  local copies, waits for them, and re-layouts  4.05 us (6%)
    pallas_call x3, Pallas kernels, local(): pl.pallas_call(functools.partial(local_kernel, heads, padded, local_bits,...  20.8 us
    ppermute x3, waiting for transfers between devices, on_device(): lax.ppermute(payload, 'seq', [(i, i ^ 1 << bit) for i in range(ranks)])  7.1 us
    ppermute x3, starting transfers between devices, on_device(): lax.ppermute(payload, 'seq', [(i, i ^ 1 << bit) for i in range(ranks)])  5.88 us
    ppermute x4, starting transfers between devices, gather_columns(): other = lax.ppermute(pieces, axis, [(i, i ^ stride) for i in range(size)])  5.32 us
    pallas_call x1, Pallas kernels, on_device(): pl.pallas_call(functools.partial(final_kernel, starts, local_bits, device...  4.11 us
    unnamed x16, local copies, waits for them, and re-layouts  4.04 us
    ppermute x4, waiting for transfers between devices, gather_columns(): other = lax.ppermute(pieces, axis, [(i, i ^ stride) for i in range(size)])  3.71 us
    pallas_call x1, Pallas kernels, on_device(): pl.pallas_call(functools.partial(scale_kernel, heads, padded, layout), in...  3.69 us
  transfers between devices with their start and end apart: 7, of which 3 were waited for; matrix products, arithmetic and copies ran while one was open for 0% of the time, Pallas kernels for 51%

profile of v3, /device:TPU:0, one launch (start us, length us, event | category | flops | bytes accessed | tf_op | source)
XLA Modules:
  0.0 62.2 jit_solution(1495555896868748034)
XLA Ops:
  0.0 3.0 %collective-permute-start = (bf16[32,2048]{1,0:T(8,128)(2,1)}, bf16[32,2048]{1,0:T(8,128)(2,1)S(1)}, u32[]{:S(2)}, u32[]{:S(2)}) collective-permute-start(bf16[32,2048]{1,0:T(8,128)(2,1)} %bitcast.3), channel_id=1, source_target_pairs={{0,2},{1,3},{2,0},{3,1},{4,6},{5,7},{6,4},{7,5},{8,10},{9,11},{10,... | collective-permute-start | bytes 393224 | tf_op jit(solution)/shard_map/ppermute | solution.py:378
  3.0 3.7 %collective-permute-done.second = bf16[32,2048]{1,0:T(8,128)(2,1)S(1)} collective-permute-done((bf16[32,2048]{1,0:T(8,128)(2,1)}, bf16[32,2048]{1,0:T(8,128)(2,1)S(1)}, u32[]{:S(2)}, u32[]{:S(2)}) %collective-permute-start) | collective-permute-done | bytes 131104 | tf_op jit(solution)/shard_map/ppermute | solution.py:378
  6.7 1.7 %collective-permute-start.1 = (bf16[32,2048]{1,0:T(8,128)(2,1)}, bf16[32,2048]{1,0:T(8,128)(2,1)S(1)}, u32[]{:S(2)}, u32[]{:S(2)}) collective-permute-start(bf16[32,2048]{1,0:T(8,128)(2,1)} %bitcast.5), channel_id=1, source_target_pairs={{0,2},{1,3},{2,0},{3,1},{4,6},{5,7},{6,4},{7,5},{8,10},{9,11},{10,... | collective-permute-start | bytes 393224 | tf_op jit(solution)/shard_map/ppermute | solution.py:378
  8.4 0.9 %copy-done.3 = f32[20,2048]{1,0:T(8,128)S(1)} copy-done((f32[20,2048]{1,0:T(8,128)S(1)}, f32[20,2048]{1,0:T(8,128)}, u32[]{:S(2)}) %copy-start.3) | copy-done | bytes 163864
  9.3 0.9 %copy-done.4 = f32[20,2048]{1,0:T(8,128)S(1)} copy-done((f32[20,2048]{1,0:T(8,128)S(1)}, f32[20,2048]{1,0:T(8,128)}, u32[]{:S(2)}) %copy-start.4) | copy-done | bytes 163864
  10.3 0.8 %copy-done.5 = s32[7,2048]{1,0:T(8,128)S(1)} copy-done((s32[7,2048]{1,0:T(8,128)S(1)}, s32[7,2048]{1,0:T(8,128)}, u32[]{:S(2)}) %copy-start.5) | copy-done | bytes 57368
  11.1 0.7 %copy-done.6 = f32[7,8]{1,0:T(8,128)S(1)} copy-done((f32[7,8]{1,0:T(8,128)S(1)}, f32[7,8]{1,0:T(8,128)}, u32[]{:S(2)}) %copy-start.6) | copy-done | bytes 248
  11.8 0.7 %copy-done.7 = f32[20]{0:T(128)S(1)} copy-done((f32[20]{0:T(128)S(1)}, f32[20]{0:T(128)}, u32[]{:S(2)}) %copy-start.7) | copy-done | bytes 104
  12.5 2.5 %prep.1 = (bf16[2048,128]{1,0:T(8,128)(2,1)S(1)}, f32[2048,128]{1,0:T(8,128)S(1)}, f32[32,2048]{1,0:T(8,128)S(1)}, f32[7,2048]{1,0:T(8,128)S(1)}, f32[80,1280]{1,0:T(8,128)S(1)}) custom-call(f32[20,2048]{1,0:T(8,128)S(1)} %copy-done.3, f32[20,2048]{1,0:T(8,128)S(1)} %copy-done.4, s32[7,2048]{1,0:T(8,128)S(1)} %copy-done.5, f32[7,8]{1,0:T(8,128)S(1)} %copy-done.6, ...), custom_call_target="tpu_custom_call" | custom-call | flops 2000000000 | bytes 4000000 | tf_op jit(solution)/shard_map/prep/pallas_call | solution.py:421
  14.9 0.0 copy-done.1
  15.0 0.1 collective-permute-start.3
  15.1 0.0 collective-permute-done.1.second
  15.1 0.0 copy-done.2
  15.1 0.5 collective-permute-start.2
  15.7 0.0 copy-done
  15.7 3.7 %scale.1 = (bf16[2048,1280]{1,0:T(8,128)(2,1)S(1)}, bf16[2048,1280]{1,0:T(8,128)(2,1)S(1)}) custom-call(bf16[2048,1280]{1,0:T(8,128)(2,1)S(1)} %copy-done, bf16[2048,128]{1,0:T(8,128)(2,1)S(1)} %get-tuple-element.32.factors, f32[80,1280]{1,0:T(8,128)S(1)} %get-tuple-element.33.rows.after), custom_call_target="tpu_custom_call" | custom-call | flops 3000000000 | bytes 15728640 | tf_op jit(solution)/shard_map/scale/pallas_call | solution.py:445
  19.4 0.0 collective-permute-done.3.second
  19.4 0.9 %state.1 = (f32[128,1280]{1,0:T(8,128)S(1)}, f32[8,1280]{1,0:T(8,128)S(1)}, bf16[136,1280]{1,0:T(8,128)(2,1)S(1)}) custom-call(bf16[2048,1280]{1,0:T(8,128)(2,1)S(1)} %get-tuple-element.34.to_total, bf16[128,2048]{1,0:T(8,128)(2,1)S(1)} %join.7.write_t, f32[80,1280]{1,0:T(8,128)S(1)} %get-tuple-element.33.rows.after), custom_call_target="tpu_custom_call" | custom-call | flops 671088640 | bytes 5242880 | tf_op jit(solution)/shard_map/state/pallas_call | solution.py:457
  20.3 1.6 %collective-permute-start.4 = (bf16[136,1280]{1,0:T(8,128)(2,1)S(1)}, bf16[136,1280]{1,0:T(8,128)(2,1)S(1)}, u32[]{:S(2)}, u32[]{:S(2)}) collective-permute-start(bf16[136,1280]{1,0:T(8,128)(2,1)S(1)} %get-tuple-element.35), channel_id=1, source_target_pairs={{0,4},{4,0},{8,12},{12,8},{16,20},{20,16},{24,28},{28,24},{1,5},{5... | collective-permute-start | bytes 1044488 | tf_op jit(solution)/shard_map/ppermute | solution.py:501
  21.9 0.0 collective-permute-done.2.second
  21.9 4.1 %local.3 = (f32[512,1280]{1,0:T(8,128)S(1)}, f32[512,1280]{1,0:T(8,128)S(1)}, f32[3,128,1280]{2,1,0:T(8,128)S(1)}) custom-call(bf16[2048,1280]{1,0:T(8,128)(2,1)S(1)} %copy-done, bf16[2048,1280]{1,0:T(8,128)(2,1)S(1)} %get-tuple-element.38.scaled, bf16[128,2048]{1,0:T(8,128)(2,1)S(1)} %join.7.write_t, bf16[128,2048]{1,0:T(8,128)(2,1)S(1)} %join.5.read_t, ...), custom_call_target="tpu_custom_call" | custom-call | flops 2621440000 | bytes 5242880 | tf_op jit(solution)/shard_map/local/pallas_call | solution.py:468
  26.0 4.4 %collective-permute-done.4.received.rest_0_ = bf16[136,1280]{1,0:T(8,128)(2,1)S(1)} collective-permute-done((bf16[136,1280]{1,0:T(8,128)(2,1)S(1)}, bf16[136,1280]{1,0:T(8,128)(2,1)S(1)}, u32[]{:S(2)}, u32[]{:S(2)}) %collective-permute-start.4) | collective-permute-done | bytes 348192 | tf_op jit(solution)/shard_map/ppermute | solution.py:501
  30.4 0.2 merge.2
  30.6 1.6 %collective-permute-start.5 = (bf16[136,1280]{1,0:T(8,128)(2,1)S(1)}, bf16[136,1280]{1,0:T(8,128)(2,1)S(1)}, u32[]{:S(2)}, u32[]{:S(2)}) collective-permute-start(bf16[136,1280]{1,0:T(8,128)(2,1)S(1)} %get-tuple-element.42.after), channel_id=1, source_target_pairs={{0,8},{4,12},{8,0},{12,4},{16,24},{20,28},{24,16},{28,20},{1,9},{5... | collective-permute-start | bytes 1044488 | tf_op jit(solution)/shard_map/ppermute | solution.py:501
  32.2 4.9 %local.4 = (f32[512,1280]{1,0:T(8,128)S(1)}, f32[512,1280]{1,0:T(8,128)S(1)}, f32[3,128,1280]{2,1,0:T(8,128)S(1)}) custom-call(bf16[2048,1280]{1,0:T(8,128)(2,1)S(1)} %copy-done, bf16[2048,1280]{1,0:T(8,128)(2,1)S(1)} %get-tuple-element.38.scaled, bf16[128,2048]{1,0:T(8,128)(2,1)S(1)} %join.7.write_t, bf16[128,2048]{1,0:T(8,128)(2,1)S(1)} %join.5.read_t, ...), custom_call_target="tpu_custom_call" | custom-call | flops 2621440000 | bytes 5242880 | tf_op jit(solution)/shard_map/local/pallas_call | solution.py:468
  37.2 2.7 %collective-permute-done.5.received.rest_1_ = bf16[136,1280]{1,0:T(8,128)(2,1)S(1)} collective-permute-done((bf16[136,1280]{1,0:T(8,128)(2,1)S(1)}, bf16[136,1280]{1,0:T(8,128)(2,1)S(1)}, u32[]{:S(2)}, u32[]{:S(2)}) %collective-permute-start.5) | collective-permute-done | bytes 348192 | tf_op jit(solution)/shard_map/ppermute | solution.py:501
  39.9 0.1 merge.3.after
  40.0 2.7 %collective-permute-start.6 = (bf16[136,1280]{1,0:T(8,128)(2,1)S(1)}, bf16[136,1280]{1,0:T(8,128)(2,1)S(1)}, u32[]{:S(2)}, u32[]{:S(2)}) collective-permute-start(bf16[136,1280]{1,0:T(8,128)(2,1)S(1)} %merge.3.after), channel_id=1, source_target_pairs={{0,16},{4,20},{8,24},{12,28},{16,0},{20,4},{24,8},{28,12},{1,17},{... | collective-permute-start | bytes 1044488 | tf_op jit(solution)/shard_map/ppermute | solution.py:501
  42.7 11.7 %local.5 = (f32[1024,1280]{1,0:T(8,128)S(1)}, f32[1024,1280]{1,0:T(8,128)S(1)}, f32[3,128,1280]{2,1,0:T(8,128)}) custom-call(bf16[2048,1280]{1,0:T(8,128)(2,1)S(1)} %copy-done, bf16[2048,1280]{1,0:T(8,128)(2,1)S(1)} %get-tuple-element.38.scaled, bf16[128,2048]{1,0:T(8,128)(2,1)S(1)} %join.7.write_t, bf16[128,2048]{1,0:T(8,128)(2,1)S(1)} %join.5.read_t, ...), custom_call_target="tpu_custom_call" | custom-call | flops 5242880000 | bytes 10485760 | tf_op jit(solution)/shard_map/local/pallas_call | solution.py:468
  54.4 3.7 %middle.1 = (f32[512,1280]{1,0:T(8,128)S(1)}, f32[512,1280]{1,0:T(8,128)S(1)}, f32[1024,1280]{1,0:T(8,128)S(1)}) custom-call(bf16[128,2048]{1,0:T(8,128)(2,1)S(1)} %join.5.read_t, f32[7,2048]{1,0:T(8,128)S(1)} %get-tuple-element.31.weight_h, ...), custom_call_target="tpu_custom_call", output_to_operand_aliasing={{0}: (4, {}), {1}: (5, {}), {2}: (6, {})} | custom-call | flops 1342177280 | bytes 15728640 | tf_op jit(solution)/shard_map/middle/pallas_call | solution.py:525
  58.1 0.0 collective-permute-done.6.rest_2_
  58.1 4.1 %final.1 = bf16[2048,1280]{1,0:T(8,128)(2,1)} custom-call(bf16[128,2048]{1,0:T(8,128)(2,1)S(1)} %join.5.read_t, f32[7,2048]{1,0:T(8,128)S(1)} %get-tuple-element.31.weight_h, bf16[136,1280]{1,0:T(8,128)(2,1)S(1)} %collective-permute-done.4.received.rest_0_, bf16[136,1280]{1,0:T(8,128)(2,1)S(1)} %collective-permute-done.5.received.rest_1_, ...), custom_call_target="tpu_custom_call" | custom-call | flops 2013265920 | bytes 15728640 | tf_op jit(solution)/shard_map/final/pallas_call | solution.py:537
  (13 shorter events, 0.1 us)
Async XLA Ops:
  0.0 6.7 %collective-permute-start = (bf16[32,2048]{1,0:T(8,128)(2,1)}, bf16[32,2048]{1,0:T(8,128)(2,1)S(1)}, u32[]{:S(2)}, u32[]{:S(2)}) collective-permute-start(bf16[32,2048]{1,0:T(8,128)(2,1)} %bitcast.3), channel_id=1, source_target_pairs={{0,2},{1,3},{2,0},{3,1},{4,6},{5,7},{6,4},{7,5},{8,10},{9,11},{10,... | collective-permute-start | bytes 393224 | tf_op jit(solution)/shard_map/ppermute | solution.py:378
  6.7 8.4 %collective-permute-start.1 = (bf16[32,2048]{1,0:T(8,128)(2,1)}, bf16[32,2048]{1,0:T(8,128)(2,1)S(1)}, u32[]{:S(2)}, u32[]{:S(2)}) collective-permute-start(bf16[32,2048]{1,0:T(8,128)(2,1)} %bitcast.5), channel_id=1, source_target_pairs={{0,2},{1,3},{2,0},{3,1},{4,6},{5,7},{6,4},{7,5},{8,10},{9,11},{10,... | collective-permute-start | bytes 393224 | tf_op jit(solution)/shard_map/ppermute | solution.py:378
  8.4 0.9 %copy-start.3 = (f32[20,2048]{1,0:T(8,128)S(1)}, f32[20,2048]{1,0:T(8,128)}, u32[]{:S(2)}) copy-start(f32[20,2048]{1,0:T(8,128)} %log_decay_far.1) | copy-start | bytes 491524
  9.3 0.9 %copy-start.4 = (f32[20,2048]{1,0:T(8,128)S(1)}, f32[20,2048]{1,0:T(8,128)}, u32[]{:S(2)}) copy-start(f32[20,2048]{1,0:T(8,128)} %step_size_far.1) | copy-start | bytes 491524
  10.3 0.8 %copy-start.5 = (s32[7,2048]{1,0:T(8,128)S(1)}, s32[7,2048]{1,0:T(8,128)}, u32[]{:S(2)}) copy-start(s32[7,2048]{1,0:T(8,128)} %level_index_far.1) | copy-start | bytes 172036
  11.1 0.7 %copy-start.6 = (f32[7,8]{1,0:T(8,128)S(1)}, f32[7,8]{1,0:T(8,128)}, u32[]{:S(2)}) copy-start(f32[7,8]{1,0:T(8,128)} %level_table_far.1) | copy-start | bytes 676
  11.8 0.7 %copy-start.7 = (f32[20]{0:T(128)S(1)}, f32[20]{0:T(128)}, u32[]{:S(2)}) copy-start(f32[20]{0:T(128)} %param.13) | copy-start | bytes 244
  12.5 2.5 %copy-start.1 = (bf16[2048,32]{0,1:T(8,128)(2,1)S(1)}, bf16[2048,32]{0,1:T(8,128)(2,1)}, u32[]{:S(2)}) copy-start(bf16[2048,32]{0,1:T(8,128)(2,1)} %param.9) | copy-start | bytes 393220
  12.5 2.6 %copy-start.2 = (bf16[2048,32]{0,1:T(8,128)(2,1)S(1)}, bf16[2048,32]{0,1:T(8,128)(2,1)}, u32[]{:S(2)}) copy-start(bf16[2048,32]{0,1:T(8,128)(2,1)} %param.10) | copy-start | bytes 393220
  12.5 3.2 %copy-start = (bf16[2048,1280]{1,0:T(8,128)(2,1)S(1)}, bf16[2048,1280]{1,0:T(8,128)(2,1)}, u32[]{:S(2)}) copy-start(bf16[2048,1280]{1,0:T(8,128)(2,1)} %mixer.7) | copy-start | bytes 15728644
  15.0 4.4 %collective-permute-start.3 = (bf16[64,2048]{1,0:T(8,128)(2,1)S(1)}, bf16[64,2048]{1,0:T(8,128)(2,1)S(1)}, u32[]{:S(2)}, u32[]{:S(2)}) collective-permute-start(bf16[64,2048]{1,0:T(8,128)(2,1)S(1)} %join.6.first), channel_id=1, source_target_pairs={{0,1},{1,0},{2,3},{3,2},{4,5},{5,4},{6,7},{7,6},{8,9},{9,8},{10,11... | collective-permute-start | bytes 786440 | tf_op jit(solution)/shard_map/ppermute | solution.py:378
  15.1 6.7 %collective-permute-start.2 = (bf16[64,2048]{1,0:T(8,128)(2,1)S(1)}, bf16[64,2048]{1,0:T(8,128)(2,1)S(1)}, u32[]{:S(2)}, u32[]{:S(2)}) collective-permute-start(bf16[64,2048]{1,0:T(8,128)(2,1)S(1)} %join.4.first), channel_id=1, source_target_pairs={{0,1},{1,0},{2,3},{3,2},{4,5},{5,4},{6,7},{7,6},{8,9},{9,8},{10,11... | collective-permute-start | bytes 786440 | tf_op jit(solution)/shard_map/ppermute | solution.py:378
  20.3 10.2 %collective-permute-start.4 = (bf16[136,1280]{1,0:T(8,128)(2,1)S(1)}, bf16[136,1280]{1,0:T(8,128)(2,1)S(1)}, u32[]{:S(2)}, u32[]{:S(2)}) collective-permute-start(bf16[136,1280]{1,0:T(8,128)(2,1)S(1)} %get-tuple-element.35), channel_id=1, source_target_pairs={{0,4},{4,0},{8,12},{12,8},{16,20},{20,16},{24,28},{28,24},{1,5},{5... | collective-permute-start | bytes 1044488 | tf_op jit(solution)/shard_map/ppermute | solution.py:501
  30.6 9.3 %collective-permute-start.5 = (bf16[136,1280]{1,0:T(8,128)(2,1)S(1)}, bf16[136,1280]{1,0:T(8,128)(2,1)S(1)}, u32[]{:S(2)}, u32[]{:S(2)}) collective-permute-start(bf16[136,1280]{1,0:T(8,128)(2,1)S(1)} %get-tuple-element.42.after), channel_id=1, source_target_pairs={{0,8},{4,12},{8,0},{12,4},{16,24},{20,28},{24,16},{28,20},{1,9},{5... | collective-permute-start | bytes 1044488 | tf_op jit(solution)/shard_map/ppermute | solution.py:501
  40.0 18.1 %collective-permute-start.6 = (bf16[136,1280]{1,0:T(8,128)(2,1)S(1)}, bf16[136,1280]{1,0:T(8,128)(2,1)S(1)}, u32[]{:S(2)}, u32[]{:S(2)}) collective-permute-start(bf16[136,1280]{1,0:T(8,128)(2,1)S(1)} %merge.3.after), channel_id=1, source_target_pairs={{0,16},{4,20},{8,24},{12,28},{16,0},{20,4},{24,8},{28,12},{1,17},{... | collective-permute-start | bytes 1044488 | tf_op jit(solution)/shard_map/ppermute | solution.py:501

commit v4 on v3

--- a/solution.py
+++ b/solution.py
@@ -6,6 +6,7 @@
 from jax.experimental import pallas as pl
 from jax.experimental.pallas import tpu as pltpu
 from jax.sharding import PartitionSpec as P
+
 
 BLOCK = 256
 HALF = BLOCK // 2
@@ -168,14 +169,24 @@
     return jnp.where(where == 0, high, jnp.where(where == 1, total - high, 0.0)).astype(BF16)
 
 
-def state_kernel(layout, to_total, write_t, rows, mine, mine_exp, payload):
+def own_columns(width):
+    rank = lax.axis_index("seq")
+    mine = (rank & 1) * (width // 2)
+    other = width // 2 - mine
+    aligned = lambda at: pl.ds(pl.multiple_of(at, LANES), width // 2)
+    return aligned(mine), aligned(other)
+
+
+def state_kernel(layout, to_total, write_t, rows, first, second, mine, mine_exp, whole):
     state = write_t.shape[0]
-    new = dot(write_t[...], to_total[...])
-    mine[...] = new
-    payload[0:state, :] = new.astype(BF16)
-    total = rows[layout.total : layout.total + 1, :]
-    payload[state:, :] = exp_rows(total, payload.shape[0] - state)
-    mine_exp[...] = jnp.broadcast_to(total, mine_exp.shape)
+    own, other = own_columns(whole.shape[1])
+    whole[...] = dot(write_t[...], to_total[...])
+    for payload, at in ((first, other), (second, own)):
+        payload[0:state, :] = whole[:, at].astype(BF16)
+        total = rows[layout.total : layout.total + 1, at]
+        payload[state:, :] = exp_rows(total, payload.shape[0] - state)
+    mine[...] = whole[:, own]
+    mine_exp[...] = jnp.broadcast_to(rows[layout.total : layout.total + 1, own], mine_exp.shape)
 
 
 def upper_half(bit, width):
@@ -201,7 +212,8 @@
         merged_exp[...] = jnp.broadcast_to(total, merged_exp.shape)
 
 
-def join_kernel(first, second, joined):
+def join_kernel(first, second, *rest):
+    joined = rest[-1]
     joined[: first.shape[0], :] = first[...]
     joined[first.shape[0] :, :] = second[...]
 
@@ -209,98 +221,99 @@
 def local_kernel(
     heads, padded, bits, first, count, layout, tile,
     mixer, scaled, write_t, read_t, factors, columns, cum_h, weight_h, rows, slots_in, after,
-    base, reach, slots, scores, inter, fresh,
+    base, reach, slots, scores, narrow, off_scores, queries,
 ):
     width = mixer.shape[1]
+    state = write_t.shape[0]
     per_head = width // heads
     heads_here = LANES // per_head
-    skip = rows[layout.skip : layout.skip + 1, :]
     wide = spread(2 * padded, padded, heads, width)
-    if first == 0:
-        slots[...] = jnp.zeros_like(slots)
-    else:
-        slots[...] = slots_in[...]
-
-    def block(g, carry):
-        c = first + g
-        at = pl.ds(pl.multiple_of(c * BLOCK, BLOCK), BLOCK)
-        out_at = pl.ds(pl.multiple_of(g * BLOCK, BLOCK), BLOCK)
-        read = read_t[:, at]
-        write = write_t[:, at]
-
-        inter[...] = jnp.zeros_like(inter)
-        for bit in range(bits):
-
-            @pl.when((c >> bit) & 1 == 1)
-            def _(bit=bit):
-                query = (read.astype(F32) * weight_h[bit + 1 : bit + 2, at]).astype(BF16)
-                inter[...] += dot(query, slots[bit].astype(BF16), TN)
-
-        weighted = dot(read, write, TN) * columns[at, padded : padded + 1]
-        causal = iota((HALF, HALF), 0) >= iota((HALF, HALF), 1)
-        off_scores = weighted[HALF:, :HALF].astype(BF16)
+    causal = iota((HALF, HALF), 0) >= iota((HALF, HALF), 1)
+    lane = iota((HALF, LANES), 1)
+    own = [as_bf16((lane >= k * per_head) & (lane < (k + 1) * per_head)) for k in range(heads_here)]
+    live = [bit for bit in range(bits) if (first >> bit) & 1]
+    for bit in live:
+        slots[bit] = slots_in[bit]
+        narrow[bit * state : (bit + 1) * state, :] = slots_in[bit].astype(BF16)
+
+    def head_part(c):
+        at = slice(c * BLOCK, (c + 1) * BLOCK)
+        live = [bit for bit in range(bits) if (c >> bit) & 1]
+        if live:
+            queries[0 : len(live) * state, :] = read_levels(read_t, weight_h, at, [bit + 1 for bit in live])
+        weighted = dot(read_t[:, at], write_t[:, at], TN) * columns[at, padded : padded + 1]
+        off_scores[...] = weighted[HALF:, :HALF].astype(BF16)
         scores[0] = jnp.where(causal, weighted[:HALF, :HALF], 0.0)
         scores[1] = jnp.where(causal, weighted[HALF:, HALF:], 0.0)
-        lane = iota((HALF, LANES), 1)
-        own = [as_bf16((lane >= k * per_head) & (lane < (k + 1) * per_head)) for k in range(heads_here)]
-        middle = rows[pl.ds(layout.middle + c, 1), :]
-        for half in range(2):
-            half_at = pl.ds(pl.multiple_of(c * BLOCK + half * HALF, HALF), HALF)
-            put_at = pl.ds(pl.multiple_of(g * BLOCK + half * HALF, HALF), HALF)
-            first_at = pl.ds(pl.multiple_of(c * BLOCK, HALF), HALF)
-            row_at = slice(half * HALF, (half + 1) * HALF)
-            run = rows[pl.ds(layout.run + 2 * c + half, 1), :]
-            for left in range(0, width, tile):
-                lanes = slice(left, left + tile)
-                near = dot(factors[half_at, :], wide[:, lanes])
-                reach[put_at, lanes] = near * run[:, lanes]
-                if half == 0:
-                    rest = near * inter[row_at, lanes]
-                else:
-                    off = dot(off_scores, scaled[first_at, lanes])
-                    rest = near * (off + middle[:, lanes] * inter[row_at, lanes])
-                for inner in range(left, left + tile, LANES):
-                    here = slice(inner, inner + LANES)
-                    head = inner // per_head
-                    value = mixer[half_at, here]
-                    left_side = []
-                    for k in range(heads_here):
-                        gap = columns[half_at, head + k : head + k + 1] - cum_h[head + k : head + k + 1, half_at]
-                        mixing = scores[half] * jnp.exp2(jnp.minimum(gap, 0.0))
-                        left_side.append(mixing.astype(BF16))
-                    part = dot(
-                        jnp.concatenate(left_side, 1),
-                        jnp.concatenate([value * mask for mask in own], 0),
-                    )
-                    base[put_at, here] = (
-                        part + rest[:, inner - left : inner - left + LANES]
-                        + skip[:, here] * value.astype(F32)
-                    )
-
-        upper = rows[pl.ds(layout.upper + c, 1), :]
-        start = pl.multiple_of(c * BLOCK, HALF)
-        fresh[...] = upper * dot(
-            write_t[:, pl.ds(start, HALF)], scaled[pl.ds(start, HALF), :]
-        ) + dot(write_t[:, pl.ds(start + HALF, HALF)], scaled[pl.ds(start + HALF, HALF), :])
-        shrink = rows[pl.ds(layout.decay + c, 1), :]
-        for bit in range(bits):
-            below = (1 << bit) - 1
-
-            @pl.when(((c >> bit) & 1 == 1) & (c & below == below))
-            def _(bit=bit):
-                fresh[...] += shrink * slots[bit]
-
-            @pl.when(((c >> bit) & 1 == 1) & (c & below != below))
-            def _(bit=bit):
-                slots[bit] = shrink * slots[bit]
-
-            @pl.when(((c >> bit) & 1 == 0) & (c & below == below))
-            def _(bit=bit):
-                slots[bit] = fresh[...]
-
-        return carry
-
-    lax.fori_loop(0, count, block, 0)
+
+    def half_part(c, half):
+        live = [bit for bit in range(bits) if (c >> bit) & 1]
+        low = c * BLOCK + half * HALF
+        half_at = slice(low, low + HALF)
+        put_at = slice(low - first * BLOCK, low - first * BLOCK + HALF)
+        for left in range(0, width, tile):
+            lanes = slice(left, left + tile)
+            near = dot(factors[half_at, :], wide[:, lanes])
+            reach[put_at, lanes] = near * rows[layout.run + 2 * c + half : layout.run + 2 * c + half + 1, lanes]
+            rest = None
+            if half == 1:
+                rest = dot(off_scores[...], scaled[c * BLOCK : c * BLOCK + HALF, lanes])
+            if live:
+                stored = [narrow[bit * state : (bit + 1) * state, lanes] for bit in live]
+                stored = jnp.concatenate(stored, 0) if len(stored) > 1 else stored[0]
+                level = dot(
+                    queries[0 : len(live) * state, half * HALF : (half + 1) * HALF], stored, TN
+                )
+                middle = rows[layout.middle + c : layout.middle + c + 1, lanes]
+                rest = level if rest is None else rest + middle * level
+            skipped = rows[layout.skip : layout.skip + 1, lanes] * mixer[half_at, lanes].astype(F32)
+            rest = skipped if rest is None else skipped + near * rest
+            for inner in range(0, tile, LANES):
+                here = slice(left + inner, left + inner + LANES)
+                head = (left + inner) // per_head
+                value = mixer[half_at, here]
+                left_side = []
+                for k in range(heads_here):
+                    gap = columns[half_at, head + k : head + k + 1] - cum_h[head + k : head + k + 1, half_at]
+                    mixing = scores[half] * jnp.exp2(jnp.minimum(gap, 0.0))
+                    left_side.append(mixing.astype(BF16))
+                part = dot(
+                    jnp.concatenate(left_side, 1),
+                    jnp.concatenate([value * mask for mask in own], 0),
+                )
+                base[put_at, here] = part + rest[:, inner : inner + LANES]
+
+    def update_part(c):
+        live = [bit for bit in range(bits) if (c >> bit) & 1]
+        ones = 0
+        while ones < bits and (c >> ones) & 1:
+            ones += 1
+        low = c * BLOCK
+        if ones == bits:
+            return
+        for left in range(0, width, tile):
+            lanes = slice(left, left + tile)
+            shrink = rows[layout.decay + c : layout.decay + c + 1, lanes]
+            upper = rows[layout.upper + c : layout.upper + c + 1, lanes]
+            fresh = upper * dot(
+                write_t[:, low : low + HALF], scaled[low : low + HALF, lanes]
+            ) + dot(write_t[:, low + HALF : low + BLOCK], scaled[low + HALF : low + BLOCK, lanes])
+            for bit in range(ones):
+                fresh = fresh + shrink * slots[bit, :, lanes]
+            slots[ones, :, lanes] = fresh
+            narrow[ones * state : (ones + 1) * state, lanes] = fresh.astype(BF16)
+            for bit in live:
+                if bit > ones:
+                    kept = shrink * slots[bit, :, lanes]
+                    slots[bit, :, lanes] = kept
+                    narrow[bit * state : (bit + 1) * state, lanes] = kept.astype(BF16)
+
+    when_here = pl.when(lax.axis_index("seq") >= 0)
+    for c in range(first, first + count):
+        when_here(functools.partial(head_part, c))
+        when_here(functools.partial(half_part, c, 0))
+        when_here(functools.partial(half_part, c, 1))
+        when_here(functools.partial(update_part, c))
 
 
 def bucket_rows(received, bits, state, width, wanted):
@@ -325,10 +338,12 @@
 
 def middle_kernel(starts, local_bits, bits, read_t, weight_h, *rest):
     pieces = len(starts) - 1
-    received, rest = rest[:bits], rest[bits:]
+    received, rest = (rest[:bits], rest[bits : 2 * bits]), rest[2 * bits :]
     bases, reaches, rest = rest[:pieces], rest[pieces : 2 * pieces], rest[2 * pieces :]
     outs, buckets = rest[:pieces], rest[pieces]
-    buckets[...] = bucket_rows(received, bits, read_t.shape[0], buckets.shape[1], range(bits))
+    width = buckets.shape[1]
+    for parts, at in zip(received, own_columns(width)):
+        buckets[:, at] = bucket_rows(parts, bits, read_t.shape[0], width // 2, range(bits))
     for piece in range(pieces):
 
         def block(g, carry, piece=piece):
@@ -342,15 +357,16 @@
         lax.fori_loop(0, starts[piece + 1] - starts[piece], block, 0)
 
 
-def final_kernel(starts, local_bits, bits, read_t, weight_h, *rest):
+def final_kernel(starts, local_bits, bits, side, read_t, weight_h, *rest):
     pieces = len(starts) - 1
     received, rest = rest[:bits], rest[bits:]
     bases, reaches, rest = rest[:pieces], rest[pieces : 2 * pieces], rest[2 * pieces :]
-    out, buckets, ready, sems = rest
-    buckets[...] = bucket_rows(received, bits, read_t.shape[0], out.shape[1], [bits - 1])
+    out, buckets, ready, sems = rest[-4:]
+    columns = own_columns(out.shape[1])[side]
+    buckets[...] = bucket_rows(received, bits, read_t.shape[0], buckets.shape[1], [bits - 1])
 
     def copy(c, at):
-        return pltpu.make_async_copy(ready.at[c], out.at[pl.ds(at, BLOCK), :], sems.at[c])
+        return pltpu.make_async_copy(ready.at[c], out.at[pl.ds(at, BLOCK), columns], sems.at[c])
 
     for piece in range(pieces):
 
@@ -360,7 +376,7 @@
             here = pl.ds(pl.multiple_of(g * BLOCK, BLOCK), BLOCK)
             query = read_levels(read_t, weight_h, pl.ds(at, BLOCK), [local_bits + bits])
             part = dot(query, buckets[...], TN)
-            ready[c] = (bases[piece][here, :] + part * reaches[piece][here, :]).astype(BF16)
+            ready[c] = (bases[piece][here, columns] + part * reaches[piece][here, columns]).astype(BF16)
             copy(c, at).start()
             return carry
 
@@ -369,25 +385,23 @@
         copy(c, c * BLOCK).wait()
 
 
-def gather_columns(mine, axis, other):
-    pieces, _ = lax.optimization_barrier((mine, other)) if other is not None else (mine, None)
+def gather_columns(mine, axis, after):
+    pieces = mine
     size = lax.axis_size(axis)
     stride = size // 2
-    first = None
     while stride:
         other = lax.ppermute(pieces, axis, [(i, i ^ stride) for i in range(size)])
-        first = other if first is None else first
         pieces = pl.pallas_call(
             join_kernel,
-            in_specs=[VMEM_SPEC] * 2,
+            in_specs=[VMEM_SPEC] * 2 + [ANY_SPEC],
             out_specs=VMEM_SPEC,
             out_shape=jax.ShapeDtypeStruct((2 * pieces.shape[0], pieces.shape[1]), BF16),
             compiler_params=grant(2),
             cost_estimate=cost(0, 4 * pieces.size),
             name="join",
-        )(pieces, other)
+        )(pieces, other, after)
         stride //= 2
-    return pieces, first
+    return pieces
 
 
 def cost(flops, bytes_accessed):
@@ -403,7 +417,6 @@
 ):
     tokens, width = mixer_input.shape
     heads = log_decay.shape[0]
-    per_head = width // heads
     blocks = tokens // BLOCK
     local_bits = blocks.bit_length() - 1
     ranks = lax.axis_size("seq")
@@ -413,10 +426,6 @@
     tile = 256
     layout = Rows(blocks)
     sds = jax.ShapeDtypeStruct
-
-    write_t, arrived = gather_columns(write_map.T, "head", None)
-    read_t, _ = gather_columns(read_map.T, "head", arrived)
-    state = write_t.shape[0]
 
     factors, columns, cum_h, weight_h, rows = pl.pallas_call(
         functools.partial(prep_kernel, heads, padded, layout),
@@ -440,7 +449,16 @@
         compiler_params=grant(6),
         cost_estimate=cost(2_000_000_000, 4_000_000),
         name="prep",
-    )(log_decay, step_size, level_index, level_table, skip_gain[None, :])
+    )(
+        *(
+            pltpu.with_memory_space_constraint(value, pltpu.HBM)
+            for value in (log_decay, step_size, level_index, level_table, skip_gain[None, :])
+        )
+    )
+
+    write_t = gather_columns(write_map.T, "head", rows)
+    read_t = gather_columns(read_map.T, "head", rows)
+    state = write_t.shape[0]
 
     scaled, to_total = pl.pallas_call(
         functools.partial(scale_kernel, heads, padded, layout),
@@ -452,13 +470,14 @@
         name="scale",
     )(mixer_input, factors, rows)
 
-    payload_rows = state + 8
-    carried = (sds((state, width), F32), sds((8, width), F32), sds((payload_rows, width), BF16))
-    mine, mine_exp, payload = pl.pallas_call(
+    half = width // 2
+    carried = (sds((state + 8, half), BF16), sds((state, half), F32), sds((8, half), F32))
+    first_out, second_out, mine, mine_exp = pl.pallas_call(
         functools.partial(state_kernel, layout),
         in_specs=[VMEM_SPEC] * 3,
-        out_specs=(VMEM_SPEC,) * 3,
-        out_shape=carried,
+        out_specs=(VMEM_SPEC,) * 4,
+        out_shape=carried[:1] + carried,
+        scratch_shapes=[pltpu.VMEM((state, width), F32)],
         compiler_params=grant(4),
         cost_estimate=cost(2 * tokens * width * state, tokens * width * 2),
         name="state",
@@ -477,8 +496,9 @@
             ),
             scratch_shapes=[
                 pltpu.VMEM((2, HALF, HALF), F32),
-                pltpu.VMEM((BLOCK, width), F32),
-                pltpu.VMEM((state, width), F32),
+                pltpu.VMEM((local_bits * state, width), BF16),
+                pltpu.VMEM((HALF, HALF), BF16),
+                pltpu.VMEM((local_bits * state, BLOCK), BF16),
             ],
             compiler_params=grant(8),
             cost_estimate=cost(count * BLOCK * width * 2 * 2000, count * BLOCK * width * 8),
@@ -488,66 +508,87 @@
             slots, after,
         )
 
-    shares = [1] * (device_bits - 2) + [1, 2] if device_bits > 1 else [1]
+    def swap(value, bit):
+        return lax.ppermute(value, "seq", [(i, i ^ 1 << bit) for i in range(ranks)])
+
+    shares = [3] * (device_bits - 1) + [2]
     starts = [0]
-    for k, share in enumerate(shares):
-        starts.append(starts[-1] + blocks * share // sum(shares))
-    starts[-1] = blocks
-
-    slots = jnp.zeros((8, LANES), F32)
-    bases, reaches, received = [], [], []
+    for share in shares:
+        starts.append(starts[-1] + max(1, blocks * share // sum(shares)))
+    starts = [min(start, blocks) for start in starts[:-1]] + [blocks]
+
+    slots = jnp.zeros((local_bits, 8, LANES), F32)
+    bases, reaches = [], []
+    own_parts = [swap(first_out, 0)]
+    other_parts = [swap(second_out, 0)]
     after = rows
+    payload = None
     for bit in range(device_bits):
-        other = lax.ppermute(payload, "seq", [(i, i ^ 1 << bit) for i in range(ranks)])
-        if bit < len(starts) - 1 and starts[bit + 1] > starts[bit]:
+        if starts[bit + 1] > starts[bit]:
             base, reach, slots = local(starts[bit], starts[bit + 1] - starts[bit], slots, after)
             bases.append(base)
             reaches.append(reach)
-        received.append(other)
         if bit + 1 < device_bits:
             last = bit + 2 == device_bits
-            shapes = (carried[2],) if last else (carried[2],) + carried[:2]
+            shapes = carried[:1] if last else carried
             payload, *more = pl.pallas_call(
                 functools.partial(merge_kernel, bit),
                 in_specs=[VMEM_SPEC] * 3 + [ANY_SPEC],
                 out_specs=(VMEM_SPEC,) * len(shapes),
                 out_shape=shapes,
                 compiler_params=grant(4),
-                cost_estimate=cost(4 * state * width, state * width * 12),
+                cost_estimate=cost(2 * state * width, state * width * 6),
                 name="merge",
-            )(other, mine, mine_exp, slots)
+            )(own_parts[bit], mine, mine_exp, slots)
             if more:
                 mine, mine_exp = more
             after = payload
+            own_parts.append(swap(payload, bit + 1))
+            if bit > 0:
+                other_parts.append(swap(own_parts[bit], 0))
+    starts = sorted(set(starts))
+    count = len(bases)
 
     if device_bits > 1:
-        count = len(bases)
+        near_bits = device_bits - 1
         bases = pl.pallas_call(
-            functools.partial(middle_kernel, starts, local_bits, device_bits - 1),
-            in_specs=[VMEM_SPEC] * (2 + device_bits - 1 + 2 * count),
+            functools.partial(middle_kernel, starts, local_bits, near_bits),
+            in_specs=[VMEM_SPEC] * (2 + 2 * near_bits + 2 * count),
             out_specs=(VMEM_SPEC,) * count,
             out_shape=tuple(sds(base.shape, F32) for base in bases),
-            input_output_aliases={2 + device_bits - 1 + k: k for k in range(count)},
-            scratch_shapes=[pltpu.VMEM(((device_bits - 1) * state, width), BF16)],
+            input_output_aliases={2 + 2 * near_bits + k: k for k in range(count)},
+            scratch_shapes=[pltpu.VMEM((near_bits * state, width), BF16)],
             compiler_params=grant(4),
             cost_estimate=cost(2 * tokens * width * state * 2, tokens * width * 6),
             name="middle",
-        )(read_t, weight_h, *received[:-1], *bases, *reaches)
-
-    return pl.pallas_call(
-        functools.partial(final_kernel, starts, local_bits, device_bits),
-        in_specs=[VMEM_SPEC] * (2 + device_bits + 2 * len(bases)),
-        out_specs=ANY_SPEC,
-        out_shape=sds((tokens, width), BF16),
-        scratch_shapes=[
-            pltpu.VMEM((state, width), BF16),
-            pltpu.VMEM((blocks, BLOCK, width), BF16),
-            pltpu.SemaphoreType.DMA((blocks,)),
-        ],
-        compiler_params=grant(8),
-        cost_estimate=cost(2 * tokens * width * state * device_bits, tokens * width * 6),
-        name="final",
-    )(read_t, weight_h, *received, *bases, *reaches)
+        )(read_t, weight_h, *own_parts[:-1], *other_parts, *bases, *reaches)
+        other_parts.append(swap(own_parts[-1], 0))
+
+    out = None
+    for side, parts in enumerate((own_parts, other_parts)):
+        operands = [read_t, weight_h, *parts, *bases, *reaches]
+        specs = [VMEM_SPEC] * len(operands)
+        aliases = {}
+        if out is not None:
+            aliases = {len(operands): 0}
+            operands.append(out)
+            specs.append(ANY_SPEC)
+        out = pl.pallas_call(
+            functools.partial(final_kernel, starts, local_bits, device_bits, side),
+            in_specs=specs,
+            out_specs=ANY_SPEC,
+            out_shape=sds((tokens, width), BF16),
+            input_output_aliases=aliases,
+            scratch_shapes=[
+                pltpu.VMEM((state, half), BF16),
+                pltpu.VMEM((blocks, BLOCK, half), BF16),
+                pltpu.SemaphoreType.DMA((blocks,)),
+            ],
+            compiler_params=grant(6),
+            cost_estimate=cost(tokens * width * state, tokens * width * 3),
+            name="final",
+        )(*operands)
+    return out
 
 
 def solution(mesh):
@@ -561,6 +602,7 @@
         P(),
         P(None, "seq"),
     )
+
     return jax.shard_map(
         on_device, mesh=mesh, in_specs=placed, out_specs=P("seq", "head"), check_vma=False
     )

time: 62.5 us -> 54.9 us (0.88)
  Pallas kernels: 36 us -> 31.8 us
  local copies, waits for them, and re-layouts: 4.05 us -> 0.01 us
  starting transfers between devices: 11.2 us -> 13 us
  waiting for transfers between devices: 10.8 us -> 9.65 us
    pallas_call x3, Pallas kernels: 20.8 us -> 13.9 us  [local(): pl.pallas_call(functools.partial(local_kernel, heads, padded, local_bits,...]
    unnamed x16 -> x6, local copies, waits for them, and re-layouts: 4.04 us -> 0.01 us
    ppermute x3 -> x6, starting transfers between devices: 5.88 us -> 9.84 us  [swap(): return lax.ppermute(value, 'seq', [(i, i ^ 1 << bit) for i in range(ranks)])]
    ppermute x4, starting transfers between devices: 5.32 us -> 3.17 us  [gather_columns(): other = lax.ppermute(pieces, axis, [(i, i ^ stride) for i in range(size)])]
    pallas_call x1 -> x2, Pallas kernels: 4.11 us -> 6.26 us  [on_device(): pl.pallas_call(functools.partial(final_kernel, starts, local_bits, device...]
    ppermute x3 -> x6, waiting for transfers between devices: 7.1 us -> 6.29 us  [swap(): return lax.ppermute(value, 'seq', [(i, i ^ 1 << bit) for i in range(ranks)])]
  transfers between devices with their start and end apart: 7 -> 10, of which waited for: 3 -> 4; matrix products, arithmetic and copies ran while one was open for 0% -> 0% of each run, Pallas kernels for 51% -> 52%
where the time goes in v4:
time: 54.9 us; the launch traced here: 54.8 us
  Pallas kernels  31.8 us (58%)
  starting transfers between devices  13 us (24%)
  waiting for transfers between devices  9.65 us (18%)
    pallas_call x3, Pallas kernels, local(): pl.pallas_call(functools.partial(local_kernel, heads, padded, local_bits,...  13.9 us
    ppermute x6, starting transfers between devices, swap(): return lax.ppermute(value, 'seq', [(i, i ^ 1 << bit) for i in range(ranks)])  9.84 us
    ppermute x6, waiting for transfers between devices, swap(): return lax.ppermute(value, 'seq', [(i, i ^ 1 << bit) for i in range(ranks)])  6.29 us
    pallas_call x2, Pallas kernels, on_device(): pl.pallas_call(functools.partial(final_kernel, starts, local_bits, device...  6.26 us
    pallas_call x1, Pallas kernels, on_device(): pl.pallas_call(functools.partial(scale_kernel, heads, padded, layout), in...  3.7 us
    pallas_call x1, Pallas kernels, on_device(): pl.pallas_call(functools.partial(middle_kernel, starts, local_bits, near_...  3.62 us
    ppermute x4, waiting for transfers between devices, gather_columns(): other = lax.ppermute(pieces, axis, [(i, i ^ stride) for i in range(size)])  3.37 us
    ppermute x4, starting transfers between devices, gather_columns(): other = lax.ppermute(pieces, axis, [(i, i ^ stride) for i in range(size)])  3.17 us
  transfers between devices with their start and end apart: 10, of which 4 were waited for; matrix products, arithmetic and copies ran while one was open for 0% of the time, Pallas kernels for 52%

profile of v4, /device:TPU:0, one launch (start us, length us, event | category | flops | bytes accessed | tf_op | source)
XLA Modules:
  0.0 54.8 jit_solution(17093028696206138725)
XLA Ops:
  0.0 3.0 %collective-permute-start = (bf16[32,2048]{1,0:T(8,128)(2,1)}, bf16[32,2048]{1,0:T(8,128)(2,1)S(1)}, u32[]{:S(2)}, u32[]{:S(2)}) collective-permute-start(bf16[32,2048]{1,0:T(8,128)(2,1)} %bitcast.3), channel_id=1, source_target_pairs={{0,2},{1,3},{2,0},{3,1},{4,6},{5,7},{6,4},{7,5},{8,10},{9,11},{10,... | collective-permute-start | bytes 393224 | tf_op jit(solution)/shard_map/ppermute | solution.py:393
  3.0 0.1 collective-permute-start.2
  3.0 3.0 %prep.1 = (bf16[2048,128]{1,0:T(8,128)(2,1)S(1)}, f32[2048,128]{1,0:T(8,128)S(1)}, f32[32,2048]{1,0:T(8,128)S(1)}, f32[7,2048]{1,0:T(8,128)S(1)}, f32[80,1280]{1,0:T(8,128)S(1)}) custom-call(f32[20,2048]{1,0:T(8,128)} %log_decay_far.1, f32[20,2048]{1,0:T(8,128)} %step_size_far.1, s32[7,2048]{1,0:T(8,128)} %level_index_far.1, f32[7,8]{1,0:T(8,128)} %level_table_far.1, ...), custom_call_target="tpu_custom_call" | custom-call | flops 2000000000 | bytes 4000000 | tf_op jit(solution)/shard_map/prep/pallas_call | solution.py:430
  6.1 1.5 %collective-permute-done.second = bf16[32,2048]{1,0:T(8,128)(2,1)S(1)} collective-permute-done((bf16[32,2048]{1,0:T(8,128)(2,1)}, bf16[32,2048]{1,0:T(8,128)(2,1)S(1)}, u32[]{:S(2)}, u32[]{:S(2)}) %collective-permute-start) | collective-permute-done | bytes 131104 | tf_op jit(solution)/shard_map/ppermute | solution.py:393
  7.6 0.0 copy-done.1
  7.6 0.1 collective-permute-start.1
  7.7 1.9 %collective-permute-done.2.second = bf16[32,2048]{1,0:T(8,128)(2,1)S(1)} collective-permute-done((bf16[32,2048]{1,0:T(8,128)(2,1)}, bf16[32,2048]{1,0:T(8,128)(2,1)S(1)}, u32[]{:S(2)}, u32[]{:S(2)}) %collective-permute-start.2) | collective-permute-done | bytes 131104 | tf_op jit(solution)/shard_map/ppermute | solution.py:393
  9.6 0.1 collective-permute-start.3
  9.7 3.7 %scale.1 = (bf16[2048,1280]{1,0:T(8,128)(2,1)S(1)}, bf16[2048,1280]{1,0:T(8,128)(2,1)S(1)}) custom-call(bf16[2048,1280]{1,0:T(8,128)(2,1)S(1)} %copy-done, bf16[2048,128]{1,0:T(8,128)(2,1)S(1)} %get-tuple-element.32.factors, f32[80,1280]{1,0:T(8,128)S(1)} %get-tuple-element.30.rest_0_.rows.after), custom_call_target="tpu_custom_call" | custom-call | flops 3000000000 | bytes 15728640 | tf_op jit(solution)/shard_map/scale/pallas_call | solution.py:463
  13.4 0.0 collective-permute-done.3.second
  13.4 0.9 %state.1 = (bf16[136,640]{1,0:T(8,128)(2,1)S(1)}, bf16[136,640]{1,0:T(8,128)(2,1)S(1)}, f32[128,640]{1,0:T(8,128)S(1)}, f32[8,640]{1,0:T(8,128)S(1)}) custom-call(bf16[2048,1280]{1,0:T(8,128)(2,1)S(1)} %get-tuple-element.33.to_total, bf16[128,2048]{1,0:T(8,128)(2,1)S(1)} %join.7.write_t, f32[80,1280]{1,0:T(8,128)S(1)} %get-tuple-element.30.rest_0_.rows.after), custom_call_target="tpu_custom_call" | custom-call | flops 671088640 | bytes 5242880 | tf_op jit(solution)/shard_map/state/pallas_call | solution.py:475
  14.4 1.8 %collective-permute-start.5 = (bf16[136,640]{1,0:T(8,128)(2,1)S(1)}, bf16[136,640]{1,0:T(8,128)(2,1)S(1)}, u32[]{:S(2)}, u32[]{:S(2)}) collective-permute-start(bf16[136,640]{1,0:T(8,128)(2,1)S(1)} %get-tuple-element.35), channel_id=1, source_target_pairs={{0,4},{4,0},{8,12},{12,8},{16,20},{20,16},{24,28},{28,24},{1,5},{5... | collective-permute-start | bytes 522248 | tf_op jit(solution)/shard_map/ppermute | solution.py:512
  16.1 0.0 collective-permute-done.1.second
  16.2 4.3 %local.3 = (f32[768,1280]{1,0:T(8,128)S(1)}, f32[768,1280]{1,0:T(8,128)S(1)}, f32[3,128,1280]{2,1,0:T(8,128)S(1)}) custom-call(bf16[2048,1280]{1,0:T(8,128)(2,1)S(1)} %copy-done, bf16[2048,1280]{1,0:T(8,128)(2,1)S(1)} %get-tuple-element.38.scaled, bf16[128,2048]{1,0:T(8,128)(2,1)S(1)} %join.7.write_t, bf16[128,2048]{1,0:T(8,128)(2,1)S(1)} %join.5.read_t, ...), custom_call_target="tpu_custom_call" | custom-call | flops 3932160000 | bytes 7864320 | tf_op jit(solution)/shard_map/local/pallas_call | solution.py:487
  20.5 0.8 %collective-permute-done.5.received.rest_0_ = bf16[136,640]{1,0:T(8,128)(2,1)S(1)} collective-permute-done((bf16[136,640]{1,0:T(8,128)(2,1)S(1)}, bf16[136,640]{1,0:T(8,128)(2,1)S(1)}, u32[]{:S(2)}, u32[]{:S(2)}) %collective-permute-start.5) | collective-permute-done | bytes 174112 | tf_op jit(solution)/shard_map/ppermute | solution.py:512
  21.2 0.1 merge.2
  21.3 1.8 %collective-permute-start.6 = (bf16[136,640]{1,0:T(8,128)(2,1)S(1)}, bf16[136,640]{1,0:T(8,128)(2,1)S(1)}, u32[]{:S(2)}, u32[]{:S(2)}) collective-permute-start(bf16[136,640]{1,0:T(8,128)(2,1)S(1)} %get-tuple-element.42.after), channel_id=1, source_target_pairs={{0,8},{4,12},{8,0},{12,4},{16,24},{20,28},{24,16},{28,20},{1,9},{5... | collective-permute-start | bytes 522248 | tf_op jit(solution)/shard_map/ppermute | solution.py:512
  23.1 5.1 %local.4 = (f32[768,1280]{1,0:T(8,128)S(1)}, f32[768,1280]{1,0:T(8,128)S(1)}, f32[3,128,1280]{2,1,0:T(8,128)S(1)}) custom-call(bf16[2048,1280]{1,0:T(8,128)(2,1)S(1)} %copy-done, bf16[2048,1280]{1,0:T(8,128)(2,1)S(1)} %get-tuple-element.38.scaled, bf16[128,2048]{1,0:T(8,128)(2,1)S(1)} %join.7.write_t, bf16[128,2048]{1,0:T(8,128)(2,1)S(1)} %join.5.read_t, ...), custom_call_target="tpu_custom_call" | custom-call | flops 3932160000 | bytes 7864320 | tf_op jit(solution)/shard_map/local/pallas_call | solution.py:487
  28.3 0.0 collective-permute-done.6.received.rest_1_
  28.3 0.1 merge.3.after
  28.4 2.7 %collective-permute-start.8 = (bf16[136,640]{1,0:T(8,128)(2,1)S(1)}, bf16[136,640]{1,0:T(8,128)(2,1)S(1)}, u32[]{:S(2)}, u32[]{:S(2)}) collective-permute-start(bf16[136,640]{1,0:T(8,128)(2,1)S(1)} %merge.3.after), channel_id=1, source_target_pairs={{0,16},{4,20},{8,24},{12,28},{16,0},{20,4},{24,8},{28,12},{1,17},{... | collective-permute-start | bytes 522248 | tf_op jit(solution)/shard_map/ppermute | solution.py:512
  31.0 1.5 %collective-permute-start.4 = (bf16[136,640]{1,0:T(8,128)(2,1)S(1)}, bf16[136,640]{1,0:T(8,128)(2,1)S(1)}, u32[]{:S(2)}, u32[]{:S(2)}) collective-permute-start(bf16[136,640]{1,0:T(8,128)(2,1)S(1)} %get-tuple-element.34), channel_id=1, source_target_pairs={{0,4},{4,0},{8,12},{12,8},{16,20},{20,16},{24,28},{28,24},{1,5},{5... | collective-permute-start | bytes 522248 | tf_op jit(solution)/shard_map/ppermute | solution.py:512
  32.6 0.5 collective-permute-start.7
  33.1 5.5 %collective-permute-done.8.rest_2_ = bf16[136,640]{1,0:T(8,128)(2,1)S(1)} collective-permute-done((bf16[136,640]{1,0:T(8,128)(2,1)S(1)}, bf16[136,640]{1,0:T(8,128)(2,1)S(1)}, u32[]{:S(2)}, u32[]{:S(2)}) %collective-permute-start.8) | collective-permute-done | bytes 174112 | tf_op jit(solution)/shard_map/ppermute | solution.py:512
  38.6 1.6 %collective-permute-start.9 = (bf16[136,640]{1,0:T(8,128)(2,1)S(1)}, bf16[136,640]{1,0:T(8,128)(2,1)S(1)}, u32[]{:S(2)}, u32[]{:S(2)}) collective-permute-start(bf16[136,640]{1,0:T(8,128)(2,1)S(1)} %collective-permute-done.8.rest_2_), channel_id=1, source_target_pairs={{0,4},{4,0},{8,12},{12,8},{16,20},{20,16},{24,28},{28,24},{1,5},{5... | collective-permute-start | bytes 522248 | tf_op jit(solution)/shard_map/ppermute | solution.py:512
  40.2 4.5 %local.5 = (f32[512,1280]{1,0:T(8,128)S(1)}, f32[512,1280]{1,0:T(8,128)S(1)}, f32[3,128,1280]{2,1,0:T(8,128)}) custom-call(bf16[2048,1280]{1,0:T(8,128)(2,1)S(1)} %copy-done, bf16[2048,1280]{1,0:T(8,128)(2,1)S(1)} %get-tuple-element.38.scaled, bf16[128,2048]{1,0:T(8,128)(2,1)S(1)} %join.7.write_t, bf16[128,2048]{1,0:T(8,128)(2,1)S(1)} %join.5.read_t, ...), custom_call_target="tpu_custom_call" | custom-call | flops 2621440000 | bytes 5242880 | tf_op jit(solution)/shard_map/local/pallas_call | solution.py:487
  44.7 0.0 collective-permute-done.4.rest_2_.rest_0_
  44.7 0.0 collective-permute-done.7.rest_3_.rest_1_
  44.7 3.6 %middle.1 = (f32[768,1280]{1,0:T(8,128)S(1)}, f32[768,1280]{1,0:T(8,128)S(1)}, f32[512,1280]{1,0:T(8,128)S(1)}) custom-call(bf16[128,2048]{1,0:T(8,128)(2,1)S(1)} %join.5.read_t, f32[7,2048]{1,0:T(8,128)S(1)} %get-tuple-element.31.weight_h, ...), custom_call_target="tpu_custom_call", output_to_operand_aliasing={{0}: (6, {}), {1}: (7, {}), {2}: (8, {})} | custom-call | flops 1342177280 | bytes 15728640 | tf_op jit(solution)/shard_map/middle/pallas_call | solution.py:554
  48.3 3.1 %final.2.rest_9_ = bf16[2048,1280]{1,0:T(8,128)(2,1)} custom-call(bf16[128,2048]{1,0:T(8,128)(2,1)S(1)} %join.5.read_t, f32[7,2048]{1,0:T(8,128)S(1)} %get-tuple-element.31.weight_h, bf16[136,640]{1,0:T(8,128)(2,1)S(1)} %collective-permute-done.5.received.rest_0_, bf16[136,640]{1,0:T(8,128)(2,1)S(1)} %collective-permute-done.6.received.rest_1_, ...), custom_call_target="tpu_custom_call" | custom-call | flops 335544320 | bytes 7864320 | tf_op jit(solution)/shard_map/final/pallas_call | solution.py:576
  51.5 0.0 collective-permute-done.9.rest_2_
  51.5 3.1 %final.3 = bf16[2048,1280]{1,0:T(8,128)(2,1)} custom-call(bf16[128,2048]{1,0:T(8,128)(2,1)S(1)} %join.5.read_t, f32[7,2048]{1,0:T(8,128)S(1)} %get-tuple-element.31.weight_h, bf16[136,640]{1,0:T(8,128)(2,1)S(1)} %collective-permute-done.4.rest_2_.rest_0_, ...), custom_call_target="tpu_custom_call", output_to_operand_aliasing={{}: (11, {})} | custom-call | flops 335544320 | bytes 7864320 | tf_op jit(solution)/shard_map/final/pallas_call | solution.py:576
  (10 shorter events, 0.1 us)
Async XLA Ops:
  0.0 7.6 %copy-start.1 = (bf16[2048,32]{0,1:T(8,128)(2,1)S(1)}, bf16[2048,32]{0,1:T(8,128)(2,1)}, u32[]{:S(2)}) copy-start(bf16[2048,32]{0,1:T(8,128)(2,1)} %param.10) | copy-start | bytes 393220
  0.0 7.6 %collective-permute-start = (bf16[32,2048]{1,0:T(8,128)(2,1)}, bf16[32,2048]{1,0:T(8,128)(2,1)S(1)}, u32[]{:S(2)}, u32[]{:S(2)}) collective-permute-start(bf16[32,2048]{1,0:T(8,128)(2,1)} %bitcast.3), channel_id=1, source_target_pairs={{0,2},{1,3},{2,0},{3,1},{4,6},{5,7},{6,4},{7,5},{8,10},{9,11},{10,... | collective-permute-start | bytes 393224 | tf_op jit(solution)/shard_map/ppermute | solution.py:393
  3.0 6.6 %collective-permute-start.2 = (bf16[32,2048]{1,0:T(8,128)(2,1)}, bf16[32,2048]{1,0:T(8,128)(2,1)S(1)}, u32[]{:S(2)}, u32[]{:S(2)}) collective-permute-start(bf16[32,2048]{1,0:T(8,128)(2,1)} %bitcast.5), channel_id=1, source_target_pairs={{0,2},{1,3},{2,0},{3,1},{4,6},{5,7},{6,4},{7,5},{8,10},{9,11},{10,... | collective-permute-start | bytes 393224 | tf_op jit(solution)/shard_map/ppermute | solution.py:393
  3.0 6.5 %copy-start.2 = (bf16[2048,32]{0,1:T(8,128)(2,1)S(1)}, bf16[2048,32]{0,1:T(8,128)(2,1)}, u32[]{:S(2)}) copy-start(bf16[2048,32]{0,1:T(8,128)(2,1)} %param.9) | copy-start | bytes 393220
  3.0 6.6 %copy-start = (bf16[2048,1280]{1,0:T(8,128)(2,1)S(1)}, bf16[2048,1280]{1,0:T(8,128)(2,1)}, u32[]{:S(2)}) copy-start(bf16[2048,1280]{1,0:T(8,128)(2,1)} %mixer.7) | copy-start | bytes 15728644
  7.6 8.5 %collective-permute-start.1 = (bf16[64,2048]{1,0:T(8,128)(2,1)S(1)}, bf16[64,2048]{1,0:T(8,128)(2,1)S(1)}, u32[]{:S(2)}, u32[]{:S(2)}) collective-permute-start(bf16[64,2048]{1,0:T(8,128)(2,1)S(1)} %join.4.first), channel_id=1, source_target_pairs={{0,1},{1,0},{2,3},{3,2},{4,5},{5,4},{6,7},{7,6},{8,9},{9,8},{10,11... | collective-permute-start | bytes 786440 | tf_op jit(solution)/shard_map/ppermute | solution.py:393
  9.6 3.8 %collective-permute-start.3 = (bf16[64,2048]{1,0:T(8,128)(2,1)S(1)}, bf16[64,2048]{1,0:T(8,128)(2,1)S(1)}, u32[]{:S(2)}, u32[]{:S(2)}) collective-permute-start(bf16[64,2048]{1,0:T(8,128)(2,1)S(1)} %join.6.first), channel_id=1, source_target_pairs={{0,1},{1,0},{2,3},{3,2},{4,5},{5,4},{6,7},{7,6},{8,9},{9,8},{10,11... | collective-permute-start | bytes 786440 | tf_op jit(solution)/shard_map/ppermute | solution.py:393
  14.4 6.9 %collective-permute-start.5 = (bf16[136,640]{1,0:T(8,128)(2,1)S(1)}, bf16[136,640]{1,0:T(8,128)(2,1)S(1)}, u32[]{:S(2)}, u32[]{:S(2)}) collective-permute-start(bf16[136,640]{1,0:T(8,128)(2,1)S(1)} %get-tuple-element.35), channel_id=1, source_target_pairs={{0,4},{4,0},{8,12},{12,8},{16,20},{20,16},{24,28},{28,24},{1,5},{5... | collective-permute-start | bytes 522248 | tf_op jit(solution)/shard_map/ppermute | solution.py:512
  21.3 7.0 %collective-permute-start.6 = (bf16[136,640]{1,0:T(8,128)(2,1)S(1)}, bf16[136,640]{1,0:T(8,128)(2,1)S(1)}, u32[]{:S(2)}, u32[]{:S(2)}) collective-permute-start(bf16[136,640]{1,0:T(8,128)(2,1)S(1)} %get-tuple-element.42.after), channel_id=1, source_target_pairs={{0,8},{4,12},{8,0},{12,4},{16,24},{20,28},{24,16},{28,20},{1,9},{5... | collective-permute-start | bytes 522248 | tf_op jit(solution)/shard_map/ppermute | solution.py:512
  28.4 10.2 %collective-permute-start.8 = (bf16[136,640]{1,0:T(8,128)(2,1)S(1)}, bf16[136,640]{1,0:T(8,128)(2,1)S(1)}, u32[]{:S(2)}, u32[]{:S(2)}) collective-permute-start(bf16[136,640]{1,0:T(8,128)(2,1)S(1)} %merge.3.after), channel_id=1, source_target_pairs={{0,16},{4,20},{8,24},{12,28},{16,0},{20,4},{24,8},{28,12},{1,17},{... | collective-permute-start | bytes 522248 | tf_op jit(solution)/shard_map/ppermute | solution.py:512
  31.0 13.6 %collective-permute-start.4 = (bf16[136,640]{1,0:T(8,128)(2,1)S(1)}, bf16[136,640]{1,0:T(8,128)(2,1)S(1)}, u32[]{:S(2)}, u32[]{:S(2)}) collective-permute-start(bf16[136,640]{1,0:T(8,128)(2,1)S(1)} %get-tuple-element.34), channel_id=1, source_target_pairs={{0,4},{4,0},{8,12},{12,8},{16,20},{20,16},{24,28},{28,24},{1,5},{5... | collective-permute-start | bytes 522248 | tf_op jit(solution)/shard_map/ppermute | solution.py:512
  32.6 12.1 %collective-permute-start.7 = (bf16[136,640]{1,0:T(8,128)(2,1)S(1)}, bf16[136,640]{1,0:T(8,128)(2,1)S(1)}, u32[]{:S(2)}, u32[]{:S(2)}) collective-permute-start(bf16[136,640]{1,0:T(8,128)(2,1)S(1)} %collective-permute-done.6.received.rest_1_), channel_id=1, source_target_pairs={{0,4},{4,0},{8,12},{12,8},{16,20},{20,16},{24,28},{28,24},{1,5},{5... | collective-permute-start | bytes 522248 | tf_op jit(solution)/shard_map/ppermute | solution.py:512
  38.6 12.9 %collective-permute-start.9 = (bf16[136,640]{1,0:T(8,128)(2,1)S(1)}, bf16[136,640]{1,0:T(8,128)(2,1)S(1)}, u32[]{:S(2)}, u32[]{:S(2)}) collective-permute-start(bf16[136,640]{1,0:T(8,128)(2,1)S(1)} %collective-permute-done.8.rest_2_), channel_id=1, source_target_pairs={{0,4},{4,0},{8,12},{12,8},{16,20},{20,16},{24,28},{28,24},{1,5},{5... | collective-permute-start | bytes 522248 | tf_op jit(solution)/shard_map/ppermute | solution.py:512

commit v5 on v4

--- a/solution.py
+++ b/solution.py
@@ -160,7 +160,7 @@
         to_total[at, :] = (value * row).astype(BF16)
         return carry
 
-    lax.fori_loop(0, tokens // HALF, step, 0)
+    lax.fori_loop(0, tokens // HALF, step, 0, unroll=4)
 
 
 def exp_rows(total, count):
@@ -308,53 +308,37 @@
                     slots[bit, :, lanes] = kept
                     narrow[bit * state : (bit + 1) * state, lanes] = kept.astype(BF16)
 
+    def first_region(c):
+        head_part(c)
+        half_part(c, 0)
+
+    def second_region(c):
+        half_part(c, 1)
+        update_part(c)
+
     when_here = pl.when(lax.axis_index("seq") >= 0)
     for c in range(first, first + count):
-        when_here(functools.partial(head_part, c))
-        when_here(functools.partial(half_part, c, 0))
-        when_here(functools.partial(half_part, c, 1))
-        when_here(functools.partial(update_part, c))
-
-
-def bucket_rows(received, bits, state, width, wanted):
+        when_here(functools.partial(first_region, c))
+        when_here(functools.partial(second_region, c))
+
+
+def bucket_rows(received, bits, state, width):
     running = jnp.ones((1, width), F32)
     out = []
     for bit in range(bits):
         upper = upper_half(bit, width)
-        if bit in wanted:
-            scale = jnp.where(upper, running, 0.0)
-            out.append((received[bit][0:state, :].astype(F32) * scale).astype(BF16))
+        scale = jnp.where(upper, running, 0.0)
+        out.append((received[bit][0:state, :].astype(F32) * scale).astype(BF16))
         if bit + 1 < bits:
             extra = received[bit][state:, :].astype(F32)
             running = jnp.where(upper, running * (extra[0:1] + extra[1:2]), running)
-    return jnp.concatenate(out, 0) if len(out) > 1 else out[0]
+    return jnp.concatenate(out, 0)
 
 
 def read_levels(read_t, weight_h, at, levels):
     read_f = read_t[:, at].astype(F32)
     queries = [(read_f * weight_h[level : level + 1, at]).astype(BF16) for level in levels]
     return jnp.concatenate(queries, 0) if len(queries) > 1 else queries[0]
-
-
-def middle_kernel(starts, local_bits, bits, read_t, weight_h, *rest):
-    pieces = len(starts) - 1
-    received, rest = (rest[:bits], rest[bits : 2 * bits]), rest[2 * bits :]
-    bases, reaches, rest = rest[:pieces], rest[pieces : 2 * pieces], rest[2 * pieces :]
-    outs, buckets = rest[:pieces], rest[pieces]
-    width = buckets.shape[1]
-    for parts, at in zip(received, own_columns(width)):
-        buckets[:, at] = bucket_rows(parts, bits, read_t.shape[0], width // 2, range(bits))
-    for piece in range(pieces):
-
-        def block(g, carry, piece=piece):
-            at = pl.ds(pl.multiple_of((starts[piece] + g) * BLOCK, BLOCK), BLOCK)
-            here = pl.ds(pl.multiple_of(g * BLOCK, BLOCK), BLOCK)
-            levels = [local_bits + 1 + bit for bit in range(bits)]
-            part = dot(read_levels(read_t, weight_h, at, levels), buckets[...], TN)
-            outs[piece][here, :] = bases[piece][here, :] + part * reaches[piece][here, :]
-            return carry
-
-        lax.fori_loop(0, starts[piece + 1] - starts[piece], block, 0)
 
 
 def final_kernel(starts, local_bits, bits, side, read_t, weight_h, *rest):
@@ -363,7 +347,9 @@
     bases, reaches, rest = rest[:pieces], rest[pieces : 2 * pieces], rest[2 * pieces :]
     out, buckets, ready, sems = rest[-4:]
     columns = own_columns(out.shape[1])[side]
-    buckets[...] = bucket_rows(received, bits, read_t.shape[0], buckets.shape[1], [bits - 1])
+    buckets[...] = bucket_rows(received, bits, read_t.shape[0], buckets.shape[1])
+
+    levels = [local_bits + 1 + bit for bit in range(bits)]
 
     def copy(c, at):
         return pltpu.make_async_copy(ready.at[c], out.at[pl.ds(at, BLOCK), columns], sems.at[c])
@@ -374,13 +360,13 @@
             c = starts[piece] + g
             at = pl.multiple_of(c * BLOCK, BLOCK)
             here = pl.ds(pl.multiple_of(g * BLOCK, BLOCK), BLOCK)
-            query = read_levels(read_t, weight_h, pl.ds(at, BLOCK), [local_bits + bits])
+            query = read_levels(read_t, weight_h, pl.ds(at, BLOCK), levels)
             part = dot(query, buckets[...], TN)
             ready[c] = (bases[piece][here, columns] + part * reaches[piece][here, columns]).astype(BF16)
             copy(c, at).start()
             return carry
 
-        lax.fori_loop(0, starts[piece + 1] - starts[piece], block, 0)
+        lax.fori_loop(0, starts[piece + 1] - starts[piece], block, 0, unroll=True)
     for c in range(starts[-1]):
         copy(c, c * BLOCK).wait()
 
@@ -547,21 +533,8 @@
             if bit > 0:
                 other_parts.append(swap(own_parts[bit], 0))
     starts = sorted(set(starts))
-    count = len(bases)
 
     if device_bits > 1:
-        near_bits = device_bits - 1
-        bases = pl.pallas_call(
-            functools.partial(middle_kernel, starts, local_bits, near_bits),
-            in_specs=[VMEM_SPEC] * (2 + 2 * near_bits + 2 * count),
-            out_specs=(VMEM_SPEC,) * count,
-            out_shape=tuple(sds(base.shape, F32) for base in bases),
-            input_output_aliases={2 + 2 * near_bits + k: k for k in range(count)},
-            scratch_shapes=[pltpu.VMEM((near_bits * state, width), BF16)],
-            compiler_params=grant(4),
-            cost_estimate=cost(2 * tokens * width * state * 2, tokens * width * 6),
-            name="middle",
-        )(read_t, weight_h, *own_parts[:-1], *other_parts, *bases, *reaches)
         other_parts.append(swap(own_parts[-1], 0))
 
     out = None
@@ -580,7 +553,7 @@
             out_shape=sds((tokens, width), BF16),
             input_output_aliases=aliases,
             scratch_shapes=[
-                pltpu.VMEM((state, half), BF16),
+                pltpu.VMEM((device_bits * state, half), BF16),
                 pltpu.VMEM((blocks, BLOCK, half), BF16),
                 pltpu.SemaphoreType.DMA((blocks,)),
             ],

time: 54.9 us -> 48.8 us (0.89)
  Pallas kernels: 31.8 us -> 25.7 us
    pallas_call x1 -> x0, Pallas kernels: 3.62 us -> none  [on_device(): pl.pallas_call(functools.partial(middle_kernel, starts, local_bits, near_...]
    pallas_call x1, Pallas kernels: 3.7 us -> 2.22 us  [on_device(): pl.pallas_call(functools.partial(scale_kernel, heads, padded, layout), in...]
    pallas_call x2, Pallas kernels: 6.26 us -> 5.19 us  [on_device(): pl.pallas_call(functools.partial(final_kernel, starts, local_bits, device...]
  transfers between devices with their start and end apart: 10 -> 10, of which waited for: 4 -> 4; matrix products, arithmetic and copies ran while one was open for 0% -> 0% of each run, Pallas kernels for 52% -> 47%
where the time goes in v5:
time: 48.8 us; the launch traced here: 48.7 us
  Pallas kernels  25.7 us (53%)
  starting transfers between devices  13 us (27%)
  waiting for transfers between devices  9.65 us (20%)
    pallas_call x3, Pallas kernels, local(): pl.pallas_call(functools.partial(local_kernel, heads, padded, local_bits,...  14 us
    ppermute x6, starting transfers between devices, swap(): return lax.ppermute(value, 'seq', [(i, i ^ 1 << bit) for i in range(ranks)])  9.83 us
    ppermute x6, waiting for transfers between devices, swap(): return lax.ppermute(value, 'seq', [(i, i ^ 1 << bit) for i in range(ranks)])  6.28 us
    pallas_call x2, Pallas kernels, on_device(): pl.pallas_call(functools.partial(final_kernel, starts, local_bits, device...  5.19 us
    ppermute x4, waiting for transfers between devices, gather_columns(): other = lax.ppermute(pieces, axis, [(i, i ^ stride) for i in range(size)])  3.37 us
    ppermute x4, starting transfers between devices, gather_columns(): other = lax.ppermute(pieces, axis, [(i, i ^ stride) for i in range(size)])  3.17 us
    pallas_call x1, Pallas kernels, on_device(): pl.pallas_call(functools.partial(prep_kernel, heads, padded, layout), in_...  3.04 us
    pallas_call x1, Pallas kernels, on_device(): pl.pallas_call(functools.partial(scale_kernel, heads, padded, layout), in...  2.22 us
  transfers between devices with their start and end apart: 10, of which 4 were waited for; matrix products, arithmetic and copies ran while one was open for 0% of the time, Pallas kernels for 47%

profile of v5, /device:TPU:0, one launch (start us, length us, event | category | flops | bytes accessed | tf_op | source)
XLA Modules:
  0.0 48.7 jit_solution(24211811089984146)
XLA Ops:
  0.0 3.0 %collective-permute-start = (bf16[32,2048]{1,0:T(8,128)(2,1)}, bf16[32,2048]{1,0:T(8,128)(2,1)S(1)}, u32[]{:S(2)}, u32[]{:S(2)}) collective-permute-start(bf16[32,2048]{1,0:T(8,128)(2,1)} %bitcast.3), channel_id=1, source_target_pairs={{0,2},{1,3},{2,0},{3,1},{4,6},{5,7},{6,4},{7,5},{8,10},{9,11},{10,... | collective-permute-start | bytes 393224 | tf_op jit(solution)/shard_map/ppermute | solution.py:379
  3.0 0.1 collective-permute-start.2
  3.0 3.0 %prep.1 = (bf16[2048,128]{1,0:T(8,128)(2,1)S(1)}, f32[2048,128]{1,0:T(8,128)S(1)}, f32[32,2048]{1,0:T(8,128)S(1)}, f32[7,2048]{1,0:T(8,128)S(1)}, f32[80,1280]{1,0:T(8,128)S(1)}) custom-call(f32[20,2048]{1,0:T(8,128)} %log_decay_far.1, f32[20,2048]{1,0:T(8,128)} %step_size_far.1, s32[7,2048]{1,0:T(8,128)} %level_index_far.1, f32[7,8]{1,0:T(8,128)} %level_table_far.1, ...), custom_call_target="tpu_custom_call" | custom-call | flops 2000000000 | bytes 4000000 | tf_op jit(solution)/shard_map/prep/pallas_call | solution.py:416
  6.1 1.5 %collective-permute-done.second = bf16[32,2048]{1,0:T(8,128)(2,1)S(1)} collective-permute-done((bf16[32,2048]{1,0:T(8,128)(2,1)}, bf16[32,2048]{1,0:T(8,128)(2,1)S(1)}, u32[]{:S(2)}, u32[]{:S(2)}) %collective-permute-start) | collective-permute-done | bytes 131104 | tf_op jit(solution)/shard_map/ppermute | solution.py:379
  7.6 0.0 copy-done.1
  7.6 0.1 collective-permute-start.1
  7.7 1.9 %collective-permute-done.2.second = bf16[32,2048]{1,0:T(8,128)(2,1)S(1)} collective-permute-done((bf16[32,2048]{1,0:T(8,128)(2,1)}, bf16[32,2048]{1,0:T(8,128)(2,1)S(1)}, u32[]{:S(2)}, u32[]{:S(2)}) %collective-permute-start.2) | collective-permute-done | bytes 131104 | tf_op jit(solution)/shard_map/ppermute | solution.py:379
  9.6 0.0 copy-done.2
  9.6 0.1 collective-permute-start.3
  9.7 2.2 %scale.1 = (bf16[2048,1280]{1,0:T(8,128)(2,1)S(1)}, bf16[2048,1280]{1,0:T(8,128)(2,1)S(1)}) custom-call(bf16[2048,1280]{1,0:T(8,128)(2,1)S(1)} %copy-done, bf16[2048,128]{1,0:T(8,128)(2,1)S(1)} %get-tuple-element.29.factors, f32[80,1280]{1,0:T(8,128)S(1)} %get-tuple-element.27.rest_0_.rows.after), custom_call_target="tpu_custom_call" | custom-call | flops 3000000000 | bytes 15728640 | tf_op jit(solution)/shard_map/scale/pallas_call | solution.py:449
  11.9 0.0 collective-permute-done.3.second
  12.0 1.0 %state.1 = (bf16[136,640]{1,0:T(8,128)(2,1)S(1)}, bf16[136,640]{1,0:T(8,128)(2,1)S(1)}, f32[128,640]{1,0:T(8,128)S(1)}, f32[8,640]{1,0:T(8,128)S(1)}) custom-call(bf16[2048,1280]{1,0:T(8,128)(2,1)S(1)} %get-tuple-element.30.to_total, bf16[128,2048]{1,0:T(8,128)(2,1)S(1)} %join.7.write_t, f32[80,1280]{1,0:T(8,128)S(1)} %get-tuple-element.27.rest_0_.rows.after), custom_call_target="tpu_custom_call" | custom-call | flops 671088640 | bytes 5242880 | tf_op jit(solution)/shard_map/state/pallas_call | solution.py:461
  12.9 1.8 %collective-permute-start.5 = (bf16[136,640]{1,0:T(8,128)(2,1)S(1)}, bf16[136,640]{1,0:T(8,128)(2,1)S(1)}, u32[]{:S(2)}, u32[]{:S(2)}) collective-permute-start(bf16[136,640]{1,0:T(8,128)(2,1)S(1)} %get-tuple-element.32), channel_id=1, source_target_pairs={{0,4},{4,0},{8,12},{12,8},{16,20},{20,16},{24,28},{28,24},{1,5},{5... | collective-permute-start | bytes 522248 | tf_op jit(solution)/shard_map/ppermute | solution.py:498
  14.7 0.0 collective-permute-done.1.second
  14.7 4.3 %local.3 = (f32[768,1280]{1,0:T(8,128)S(1)}, f32[768,1280]{1,0:T(8,128)S(1)}, f32[3,128,1280]{2,1,0:T(8,128)S(1)}) custom-call(bf16[2048,1280]{1,0:T(8,128)(2,1)S(1)} %copy-done, bf16[2048,1280]{1,0:T(8,128)(2,1)S(1)} %get-tuple-element.35.scaled, bf16[128,2048]{1,0:T(8,128)(2,1)S(1)} %join.7.write_t, bf16[128,2048]{1,0:T(8,128)(2,1)S(1)} %join.5.read_t, ...), custom_call_target="tpu_custom_call" | custom-call | flops 3932160000 | bytes 7864320 | tf_op jit(solution)/shard_map/local/pallas_call | solution.py:473
  19.1 0.7 %collective-permute-done.5.received.rest_0_ = bf16[136,640]{1,0:T(8,128)(2,1)S(1)} collective-permute-done((bf16[136,640]{1,0:T(8,128)(2,1)S(1)}, bf16[136,640]{1,0:T(8,128)(2,1)S(1)}, u32[]{:S(2)}, u32[]{:S(2)}) %collective-permute-start.5) | collective-permute-done | bytes 174112 | tf_op jit(solution)/shard_map/ppermute | solution.py:498
  19.8 0.1 merge.2
  19.9 1.8 %collective-permute-start.6 = (bf16[136,640]{1,0:T(8,128)(2,1)S(1)}, bf16[136,640]{1,0:T(8,128)(2,1)S(1)}, u32[]{:S(2)}, u32[]{:S(2)}) collective-permute-start(bf16[136,640]{1,0:T(8,128)(2,1)S(1)} %get-tuple-element.39.after), channel_id=1, source_target_pairs={{0,8},{4,12},{8,0},{12,4},{16,24},{20,28},{24,16},{28,20},{1,9},{5... | collective-permute-start | bytes 522248 | tf_op jit(solution)/shard_map/ppermute | solution.py:498
  21.7 5.2 %local.4 = (f32[768,1280]{1,0:T(8,128)S(1)}, f32[768,1280]{1,0:T(8,128)S(1)}, f32[3,128,1280]{2,1,0:T(8,128)S(1)}) custom-call(bf16[2048,1280]{1,0:T(8,128)(2,1)S(1)} %copy-done, bf16[2048,1280]{1,0:T(8,128)(2,1)S(1)} %get-tuple-element.35.scaled, bf16[128,2048]{1,0:T(8,128)(2,1)S(1)} %join.7.write_t, bf16[128,2048]{1,0:T(8,128)(2,1)S(1)} %join.5.read_t, ...), custom_call_target="tpu_custom_call" | custom-call | flops 3932160000 | bytes 7864320 | tf_op jit(solution)/shard_map/local/pallas_call | solution.py:473
  26.9 0.0 collective-permute-done.6.received.rest_1_
  26.9 0.1 merge.3.after
  27.0 2.7 %collective-permute-start.8 = (bf16[136,640]{1,0:T(8,128)(2,1)S(1)}, bf16[136,640]{1,0:T(8,128)(2,1)S(1)}, u32[]{:S(2)}, u32[]{:S(2)}) collective-permute-start(bf16[136,640]{1,0:T(8,128)(2,1)S(1)} %merge.3.after), channel_id=1, source_target_pairs={{0,16},{4,20},{8,24},{12,28},{16,0},{20,4},{24,8},{28,12},{1,17},{... | collective-permute-start | bytes 522248 | tf_op jit(solution)/shard_map/ppermute | solution.py:498
  29.7 1.5 %collective-permute-start.4 = (bf16[136,640]{1,0:T(8,128)(2,1)S(1)}, bf16[136,640]{1,0:T(8,128)(2,1)S(1)}, u32[]{:S(2)}, u32[]{:S(2)}) collective-permute-start(bf16[136,640]{1,0:T(8,128)(2,1)S(1)} %get-tuple-element.31), channel_id=1, source_target_pairs={{0,4},{4,0},{8,12},{12,8},{16,20},{20,16},{24,28},{28,24},{1,5},{5... | collective-permute-start | bytes 522248 | tf_op jit(solution)/shard_map/ppermute | solution.py:498
  31.2 0.5 %collective-permute-start.7 = (bf16[136,640]{1,0:T(8,128)(2,1)S(1)}, bf16[136,640]{1,0:T(8,128)(2,1)S(1)}, u32[]{:S(2)}, u32[]{:S(2)}) collective-permute-start(bf16[136,640]{1,0:T(8,128)(2,1)S(1)} %collective-permute-done.6.received.rest_1_), channel_id=1, source_target_pairs={{0,4},{4,0},{8,12},{12,8},{16,20},{20,16},{24,28},{28,24},{1,5},{5... | collective-permute-start | bytes 522248 | tf_op jit(solution)/shard_map/ppermute | solution.py:498
  31.7 5.5 %collective-permute-done.8.rest_2_ = bf16[136,640]{1,0:T(8,128)(2,1)S(1)} collective-permute-done((bf16[136,640]{1,0:T(8,128)(2,1)S(1)}, bf16[136,640]{1,0:T(8,128)(2,1)S(1)}, u32[]{:S(2)}, u32[]{:S(2)}) %collective-permute-start.8) | collective-permute-done | bytes 174112 | tf_op jit(solution)/shard_map/ppermute | solution.py:498
  37.2 1.6 %collective-permute-start.9 = (bf16[136,640]{1,0:T(8,128)(2,1)S(1)}, bf16[136,640]{1,0:T(8,128)(2,1)S(1)}, u32[]{:S(2)}, u32[]{:S(2)}) collective-permute-start(bf16[136,640]{1,0:T(8,128)(2,1)S(1)} %collective-permute-done.8.rest_2_), channel_id=1, source_target_pairs={{0,4},{4,0},{8,12},{12,8},{16,20},{20,16},{24,28},{28,24},{1,5},{5... | collective-permute-start | bytes 522248 | tf_op jit(solution)/shard_map/ppermute | solution.py:498
  38.8 4.5 %local.5 = (f32[512,1280]{1,0:T(8,128)S(1)}, f32[512,1280]{1,0:T(8,128)S(1)}, f32[3,128,1280]{2,1,0:T(8,128)}) custom-call(bf16[2048,1280]{1,0:T(8,128)(2,1)S(1)} %copy-done, bf16[2048,1280]{1,0:T(8,128)(2,1)S(1)} %get-tuple-element.35.scaled, bf16[128,2048]{1,0:T(8,128)(2,1)S(1)} %join.7.write_t, bf16[128,2048]{1,0:T(8,128)(2,1)S(1)} %join.5.read_t, ...), custom_call_target="tpu_custom_call" | custom-call | flops 2621440000 | bytes 5242880 | tf_op jit(solution)/shard_map/local/pallas_call | solution.py:473
  43.3 2.6 %final.2.rest_9_ = bf16[2048,1280]{1,0:T(8,128)(2,1)} custom-call(bf16[128,2048]{1,0:T(8,128)(2,1)S(1)} %join.5.read_t, f32[7,2048]{1,0:T(8,128)S(1)} %get-tuple-element.28.weight_h, bf16[136,640]{1,0:T(8,128)(2,1)S(1)} %collective-permute-done.5.received.rest_0_, bf16[136,640]{1,0:T(8,128)(2,1)S(1)} %collective-permute-done.6.received.rest_1_, ...), custom_call_target="tpu_custom_call" | custom-call | flops 335544320 | bytes 7864320 | tf_op jit(solution)/shard_map/final/pallas_call | solution.py:549
  45.9 0.0 collective-permute-done.4.rest_0_
  45.9 0.0 collective-permute-done.7.rest_1_
  46.0 0.0 collective-permute-done.9.rest_2_
  46.0 2.6 %final.3 = bf16[2048,1280]{1,0:T(8,128)(2,1)} custom-call(bf16[128,2048]{1,0:T(8,128)(2,1)S(1)} %join.5.read_t, f32[7,2048]{1,0:T(8,128)S(1)} %get-tuple-element.28.weight_h, bf16[136,640]{1,0:T(8,128)(2,1)S(1)} %collective-permute-done.4.rest_0_, bf16[136,640]{1,0:T(8,128)(2,1)S(1)} %collective-permute-done.7.rest_1_, ...), custom_call_target="tpu_custom_call", output_to_operand_aliasing={{}: (11, {})} | custom-call | flops 335544320 | bytes 7864320 | tf_op jit(solution)/shard_map/final/pallas_call | solution.py:549
  (9 shorter events, 0.1 us)
Async XLA Ops:
  0.0 7.6 %copy-start.1 = (bf16[2048,32]{0,1:T(8,128)(2,1)S(1)}, bf16[2048,32]{0,1:T(8,128)(2,1)}, u32[]{:S(2)}) copy-start(bf16[2048,32]{0,1:T(8,128)(2,1)} %param.10) | copy-start | bytes 393220
  0.0 7.6 %collective-permute-start = (bf16[32,2048]{1,0:T(8,128)(2,1)}, bf16[32,2048]{1,0:T(8,128)(2,1)S(1)}, u32[]{:S(2)}, u32[]{:S(2)}) collective-permute-start(bf16[32,2048]{1,0:T(8,128)(2,1)} %bitcast.3), channel_id=1, source_target_pairs={{0,2},{1,3},{2,0},{3,1},{4,6},{5,7},{6,4},{7,5},{8,10},{9,11},{10,... | collective-permute-start | bytes 393224 | tf_op jit(solution)/shard_map/ppermute | solution.py:379
  3.0 6.6 %collective-permute-start.2 = (bf16[32,2048]{1,0:T(8,128)(2,1)}, bf16[32,2048]{1,0:T(8,128)(2,1)S(1)}, u32[]{:S(2)}, u32[]{:S(2)}) collective-permute-start(bf16[32,2048]{1,0:T(8,128)(2,1)} %bitcast.5), channel_id=1, source_target_pairs={{0,2},{1,3},{2,0},{3,1},{4,6},{5,7},{6,4},{7,5},{8,10},{9,11},{10,... | collective-permute-start | bytes 393224 | tf_op jit(solution)/shard_map/ppermute | solution.py:379
  3.0 6.5 %copy-start.2 = (bf16[2048,32]{0,1:T(8,128)(2,1)S(1)}, bf16[2048,32]{0,1:T(8,128)(2,1)}, u32[]{:S(2)}) copy-start(bf16[2048,32]{0,1:T(8,128)(2,1)} %param.9) | copy-start | bytes 393220
  3.0 6.6 %copy-start = (bf16[2048,1280]{1,0:T(8,128)(2,1)S(1)}, bf16[2048,1280]{1,0:T(8,128)(2,1)}, u32[]{:S(2)}) copy-start(bf16[2048,1280]{1,0:T(8,128)(2,1)} %mixer.7) | copy-start | bytes 15728644
  7.6 7.1 %collective-permute-start.1 = (bf16[64,2048]{1,0:T(8,128)(2,1)S(1)}, bf16[64,2048]{1,0:T(8,128)(2,1)S(1)}, u32[]{:S(2)}, u32[]{:S(2)}) collective-permute-start(bf16[64,2048]{1,0:T(8,128)(2,1)S(1)} %join.4.first), channel_id=1, source_target_pairs={{0,1},{1,0},{2,3},{3,2},{4,5},{5,4},{6,7},{7,6},{8,9},{9,8},{10,11... | collective-permute-start | bytes 786440 | tf_op jit(solution)/shard_map/ppermute | solution.py:379
  9.6 2.3 %collective-permute-start.3 = (bf16[64,2048]{1,0:T(8,128)(2,1)S(1)}, bf16[64,2048]{1,0:T(8,128)(2,1)S(1)}, u32[]{:S(2)}, u32[]{:S(2)}) collective-permute-start(bf16[64,2048]{1,0:T(8,128)(2,1)S(1)} %join.6.first), channel_id=1, source_target_pairs={{0,1},{1,0},{2,3},{3,2},{4,5},{5,4},{6,7},{7,6},{8,9},{9,8},{10,11... | collective-permute-start | bytes 786440 | tf_op jit(solution)/shard_map/ppermute | solution.py:379
  12.9 6.9 %collective-permute-start.5 = (bf16[136,640]{1,0:T(8,128)(2,1)S(1)}, bf16[136,640]{1,0:T(8,128)(2,1)S(1)}, u32[]{:S(2)}, u32[]{:S(2)}) collective-permute-start(bf16[136,640]{1,0:T(8,128)(2,1)S(1)} %get-tuple-element.32), channel_id=1, source_target_pairs={{0,4},{4,0},{8,12},{12,8},{16,20},{20,16},{24,28},{28,24},{1,5},{5... | collective-permute-start | bytes 522248 | tf_op jit(solution)/shard_map/ppermute | solution.py:498
  19.9 7.0 %collective-permute-start.6 = (bf16[136,640]{1,0:T(8,128)(2,1)S(1)}, bf16[136,640]{1,0:T(8,128)(2,1)S(1)}, u32[]{:S(2)}, u32[]{:S(2)}) collective-permute-start(bf16[136,640]{1,0:T(8,128)(2,1)S(1)} %get-tuple-element.39.after), channel_id=1, source_target_pairs={{0,8},{4,12},{8,0},{12,4},{16,24},{20,28},{24,16},{28,20},{1,9},{5... | collective-permute-start | bytes 522248 | tf_op jit(solution)/shard_map/ppermute | solution.py:498
  27.0 10.2 %collective-permute-start.8 = (bf16[136,640]{1,0:T(8,128)(2,1)S(1)}, bf16[136,640]{1,0:T(8,128)(2,1)S(1)}, u32[]{:S(2)}, u32[]{:S(2)}) collective-permute-start(bf16[136,640]{1,0:T(8,128)(2,1)S(1)} %merge.3.after), channel_id=1, source_target_pairs={{0,16},{4,20},{8,24},{12,28},{16,0},{20,4},{24,8},{28,12},{1,17},{... | collective-permute-start | bytes 522248 | tf_op jit(solution)/shard_map/ppermute | solution.py:498
  29.7 16.3 %collective-permute-start.4 = (bf16[136,640]{1,0:T(8,128)(2,1)S(1)}, bf16[136,640]{1,0:T(8,128)(2,1)S(1)}, u32[]{:S(2)}, u32[]{:S(2)}) collective-permute-start(bf16[136,640]{1,0:T(8,128)(2,1)S(1)} %get-tuple-element.31), channel_id=1, source_target_pairs={{0,4},{4,0},{8,12},{12,8},{16,20},{20,16},{24,28},{28,24},{1,5},{5... | collective-permute-start | bytes 522248 | tf_op jit(solution)/shard_map/ppermute | solution.py:498
  31.2 14.8 %collective-permute-start.7 = (bf16[136,640]{1,0:T(8,128)(2,1)S(1)}, bf16[136,640]{1,0:T(8,128)(2,1)S(1)}, u32[]{:S(2)}, u32[]{:S(2)}) collective-permute-start(bf16[136,640]{1,0:T(8,128)(2,1)S(1)} %collective-permute-done.6.received.rest_1_), channel_id=1, source_target_pairs={{0,4},{4,0},{8,12},{12,8},{16,20},{20,16},{24,28},{28,24},{1,5},{5... | collective-permute-start | bytes 522248 | tf_op jit(solution)/shard_map/ppermute | solution.py:498
  37.2 8.8 %collective-permute-start.9 = (bf16[136,640]{1,0:T(8,128)(2,1)S(1)}, bf16[136,640]{1,0:T(8,128)(2,1)S(1)}, u32[]{:S(2)}, u32[]{:S(2)}) collective-permute-start(bf16[136,640]{1,0:T(8,128)(2,1)S(1)} %collective-permute-done.8.rest_2_), channel_id=1, source_target_pairs={{0,4},{4,0},{8,12},{12,8},{16,20},{20,16},{24,28},{28,24},{1,5},{5... | collective-permute-start | bytes 522248 | tf_op jit(solution)/shard_map/ppermute | solution.py:498

commit v6 on v5

--- a/solution.py
+++ b/solution.py
@@ -322,17 +322,18 @@
         when_here(functools.partial(second_region, c))
 
 
-def bucket_rows(received, bits, state, width):
+def bucket_rows(received, bits, state, width, wanted):
     running = jnp.ones((1, width), F32)
     out = []
     for bit in range(bits):
         upper = upper_half(bit, width)
-        scale = jnp.where(upper, running, 0.0)
-        out.append((received[bit][0:state, :].astype(F32) * scale).astype(BF16))
+        if bit in wanted:
+            scale = jnp.where(upper, running, 0.0)
+            out.append((received[bit][0:state, :].astype(F32) * scale).astype(BF16))
         if bit + 1 < bits:
             extra = received[bit][state:, :].astype(F32)
             running = jnp.where(upper, running * (extra[0:1] + extra[1:2]), running)
-    return jnp.concatenate(out, 0)
+    return jnp.concatenate(out, 0) if len(out) > 1 else out[0]
 
 
 def read_levels(read_t, weight_h, at, levels):
@@ -341,15 +342,39 @@
     return jnp.concatenate(queries, 0) if len(queries) > 1 else queries[0]
 
 
-def final_kernel(starts, local_bits, bits, side, read_t, weight_h, *rest):
+def near_kernel(starts, local_bits, bits, read_t, weight_h, *rest):
     pieces = len(starts) - 1
     received, rest = rest[:bits], rest[bits:]
     bases, reaches, rest = rest[:pieces], rest[pieces : 2 * pieces], rest[2 * pieces :]
+    out, buckets = rest
+    columns = own_columns(bases[0].shape[1])[1]
+    buckets[...] = bucket_rows(received, bits, read_t.shape[0], buckets.shape[1], range(bits))
+    levels = [local_bits + 1 + bit for bit in range(bits)]
+    for piece in range(pieces):
+
+        def block(g, carry, piece=piece):
+            at = pl.ds(pl.multiple_of((starts[piece] + g) * BLOCK, BLOCK), BLOCK)
+            here = pl.ds(pl.multiple_of(g * BLOCK, BLOCK), BLOCK)
+            part = dot(read_levels(read_t, weight_h, at, levels), buckets[...], TN)
+            out[at, :] = bases[piece][here, columns] + part * reaches[piece][here, columns]
+            return carry
+
+        lax.fori_loop(0, starts[piece + 1] - starts[piece], block, 0, unroll=True)
+
+
+def final_kernel(starts, local_bits, bits, wanted, side, read_t, weight_h, *rest):
+    pieces = len(starts) - 1
+    received, rest = rest[:bits], rest[bits:]
+    near = None
+    if side:
+        near, rest = rest[0], rest[1:]
+        reaches = rest[:pieces]
+    else:
+        bases, reaches = rest[:pieces], rest[pieces : 2 * pieces]
     out, buckets, ready, sems = rest[-4:]
     columns = own_columns(out.shape[1])[side]
-    buckets[...] = bucket_rows(received, bits, read_t.shape[0], buckets.shape[1])
-
-    levels = [local_bits + 1 + bit for bit in range(bits)]
+    buckets[...] = bucket_rows(received, bits, read_t.shape[0], buckets.shape[1], wanted)
+    levels = [local_bits + 1 + bit for bit in wanted]
 
     def copy(c, at):
         return pltpu.make_async_copy(ready.at[c], out.at[pl.ds(at, BLOCK), columns], sems.at[c])
@@ -362,7 +387,11 @@
             here = pl.ds(pl.multiple_of(g * BLOCK, BLOCK), BLOCK)
             query = read_levels(read_t, weight_h, pl.ds(at, BLOCK), levels)
             part = dot(query, buckets[...], TN)
-            ready[c] = (bases[piece][here, columns] + part * reaches[piece][here, columns]).astype(BF16)
+            if side:
+                base = near[pl.ds(at, BLOCK), :]
+            else:
+                base = bases[piece][here, columns]
+            ready[c] = (base + part * reaches[piece][here, columns]).astype(BF16)
             copy(c, at).start()
             return carry
 
@@ -497,7 +526,7 @@
     def swap(value, bit):
         return lax.ppermute(value, "seq", [(i, i ^ 1 << bit) for i in range(ranks)])
 
-    shares = [3] * (device_bits - 1) + [2]
+    shares = ([3] + [2] * (device_bits - 2) + [3])[:device_bits]
     starts = [0]
     for share in shares:
         starts.append(starts[-1] + max(1, blocks * share // sum(shares)))
@@ -537,23 +566,21 @@
     if device_bits > 1:
         other_parts.append(swap(own_parts[-1], 0))
 
-    out = None
-    for side, parts in enumerate((own_parts, other_parts)):
-        operands = [read_t, weight_h, *parts, *bases, *reaches]
+    def finish(side, operands, wanted, out):
         specs = [VMEM_SPEC] * len(operands)
         aliases = {}
         if out is not None:
             aliases = {len(operands): 0}
-            operands.append(out)
+            operands = operands + [out]
             specs.append(ANY_SPEC)
-        out = pl.pallas_call(
-            functools.partial(final_kernel, starts, local_bits, device_bits, side),
+        return pl.pallas_call(
+            functools.partial(final_kernel, starts, local_bits, device_bits, wanted, side),
             in_specs=specs,
             out_specs=ANY_SPEC,
             out_shape=sds((tokens, width), BF16),
             input_output_aliases=aliases,
             scratch_shapes=[
-                pltpu.VMEM((device_bits * state, half), BF16),
+                pltpu.VMEM((len(wanted) * state, half), BF16),
                 pltpu.VMEM((blocks, BLOCK, half), BF16),
                 pltpu.SemaphoreType.DMA((blocks,)),
             ],
@@ -561,7 +588,20 @@
             cost_estimate=cost(tokens * width * state, tokens * width * 3),
             name="final",
         )(*operands)
-    return out
+
+    out = finish(0, [read_t, weight_h, *own_parts, *bases, *reaches], list(range(device_bits)), None)
+    near_bits = device_bits - 1
+    near = pl.pallas_call(
+        functools.partial(near_kernel, starts, local_bits, near_bits),
+        in_specs=[VMEM_SPEC] * (2 + near_bits + 2 * len(bases)),
+        out_specs=VMEM_SPEC,
+        out_shape=sds((tokens, half), F32),
+        scratch_shapes=[pltpu.VMEM((near_bits * state, half), BF16)],
+        compiler_params=grant(4),
+        cost_estimate=cost(tokens * width * state * 2, tokens * width * 3),
+        name="near",
+    )(read_t, weight_h, *other_parts[:-1], *bases, *reaches)
+    return finish(1, [read_t, weight_h, *other_parts, near, *reaches], [device_bits - 1], out)
 
 
 def solution(mesh):

time: 48.8 us -> 49.6 us (1.016)
  waiting for transfers between devices: 9.65 us -> 10.3 us
    ppermute x6, waiting for transfers between devices: 6.28 us -> 6.95 us  [swap(): return lax.ppermute(value, 'seq', [(i, i ^ 1 << bit) for i in range(ranks)])]
    pallas_call x3, Pallas kernels: 14 us -> 13.5 us  [local(): pl.pallas_call(functools.partial(local_kernel, heads, padded, local_bits,...]
    pallas_call x2 -> x3, Pallas kernels: 5.19 us -> 5.69 us  [the longest x2 4.58 us: finish(): pl.pallas_call(functools.partial(final_kernel, starts, local_bits, device...]
  transfers between devices with their start and end apart: 10 -> 10, of which waited for: 4 -> 5; matrix products, arithmetic and copies ran while one was open for 0% -> 0% of each run, Pallas kernels for 47% -> 48%
where the time goes in v6:
time: 49.6 us; the launch traced here: 49.5 us
  Pallas kernels  25.7 us (52%)
  starting transfers between devices  13.2 us (27%)
  waiting for transfers between devices  10.3 us (21%)
    pallas_call x3, Pallas kernels, local(): pl.pallas_call(functools.partial(local_kernel, heads, padded, local_bits,...  13.5 us
    ppermute x6, starting transfers between devices, swap(): return lax.ppermute(value, 'seq', [(i, i ^ 1 << bit) for i in range(ranks)])  9.98 us
    ppermute x6, waiting for transfers between devices, swap(): return lax.ppermute(value, 'seq', [(i, i ^ 1 << bit) for i in range(ranks)])  6.95 us
    pallas_call x2, Pallas kernels, finish(): pl.pallas_call(functools.partial(final_kernel, starts, local_bits, device...  4.58 us
    ppermute x4, waiting for transfers between devices, gather_columns(): other = lax.ppermute(pieces, axis, [(i, i ^ stride) for i in range(size)])  3.37 us
    ppermute x4, starting transfers between devices, gather_columns(): other = lax.ppermute(pieces, axis, [(i, i ^ stride) for i in range(size)])  3.17 us
    pallas_call x1, Pallas kernels, on_device(): pl.pallas_call(functools.partial(prep_kernel, heads, padded, layout), in_...  3.04 us
    pallas_call x1, Pallas kernels, on_device(): pl.pallas_call(functools.partial(scale_kernel, heads, padded, layout), in...  2.25 us
  transfers between devices with their start and end apart: 10, of which 5 were waited for; matrix products, arithmetic and copies ran while one was open for 0% of the time, Pallas kernels for 48%

profile of v6, /device:TPU:0, one launch (start us, length us, event | category | flops | bytes accessed | tf_op | source)
XLA Modules:
  0.0 49.5 jit_solution(15531485306196198760)
XLA Ops:
  0.0 3.0 %collective-permute-start = (bf16[32,2048]{1,0:T(8,128)(2,1)}, bf16[32,2048]{1,0:T(8,128)(2,1)S(1)}, u32[]{:S(2)}, u32[]{:S(2)}) collective-permute-start(bf16[32,2048]{1,0:T(8,128)(2,1)} %bitcast.3), channel_id=1, source_target_pairs={{0,2},{1,3},{2,0},{3,1},{4,6},{5,7},{6,4},{7,5},{8,10},{9,11},{10,... | collective-permute-start | bytes 393224 | tf_op jit(solution)/shard_map/ppermute | solution.py:408
  3.0 0.1 collective-permute-start.2
  3.0 3.0 %prep.1 = (bf16[2048,128]{1,0:T(8,128)(2,1)S(1)}, f32[2048,128]{1,0:T(8,128)S(1)}, f32[32,2048]{1,0:T(8,128)S(1)}, f32[7,2048]{1,0:T(8,128)S(1)}, f32[80,1280]{1,0:T(8,128)S(1)}) custom-call(f32[20,2048]{1,0:T(8,128)} %log_decay_far.1, f32[20,2048]{1,0:T(8,128)} %step_size_far.1, s32[7,2048]{1,0:T(8,128)} %level_index_far.1, f32[7,8]{1,0:T(8,128)} %level_table_far.1, ...), custom_call_target="tpu_custom_call" | custom-call | flops 2000000000 | bytes 4000000 | tf_op jit(solution)/shard_map/prep/pallas_call | solution.py:445
  6.1 1.5 %collective-permute-done.second = bf16[32,2048]{1,0:T(8,128)(2,1)S(1)} collective-permute-done((bf16[32,2048]{1,0:T(8,128)(2,1)}, bf16[32,2048]{1,0:T(8,128)(2,1)S(1)}, u32[]{:S(2)}, u32[]{:S(2)}) %collective-permute-start) | collective-permute-done | bytes 131104 | tf_op jit(solution)/shard_map/ppermute | solution.py:408
  7.6 0.0 copy-done.1
  7.6 0.1 collective-permute-start.1
  7.7 1.9 %collective-permute-done.2.second = bf16[32,2048]{1,0:T(8,128)(2,1)S(1)} collective-permute-done((bf16[32,2048]{1,0:T(8,128)(2,1)}, bf16[32,2048]{1,0:T(8,128)(2,1)S(1)}, u32[]{:S(2)}, u32[]{:S(2)}) %collective-permute-start.2) | collective-permute-done | bytes 131104 | tf_op jit(solution)/shard_map/ppermute | solution.py:408
  9.6 0.1 collective-permute-start.3
  9.7 2.2 %scale.1 = (bf16[2048,1280]{1,0:T(8,128)(2,1)S(1)}, bf16[2048,1280]{1,0:T(8,128)(2,1)S(1)}) custom-call(bf16[2048,1280]{1,0:T(8,128)(2,1)S(1)} %copy-done, bf16[2048,128]{1,0:T(8,128)(2,1)S(1)} %get-tuple-element.29.factors, f32[80,1280]{1,0:T(8,128)S(1)} %get-tuple-element.27.rest_0_.rows.after), custom_call_target="tpu_custom_call" | custom-call | flops 3000000000 | bytes 15728640 | tf_op jit(solution)/shard_map/scale/pallas_call | solution.py:478
  11.9 0.0 collective-permute-done.3.second
  12.0 0.9 %state.1 = (bf16[136,640]{1,0:T(8,128)(2,1)S(1)}, bf16[136,640]{1,0:T(8,128)(2,1)S(1)}, f32[128,640]{1,0:T(8,128)S(1)}, f32[8,640]{1,0:T(8,128)S(1)}) custom-call(bf16[2048,1280]{1,0:T(8,128)(2,1)S(1)} %get-tuple-element.30.to_total, bf16[128,2048]{1,0:T(8,128)(2,1)S(1)} %join.7.write_t, f32[80,1280]{1,0:T(8,128)S(1)} %get-tuple-element.27.rest_0_.rows.after), custom_call_target="tpu_custom_call" | custom-call | flops 671088640 | bytes 5242880 | tf_op jit(solution)/shard_map/state/pallas_call | solution.py:490
  12.9 1.8 %collective-permute-start.5 = (bf16[136,640]{1,0:T(8,128)(2,1)S(1)}, bf16[136,640]{1,0:T(8,128)(2,1)S(1)}, u32[]{:S(2)}, u32[]{:S(2)}) collective-permute-start(bf16[136,640]{1,0:T(8,128)(2,1)S(1)} %get-tuple-element.32), channel_id=1, source_target_pairs={{0,4},{4,0},{8,12},{12,8},{16,20},{20,16},{24,28},{28,24},{1,5},{5... | collective-permute-start | bytes 522248 | tf_op jit(solution)/shard_map/ppermute | solution.py:527
  14.7 0.0 collective-permute-done.1.second
  14.8 4.1 %local.3 = (f32[768,1280]{1,0:T(8,128)S(1)}, f32[768,1280]{1,0:T(8,128)S(1)}, f32[3,128,1280]{2,1,0:T(8,128)S(1)}) custom-call(bf16[2048,1280]{1,0:T(8,128)(2,1)S(1)} %copy-done, bf16[2048,1280]{1,0:T(8,128)(2,1)S(1)} %get-tuple-element.35.scaled, bf16[128,2048]{1,0:T(8,128)(2,1)S(1)} %join.7.write_t, bf16[128,2048]{1,0:T(8,128)(2,1)S(1)} %join.5.read_t, ...), custom_call_target="tpu_custom_call" | custom-call | flops 3932160000 | bytes 7864320 | tf_op jit(solution)/shard_map/local/pallas_call | solution.py:502
  18.9 0.9 %collective-permute-done.5.received.rest_0_ = bf16[136,640]{1,0:T(8,128)(2,1)S(1)} collective-permute-done((bf16[136,640]{1,0:T(8,128)(2,1)S(1)}, bf16[136,640]{1,0:T(8,128)(2,1)S(1)}, u32[]{:S(2)}, u32[]{:S(2)}) %collective-permute-start.5) | collective-permute-done | bytes 174112 | tf_op jit(solution)/shard_map/ppermute | solution.py:527
  19.8 0.1 merge.2
  19.9 1.8 %collective-permute-start.6 = (bf16[136,640]{1,0:T(8,128)(2,1)S(1)}, bf16[136,640]{1,0:T(8,128)(2,1)S(1)}, u32[]{:S(2)}, u32[]{:S(2)}) collective-permute-start(bf16[136,640]{1,0:T(8,128)(2,1)S(1)} %get-tuple-element.39.after), channel_id=1, source_target_pairs={{0,8},{4,12},{8,0},{12,4},{16,24},{20,28},{24,16},{28,20},{1,9},{5... | collective-permute-start | bytes 522248 | tf_op jit(solution)/shard_map/ppermute | solution.py:527
  21.7 3.2 %local.4 = (f32[512,1280]{1,0:T(8,128)S(1)}, f32[512,1280]{1,0:T(8,128)S(1)}, f32[3,128,1280]{2,1,0:T(8,128)S(1)}) custom-call(bf16[2048,1280]{1,0:T(8,128)(2,1)S(1)} %copy-done, bf16[2048,1280]{1,0:T(8,128)(2,1)S(1)} %get-tuple-element.35.scaled, bf16[128,2048]{1,0:T(8,128)(2,1)S(1)} %join.7.write_t, bf16[128,2048]{1,0:T(8,128)(2,1)S(1)} %join.5.read_t, ...), custom_call_target="tpu_custom_call" | custom-call | flops 2621440000 | bytes 5242880 | tf_op jit(solution)/shard_map/local/pallas_call | solution.py:502
  25.0 1.0 %collective-permute-done.6.received.rest_1_ = bf16[136,640]{1,0:T(8,128)(2,1)S(1)} collective-permute-done((bf16[136,640]{1,0:T(8,128)(2,1)S(1)}, bf16[136,640]{1,0:T(8,128)(2,1)S(1)}, u32[]{:S(2)}, u32[]{:S(2)}) %collective-permute-start.6) | collective-permute-done | bytes 174112 | tf_op jit(solution)/shard_map/ppermute | solution.py:527
  25.9 0.1 merge.3.after
  26.0 2.8 %collective-permute-start.8 = (bf16[136,640]{1,0:T(8,128)(2,1)S(1)}, bf16[136,640]{1,0:T(8,128)(2,1)S(1)}, u32[]{:S(2)}, u32[]{:S(2)}) collective-permute-start(bf16[136,640]{1,0:T(8,128)(2,1)S(1)} %merge.3.after), channel_id=1, source_target_pairs={{0,16},{4,20},{8,24},{12,28},{16,0},{20,4},{24,8},{28,12},{1,17},{... | collective-permute-start | bytes 522248 | tf_op jit(solution)/shard_map/ppermute | solution.py:527
  28.8 1.5 %collective-permute-start.4 = (bf16[136,640]{1,0:T(8,128)(2,1)S(1)}, bf16[136,640]{1,0:T(8,128)(2,1)S(1)}, u32[]{:S(2)}, u32[]{:S(2)}) collective-permute-start(bf16[136,640]{1,0:T(8,128)(2,1)S(1)} %get-tuple-element.31), channel_id=1, source_target_pairs={{0,4},{4,0},{8,12},{12,8},{16,20},{20,16},{24,28},{28,24},{1,5},{5... | collective-permute-start | bytes 522248 | tf_op jit(solution)/shard_map/ppermute | solution.py:527
  30.3 0.5 %collective-permute-start.7 = (bf16[136,640]{1,0:T(8,128)(2,1)S(1)}, bf16[136,640]{1,0:T(8,128)(2,1)S(1)}, u32[]{:S(2)}, u32[]{:S(2)}) collective-permute-start(bf16[136,640]{1,0:T(8,128)(2,1)S(1)} %collective-permute-done.6.received.rest_1_), channel_id=1, source_target_pairs={{0,4},{4,0},{8,12},{12,8},{16,20},{20,16},{24,28},{28,24},{1,5},{5... | collective-permute-start | bytes 522248 | tf_op jit(solution)/shard_map/ppermute | solution.py:527
  30.9 5.1 %collective-permute-done.8.rest_2_ = bf16[136,640]{1,0:T(8,128)(2,1)S(1)} collective-permute-done((bf16[136,640]{1,0:T(8,128)(2,1)S(1)}, bf16[136,640]{1,0:T(8,128)(2,1)S(1)}, u32[]{:S(2)}, u32[]{:S(2)}) %collective-permute-start.8) | collective-permute-done | bytes 174112 | tf_op jit(solution)/shard_map/ppermute | solution.py:527
  35.9 1.5 %collective-permute-start.9 = (bf16[136,640]{1,0:T(8,128)(2,1)S(1)}, bf16[136,640]{1,0:T(8,128)(2,1)S(1)}, u32[]{:S(2)}, u32[]{:S(2)}) collective-permute-start(bf16[136,640]{1,0:T(8,128)(2,1)S(1)} %collective-permute-done.8.rest_2_), channel_id=1, source_target_pairs={{0,4},{4,0},{8,12},{12,8},{16,20},{20,16},{24,28},{28,24},{1,5},{5... | collective-permute-start | bytes 522248 | tf_op jit(solution)/shard_map/ppermute | solution.py:527
  37.5 6.1 %local.5 = (f32[768,1280]{1,0:T(8,128)S(1)}, f32[768,1280]{1,0:T(8,128)S(1)}, f32[3,128,1280]{2,1,0:T(8,128)}) custom-call(bf16[2048,1280]{1,0:T(8,128)(2,1)S(1)} %copy-done, bf16[2048,1280]{1,0:T(8,128)(2,1)S(1)} %get-tuple-element.35.scaled, bf16[128,2048]{1,0:T(8,128)(2,1)S(1)} %join.7.write_t, bf16[128,2048]{1,0:T(8,128)(2,1)S(1)} %join.5.read_t, ...), custom_call_target="tpu_custom_call" | custom-call | flops 3932160000 | bytes 7864320 | tf_op jit(solution)/shard_map/local/pallas_call | solution.py:502
  43.6 2.7 %final.2.rest_7_ = bf16[2048,1280]{1,0:T(8,128)(2,1)} custom-call(bf16[128,2048]{1,0:T(8,128)(2,1)S(1)} %join.5.read_t, f32[7,2048]{1,0:T(8,128)S(1)} %get-tuple-element.28.weight_h, bf16[136,640]{1,0:T(8,128)(2,1)S(1)} %collective-permute-done.5.received.rest_0_, bf16[136,640]{1,0:T(8,128)(2,1)S(1)} %collective-permute-done.6.received.rest_1_, ...), custom_call_target="tpu_custom_call" | custom-call | flops 335544320 | bytes 7864320 | tf_op jit(solution)/shard_map/final/pallas_call | solution.py:576
  46.3 0.0 collective-permute-done.4.rest_0_
  46.3 0.0 collective-permute-done.7.rest_1_
  46.3 1.1 %near.1.rest_3_ = f32[2048,640]{1,0:T(8,128)S(1)} custom-call(bf16[128,2048]{1,0:T(8,128)(2,1)S(1)} %join.5.read_t, f32[7,2048]{1,0:T(8,128)S(1)} %get-tuple-element.28.weight_h, bf16[136,640]{1,0:T(8,128)(2,1)S(1)} %collective-permute-done.4.rest_0_, bf16[136,640]{1,0:T(8,128)(2,1)S(1)} %collective-permute-done.7.rest_1_, ...), custom_call_target="tpu_custom_call" | custom-call | flops 671088640 | bytes 7864320 | tf_op jit(solution)/shard_map/near/pallas_call | solution.py:594
  47.4 0.0 collective-permute-done.9.rest_2_
  47.4 1.9 %final.3 = bf16[2048,1280]{1,0:T(8,128)(2,1)} custom-call(bf16[128,2048]{1,0:T(8,128)(2,1)S(1)} %join.5.read_t, f32[7,2048]{1,0:T(8,128)S(1)} %get-tuple-element.28.weight_h, bf16[136,640]{1,0:T(8,128)(2,1)S(1)} %collective-permute-done.4.rest_0_, bf16[136,640]{1,0:T(8,128)(2,1)S(1)} %collective-permute-done.7.rest_1_, ...), custom_call_target="tpu_custom_call", output_to_operand_aliasing={{}: (9, {})} | custom-call | flops 335544320 | bytes 7864320 | tf_op jit(solution)/shard_map/final/pallas_call | solution.py:576
  (10 shorter events, 0.1 us)
Async XLA Ops:
  0.0 7.6 %copy-start.1 = (bf16[2048,32]{0,1:T(8,128)(2,1)S(1)}, bf16[2048,32]{0,1:T(8,128)(2,1)}, u32[]{:S(2)}) copy-start(bf16[2048,32]{0,1:T(8,128)(2,1)} %param.10) | copy-start | bytes 393220
  0.0 7.6 %collective-permute-start = (bf16[32,2048]{1,0:T(8,128)(2,1)}, bf16[32,2048]{1,0:T(8,128)(2,1)S(1)}, u32[]{:S(2)}, u32[]{:S(2)}) collective-permute-start(bf16[32,2048]{1,0:T(8,128)(2,1)} %bitcast.3), channel_id=1, source_target_pairs={{0,2},{1,3},{2,0},{3,1},{4,6},{5,7},{6,4},{7,5},{8,10},{9,11},{10,... | collective-permute-start | bytes 393224 | tf_op jit(solution)/shard_map/ppermute | solution.py:408
  3.0 6.6 %collective-permute-start.2 = (bf16[32,2048]{1,0:T(8,128)(2,1)}, bf16[32,2048]{1,0:T(8,128)(2,1)S(1)}, u32[]{:S(2)}, u32[]{:S(2)}) collective-permute-start(bf16[32,2048]{1,0:T(8,128)(2,1)} %bitcast.5), channel_id=1, source_target_pairs={{0,2},{1,3},{2,0},{3,1},{4,6},{5,7},{6,4},{7,5},{8,10},{9,11},{10,... | collective-permute-start | bytes 393224 | tf_op jit(solution)/shard_map/ppermute | solution.py:408
  3.0 6.5 %copy-start.2 = (bf16[2048,32]{0,1:T(8,128)(2,1)S(1)}, bf16[2048,32]{0,1:T(8,128)(2,1)}, u32[]{:S(2)}) copy-start(bf16[2048,32]{0,1:T(8,128)(2,1)} %param.9) | copy-start | bytes 393220
  3.0 6.6 %copy-start = (bf16[2048,1280]{1,0:T(8,128)(2,1)S(1)}, bf16[2048,1280]{1,0:T(8,128)(2,1)}, u32[]{:S(2)}) copy-start(bf16[2048,1280]{1,0:T(8,128)(2,1)} %mixer.7) | copy-start | bytes 15728644
  7.6 7.1 %collective-permute-start.1 = (bf16[64,2048]{1,0:T(8,128)(2,1)S(1)}, bf16[64,2048]{1,0:T(8,128)(2,1)S(1)}, u32[]{:S(2)}, u32[]{:S(2)}) collective-permute-start(bf16[64,2048]{1,0:T(8,128)(2,1)S(1)} %join.4.first), channel_id=1, source_target_pairs={{0,1},{1,0},{2,3},{3,2},{4,5},{5,4},{6,7},{7,6},{8,9},{9,8},{10,11... | collective-permute-start | bytes 786440 | tf_op jit(solution)/shard_map/ppermute | solution.py:408
  9.6 2.3 %collective-permute-start.3 = (bf16[64,2048]{1,0:T(8,128)(2,1)S(1)}, bf16[64,2048]{1,0:T(8,128)(2,1)S(1)}, u32[]{:S(2)}, u32[]{:S(2)}) collective-permute-start(bf16[64,2048]{1,0:T(8,128)(2,1)S(1)} %join.6.first), channel_id=1, source_target_pairs={{0,1},{1,0},{2,3},{3,2},{4,5},{5,4},{6,7},{7,6},{8,9},{9,8},{10,11... | collective-permute-start | bytes 786440 | tf_op jit(solution)/shard_map/ppermute | solution.py:408
  12.9 6.9 %collective-permute-start.5 = (bf16[136,640]{1,0:T(8,128)(2,1)S(1)}, bf16[136,640]{1,0:T(8,128)(2,1)S(1)}, u32[]{:S(2)}, u32[]{:S(2)}) collective-permute-start(bf16[136,640]{1,0:T(8,128)(2,1)S(1)} %get-tuple-element.32), channel_id=1, source_target_pairs={{0,4},{4,0},{8,12},{12,8},{16,20},{20,16},{24,28},{28,24},{1,5},{5... | collective-permute-start | bytes 522248 | tf_op jit(solution)/shard_map/ppermute | solution.py:527
  19.9 6.0 %collective-permute-start.6 = (bf16[136,640]{1,0:T(8,128)(2,1)S(1)}, bf16[136,640]{1,0:T(8,128)(2,1)S(1)}, u32[]{:S(2)}, u32[]{:S(2)}) collective-permute-start(bf16[136,640]{1,0:T(8,128)(2,1)S(1)} %get-tuple-element.39.after), channel_id=1, source_target_pairs={{0,8},{4,12},{8,0},{12,4},{16,24},{20,28},{24,16},{28,20},{1,9},{5... | collective-permute-start | bytes 522248 | tf_op jit(solution)/shard_map/ppermute | solution.py:527
  26.0 9.9 %collective-permute-start.8 = (bf16[136,640]{1,0:T(8,128)(2,1)S(1)}, bf16[136,640]{1,0:T(8,128)(2,1)S(1)}, u32[]{:S(2)}, u32[]{:S(2)}) collective-permute-start(bf16[136,640]{1,0:T(8,128)(2,1)S(1)} %merge.3.after), channel_id=1, source_target_pairs={{0,16},{4,20},{8,24},{12,28},{16,0},{20,4},{24,8},{28,12},{1,17},{... | collective-permute-start | bytes 522248 | tf_op jit(solution)/shard_map/ppermute | solution.py:527
  28.8 17.4 %collective-permute-start.4 = (bf16[136,640]{1,0:T(8,128)(2,1)S(1)}, bf16[136,640]{1,0:T(8,128)(2,1)S(1)}, u32[]{:S(2)}, u32[]{:S(2)}) collective-permute-start(bf16[136,640]{1,0:T(8,128)(2,1)S(1)} %get-tuple-element.31), channel_id=1, source_target_pairs={{0,4},{4,0},{8,12},{12,8},{16,20},{20,16},{24,28},{28,24},{1,5},{5... | collective-permute-start | bytes 522248 | tf_op jit(solution)/shard_map/ppermute | solution.py:527
  30.3 15.9 %collective-permute-start.7 = (bf16[136,640]{1,0:T(8,128)(2,1)S(1)}, bf16[136,640]{1,0:T(8,128)(2,1)S(1)}, u32[]{:S(2)}, u32[]{:S(2)}) collective-permute-start(bf16[136,640]{1,0:T(8,128)(2,1)S(1)} %collective-permute-done.6.received.rest_1_), channel_id=1, source_target_pairs={{0,4},{4,0},{8,12},{12,8},{16,20},{20,16},{24,28},{28,24},{1,5},{5... | collective-permute-start | bytes 522248 | tf_op jit(solution)/shard_map/ppermute | solution.py:527
  35.9 11.5 %collective-permute-start.9 = (bf16[136,640]{1,0:T(8,128)(2,1)S(1)}, bf16[136,640]{1,0:T(8,128)(2,1)S(1)}, u32[]{:S(2)}, u32[]{:S(2)}) collective-permute-start(bf16[136,640]{1,0:T(8,128)(2,1)S(1)} %collective-permute-done.8.rest_2_), channel_id=1, source_target_pairs={{0,4},{4,0},{8,12},{12,8},{16,20},{20,16},{24,28},{28,24},{1,5},{5... | collective-permute-start | bytes 522248 | tf_op jit(solution)/shard_map/ppermute | solution.py:527

commit v7 on v6

--- a/solution.py
+++ b/solution.py
@@ -230,7 +230,7 @@
     wide = spread(2 * padded, padded, heads, width)
     causal = iota((HALF, HALF), 0) >= iota((HALF, HALF), 1)
     lane = iota((HALF, LANES), 1)
-    own = [as_bf16((lane >= k * per_head) & (lane < (k + 1) * per_head)) for k in range(heads_here)]
+    own = [(lane >= k * per_head) & (lane < (k + 1) * per_head) for k in range(heads_here)]
     live = [bit for bit in range(bits) if (first >> bit) & 1]
     for bit in live:
         slots[bit] = slots_in[bit]
@@ -279,7 +279,9 @@
                     left_side.append(mixing.astype(BF16))
                 part = dot(
                     jnp.concatenate(left_side, 1),
-                    jnp.concatenate([value * mask for mask in own], 0),
+                    jnp.concatenate(
+                        [jnp.where(mask, value.astype(F32), 0.0).astype(BF16) for mask in own], 0
+                    ),
                 )
                 base[put_at, here] = part + rest[:, inner : inner + LANES]
 
@@ -526,7 +528,7 @@
     def swap(value, bit):
         return lax.ppermute(value, "seq", [(i, i ^ 1 << bit) for i in range(ranks)])
 
-    shares = ([3] + [2] * (device_bits - 2) + [3])[:device_bits]
+    shares = ([2] + [3] * (device_bits - 1))[:device_bits]
     starts = [0]
     for share in shares:
         starts.append(starts[-1] + max(1, blocks * share // sum(shares)))

time: 49.6 us -> 50.2 us (1.012)
  waiting for transfers between devices: 10.3 us -> 11.5 us
    ppermute x6, waiting for transfers between devices: 6.95 us -> 8.15 us  [swap(): return lax.ppermute(value, 'seq', [(i, i ^ 1 << bit) for i in range(ranks)])]
    pallas_call x3, Pallas kernels: 13.5 us -> 13 us  [local(): pl.pallas_call(functools.partial(local_kernel, heads, padded, local_bits,...]
  transfers between devices with their start and end apart: 10 -> 10, of which waited for: 5 -> 4; matrix products, arithmetic and copies ran while one was open for 0% -> 0% of each run, Pallas kernels for 48% -> 46%
where the time goes in v7:
time: 50.2 us; the launch traced here: 50.1 us
  Pallas kernels  25.3 us (50%)
  starting transfers between devices  13 us (26%)
  waiting for transfers between devices  11.5 us (23%)
    pallas_call x3, Pallas kernels, local(): pl.pallas_call(functools.partial(local_kernel, heads, padded, local_bits,...  13 us
    ppermute x6, starting transfers between devices, swap(): return lax.ppermute(value, 'seq', [(i, i ^ 1 << bit) for i in range(ranks)])  9.79 us
    ppermute x6, waiting for transfers between devices, swap(): return lax.ppermute(value, 'seq', [(i, i ^ 1 << bit) for i in range(ranks)])  8.15 us
    pallas_call x2, Pallas kernels, finish(): pl.pallas_call(functools.partial(final_kernel, starts, local_bits, device...  4.6 us
    ppermute x4, waiting for transfers between devices, gather_columns(): other = lax.ppermute(pieces, axis, [(i, i ^ stride) for i in range(size)])  3.37 us
    ppermute x4, starting transfers between devices, gather_columns(): other = lax.ppermute(pieces, axis, [(i, i ^ stride) for i in range(size)])  3.17 us
    pallas_call x1, Pallas kernels, on_device(): pl.pallas_call(functools.partial(prep_kernel, heads, padded, layout), in_...  3.04 us
    pallas_call x1, Pallas kernels, on_device(): pl.pallas_call(functools.partial(scale_kernel, heads, padded, layout), in...  2.25 us
  transfers between devices with their start and end apart: 10, of which 4 were waited for; matrix products, arithmetic and copies ran while one was open for 0% of the time, Pallas kernels for 46%

profile of v7, /device:TPU:0, one launch (start us, length us, event | category | flops | bytes accessed | tf_op | source)
XLA Modules:
  0.0 50.1 jit_solution(14026321285042038039)
XLA Ops:
  0.0 3.0 %collective-permute-start = (bf16[32,2048]{1,0:T(8,128)(2,1)}, bf16[32,2048]{1,0:T(8,128)(2,1)S(1)}, u32[]{:S(2)}, u32[]{:S(2)}) collective-permute-start(bf16[32,2048]{1,0:T(8,128)(2,1)} %bitcast.3), channel_id=1, source_target_pairs={{0,2},{1,3},{2,0},{3,1},{4,6},{5,7},{6,4},{7,5},{8,10},{9,11},{10,... | collective-permute-start | bytes 393224 | tf_op jit(solution)/shard_map/ppermute | solution.py:410
  3.0 0.1 collective-permute-start.2
  3.0 3.0 %prep.1 = (bf16[2048,128]{1,0:T(8,128)(2,1)S(1)}, f32[2048,128]{1,0:T(8,128)S(1)}, f32[32,2048]{1,0:T(8,128)S(1)}, f32[7,2048]{1,0:T(8,128)S(1)}, f32[80,1280]{1,0:T(8,128)S(1)}) custom-call(f32[20,2048]{1,0:T(8,128)} %log_decay_far.1, f32[20,2048]{1,0:T(8,128)} %step_size_far.1, s32[7,2048]{1,0:T(8,128)} %level_index_far.1, f32[7,8]{1,0:T(8,128)} %level_table_far.1, ...), custom_call_target="tpu_custom_call" | custom-call | flops 2000000000 | bytes 4000000 | tf_op jit(solution)/shard_map/prep/pallas_call | solution.py:447
  6.1 1.5 %collective-permute-done.second = bf16[32,2048]{1,0:T(8,128)(2,1)S(1)} collective-permute-done((bf16[32,2048]{1,0:T(8,128)(2,1)}, bf16[32,2048]{1,0:T(8,128)(2,1)S(1)}, u32[]{:S(2)}, u32[]{:S(2)}) %collective-permute-start) | collective-permute-done | bytes 131104 | tf_op jit(solution)/shard_map/ppermute | solution.py:410
  7.6 0.0 copy-done.1
  7.6 0.1 collective-permute-start.1
  7.7 1.9 %collective-permute-done.2.second = bf16[32,2048]{1,0:T(8,128)(2,1)S(1)} collective-permute-done((bf16[32,2048]{1,0:T(8,128)(2,1)}, bf16[32,2048]{1,0:T(8,128)(2,1)S(1)}, u32[]{:S(2)}, u32[]{:S(2)}) %collective-permute-start.2) | collective-permute-done | bytes 131104 | tf_op jit(solution)/shard_map/ppermute | solution.py:410
  9.6 0.1 collective-permute-start.3
  9.7 2.2 %scale.1 = (bf16[2048,1280]{1,0:T(8,128)(2,1)S(1)}, bf16[2048,1280]{1,0:T(8,128)(2,1)S(1)}) custom-call(bf16[2048,1280]{1,0:T(8,128)(2,1)S(1)} %copy-done, bf16[2048,128]{1,0:T(8,128)(2,1)S(1)} %get-tuple-element.29.factors, f32[80,1280]{1,0:T(8,128)S(1)} %get-tuple-element.27.rest_0_.rows.after), custom_call_target="tpu_custom_call" | custom-call | flops 3000000000 | bytes 15728640 | tf_op jit(solution)/shard_map/scale/pallas_call | solution.py:480
  11.9 0.0 collective-permute-done.3.second
  12.0 1.0 %state.1 = (bf16[136,640]{1,0:T(8,128)(2,1)S(1)}, bf16[136,640]{1,0:T(8,128)(2,1)S(1)}, f32[128,640]{1,0:T(8,128)S(1)}, f32[8,640]{1,0:T(8,128)S(1)}) custom-call(bf16[2048,1280]{1,0:T(8,128)(2,1)S(1)} %get-tuple-element.30.to_total, bf16[128,2048]{1,0:T(8,128)(2,1)S(1)} %join.7.write_t, f32[80,1280]{1,0:T(8,128)S(1)} %get-tuple-element.27.rest_0_.rows.after), custom_call_target="tpu_custom_call" | custom-call | flops 671088640 | bytes 5242880 | tf_op jit(solution)/shard_map/state/pallas_call | solution.py:492
  12.9 1.8 %collective-permute-start.5 = (bf16[136,640]{1,0:T(8,128)(2,1)S(1)}, bf16[136,640]{1,0:T(8,128)(2,1)S(1)}, u32[]{:S(2)}, u32[]{:S(2)}) collective-permute-start(bf16[136,640]{1,0:T(8,128)(2,1)S(1)} %get-tuple-element.32), channel_id=1, source_target_pairs={{0,4},{4,0},{8,12},{12,8},{16,20},{20,16},{24,28},{28,24},{1,5},{5... | collective-permute-start | bytes 522248 | tf_op jit(solution)/shard_map/ppermute | solution.py:529
  14.7 0.0 collective-permute-done.1.second
  14.8 2.6 %local.3 = (f32[512,1280]{1,0:T(8,128)S(1)}, f32[512,1280]{1,0:T(8,128)S(1)}, f32[3,128,1280]{2,1,0:T(8,128)S(1)}) custom-call(bf16[2048,1280]{1,0:T(8,128)(2,1)S(1)} %copy-done, bf16[2048,1280]{1,0:T(8,128)(2,1)S(1)} %get-tuple-element.35.scaled, bf16[128,2048]{1,0:T(8,128)(2,1)S(1)} %join.7.write_t, bf16[128,2048]{1,0:T(8,128)(2,1)S(1)} %join.5.read_t, ...), custom_call_target="tpu_custom_call" | custom-call | flops 2621440000 | bytes 5242880 | tf_op jit(solution)/shard_map/local/pallas_call | solution.py:504
  17.4 2.4 %collective-permute-done.5.received.rest_0_ = bf16[136,640]{1,0:T(8,128)(2,1)S(1)} collective-permute-done((bf16[136,640]{1,0:T(8,128)(2,1)S(1)}, bf16[136,640]{1,0:T(8,128)(2,1)S(1)}, u32[]{:S(2)}, u32[]{:S(2)}) %collective-permute-start.5) | collective-permute-done | bytes 174112 | tf_op jit(solution)/shard_map/ppermute | solution.py:529
  19.8 0.1 merge.2
  19.9 1.8 %collective-permute-start.6 = (bf16[136,640]{1,0:T(8,128)(2,1)S(1)}, bf16[136,640]{1,0:T(8,128)(2,1)S(1)}, u32[]{:S(2)}, u32[]{:S(2)}) collective-permute-start(bf16[136,640]{1,0:T(8,128)(2,1)S(1)} %get-tuple-element.39.after), channel_id=1, source_target_pairs={{0,8},{4,12},{8,0},{12,4},{16,24},{20,28},{24,16},{28,20},{1,9},{5... | collective-permute-start | bytes 522248 | tf_op jit(solution)/shard_map/ppermute | solution.py:529
  21.7 4.4 %local.4 = (f32[768,1280]{1,0:T(8,128)S(1)}, f32[768,1280]{1,0:T(8,128)S(1)}, f32[3,128,1280]{2,1,0:T(8,128)S(1)}) custom-call(bf16[2048,1280]{1,0:T(8,128)(2,1)S(1)} %copy-done, bf16[2048,1280]{1,0:T(8,128)(2,1)S(1)} %get-tuple-element.35.scaled, bf16[128,2048]{1,0:T(8,128)(2,1)S(1)} %join.7.write_t, bf16[128,2048]{1,0:T(8,128)(2,1)S(1)} %join.5.read_t, ...), custom_call_target="tpu_custom_call" | custom-call | flops 3932160000 | bytes 7864320 | tf_op jit(solution)/shard_map/local/pallas_call | solution.py:504
  26.1 0.0 collective-permute-done.6.received.rest_1_
  26.2 0.1 merge.3.after
  26.2 2.6 %collective-permute-start.8 = (bf16[136,640]{1,0:T(8,128)(2,1)S(1)}, bf16[136,640]{1,0:T(8,128)(2,1)S(1)}, u32[]{:S(2)}, u32[]{:S(2)}) collective-permute-start(bf16[136,640]{1,0:T(8,128)(2,1)S(1)} %merge.3.after), channel_id=1, source_target_pairs={{0,16},{4,20},{8,24},{12,28},{16,0},{20,4},{24,8},{28,12},{1,17},{... | collective-permute-start | bytes 522248 | tf_op jit(solution)/shard_map/ppermute | solution.py:529
  28.9 1.5 %collective-permute-start.4 = (bf16[136,640]{1,0:T(8,128)(2,1)S(1)}, bf16[136,640]{1,0:T(8,128)(2,1)S(1)}, u32[]{:S(2)}, u32[]{:S(2)}) collective-permute-start(bf16[136,640]{1,0:T(8,128)(2,1)S(1)} %get-tuple-element.31), channel_id=1, source_target_pairs={{0,4},{4,0},{8,12},{12,8},{16,20},{20,16},{24,28},{28,24},{1,5},{5... | collective-permute-start | bytes 522248 | tf_op jit(solution)/shard_map/ppermute | solution.py:529
  30.4 0.5 collective-permute-start.7
  30.9 5.7 %collective-permute-done.8.rest_2_ = bf16[136,640]{1,0:T(8,128)(2,1)S(1)} collective-permute-done((bf16[136,640]{1,0:T(8,128)(2,1)S(1)}, bf16[136,640]{1,0:T(8,128)(2,1)S(1)}, u32[]{:S(2)}, u32[]{:S(2)}) %collective-permute-start.8) | collective-permute-done | bytes 174112 | tf_op jit(solution)/shard_map/ppermute | solution.py:529
  36.6 1.5 %collective-permute-start.9 = (bf16[136,640]{1,0:T(8,128)(2,1)S(1)}, bf16[136,640]{1,0:T(8,128)(2,1)S(1)}, u32[]{:S(2)}, u32[]{:S(2)}) collective-permute-start(bf16[136,640]{1,0:T(8,128)(2,1)S(1)} %collective-permute-done.8.rest_2_), channel_id=1, source_target_pairs={{0,4},{4,0},{8,12},{12,8},{16,20},{20,16},{24,28},{28,24},{1,5},{5... | collective-permute-start | bytes 522248 | tf_op jit(solution)/shard_map/ppermute | solution.py:529
  38.1 6.0 %local.5 = (f32[768,1280]{1,0:T(8,128)S(1)}, f32[768,1280]{1,0:T(8,128)S(1)}, f32[3,128,1280]{2,1,0:T(8,128)}) custom-call(bf16[2048,1280]{1,0:T(8,128)(2,1)S(1)} %copy-done, bf16[2048,1280]{1,0:T(8,128)(2,1)S(1)} %get-tuple-element.35.scaled, bf16[128,2048]{1,0:T(8,128)(2,1)S(1)} %join.7.write_t, bf16[128,2048]{1,0:T(8,128)(2,1)S(1)} %join.5.read_t, ...), custom_call_target="tpu_custom_call" | custom-call | flops 3932160000 | bytes 7864320 | tf_op jit(solution)/shard_map/local/pallas_call | solution.py:504
  44.1 2.7 %final.2.rest_7_ = bf16[2048,1280]{1,0:T(8,128)(2,1)} custom-call(bf16[128,2048]{1,0:T(8,128)(2,1)S(1)} %join.5.read_t, f32[7,2048]{1,0:T(8,128)S(1)} %get-tuple-element.28.weight_h, bf16[136,640]{1,0:T(8,128)(2,1)S(1)} %collective-permute-done.5.received.rest_0_, bf16[136,640]{1,0:T(8,128)(2,1)S(1)} %collective-permute-done.6.received.rest_1_, ...), custom_call_target="tpu_custom_call" | custom-call | flops 335544320 | bytes 7864320 | tf_op jit(solution)/shard_map/final/pallas_call | solution.py:578
  46.8 0.0 collective-permute-done.4.rest_0_
  46.8 0.0 collective-permute-done.7.rest_1_
  46.8 1.2 %near.1.rest_3_ = f32[2048,640]{1,0:T(8,128)S(1)} custom-call(bf16[128,2048]{1,0:T(8,128)(2,1)S(1)} %join.5.read_t, f32[7,2048]{1,0:T(8,128)S(1)} %get-tuple-element.28.weight_h, bf16[136,640]{1,0:T(8,128)(2,1)S(1)} %collective-permute-done.4.rest_0_, bf16[136,640]{1,0:T(8,128)(2,1)S(1)} %collective-permute-done.7.rest_1_, ...), custom_call_target="tpu_custom_call" | custom-call | flops 671088640 | bytes 7864320 | tf_op jit(solution)/shard_map/near/pallas_call | solution.py:596
  48.0 0.0 collective-permute-done.9.rest_2_
  48.0 1.9 %final.3 = bf16[2048,1280]{1,0:T(8,128)(2,1)} custom-call(bf16[128,2048]{1,0:T(8,128)(2,1)S(1)} %join.5.read_t, f32[7,2048]{1,0:T(8,128)S(1)} %get-tuple-element.28.weight_h, bf16[136,640]{1,0:T(8,128)(2,1)S(1)} %collective-permute-done.4.rest_0_, bf16[136,640]{1,0:T(8,128)(2,1)S(1)} %collective-permute-done.7.rest_1_, ...), custom_call_target="tpu_custom_call", output_to_operand_aliasing={{}: (9, {})} | custom-call | flops 335544320 | bytes 7864320 | tf_op jit(solution)/shard_map/final/pallas_call | solution.py:578
  (10 shorter events, 0.1 us)
Async XLA Ops:
  0.0 7.6 %copy-start.1 = (bf16[2048,32]{0,1:T(8,128)(2,1)S(1)}, bf16[2048,32]{0,1:T(8,128)(2,1)}, u32[]{:S(2)}) copy-start(bf16[2048,32]{0,1:T(8,128)(2,1)} %param.10) | copy-start | bytes 393220
  0.0 7.6 %collective-permute-start = (bf16[32,2048]{1,0:T(8,128)(2,1)}, bf16[32,2048]{1,0:T(8,128)(2,1)S(1)}, u32[]{:S(2)}, u32[]{:S(2)}) collective-permute-start(bf16[32,2048]{1,0:T(8,128)(2,1)} %bitcast.3), channel_id=1, source_target_pairs={{0,2},{1,3},{2,0},{3,1},{4,6},{5,7},{6,4},{7,5},{8,10},{9,11},{10,... | collective-permute-start | bytes 393224 | tf_op jit(solution)/shard_map/ppermute | solution.py:410
  3.0 6.6 %collective-permute-start.2 = (bf16[32,2048]{1,0:T(8,128)(2,1)}, bf16[32,2048]{1,0:T(8,128)(2,1)S(1)}, u32[]{:S(2)}, u32[]{:S(2)}) collective-permute-start(bf16[32,2048]{1,0:T(8,128)(2,1)} %bitcast.5), channel_id=1, source_target_pairs={{0,2},{1,3},{2,0},{3,1},{4,6},{5,7},{6,4},{7,5},{8,10},{9,11},{10,... | collective-permute-start | bytes 393224 | tf_op jit(solution)/shard_map/ppermute | solution.py:410
  3.0 6.5 %copy-start.2 = (bf16[2048,32]{0,1:T(8,128)(2,1)S(1)}, bf16[2048,32]{0,1:T(8,128)(2,1)}, u32[]{:S(2)}) copy-start(bf16[2048,32]{0,1:T(8,128)(2,1)} %param.9) | copy-start | bytes 393220
  3.0 6.6 %copy-start = (bf16[2048,1280]{1,0:T(8,128)(2,1)S(1)}, bf16[2048,1280]{1,0:T(8,128)(2,1)}, u32[]{:S(2)}) copy-start(bf16[2048,1280]{1,0:T(8,128)(2,1)} %mixer.7) | copy-start | bytes 15728644
  7.6 7.1 %collective-permute-start.1 = (bf16[64,2048]{1,0:T(8,128)(2,1)S(1)}, bf16[64,2048]{1,0:T(8,128)(2,1)S(1)}, u32[]{:S(2)}, u32[]{:S(2)}) collective-permute-start(bf16[64,2048]{1,0:T(8,128)(2,1)S(1)} %join.4.first), channel_id=1, source_target_pairs={{0,1},{1,0},{2,3},{3,2},{4,5},{5,4},{6,7},{7,6},{8,9},{9,8},{10,11... | collective-permute-start | bytes 786440 | tf_op jit(solution)/shard_map/ppermute | solution.py:410
  9.6 2.3 %collective-permute-start.3 = (bf16[64,2048]{1,0:T(8,128)(2,1)S(1)}, bf16[64,2048]{1,0:T(8,128)(2,1)S(1)}, u32[]{:S(2)}, u32[]{:S(2)}) collective-permute-start(bf16[64,2048]{1,0:T(8,128)(2,1)S(1)} %join.6.first), channel_id=1, source_target_pairs={{0,1},{1,0},{2,3},{3,2},{4,5},{5,4},{6,7},{7,6},{8,9},{9,8},{10,11... | collective-permute-start | bytes 786440 | tf_op jit(solution)/shard_map/ppermute | solution.py:410
  12.9 6.9 %collective-permute-start.5 = (bf16[136,640]{1,0:T(8,128)(2,1)S(1)}, bf16[136,640]{1,0:T(8,128)(2,1)S(1)}, u32[]{:S(2)}, u32[]{:S(2)}) collective-permute-start(bf16[136,640]{1,0:T(8,128)(2,1)S(1)} %get-tuple-element.32), channel_id=1, source_target_pairs={{0,4},{4,0},{8,12},{12,8},{16,20},{20,16},{24,28},{28,24},{1,5},{5... | collective-permute-start | bytes 522248 | tf_op jit(solution)/shard_map/ppermute | solution.py:529
  19.9 6.2 %collective-permute-start.6 = (bf16[136,640]{1,0:T(8,128)(2,1)S(1)}, bf16[136,640]{1,0:T(8,128)(2,1)S(1)}, u32[]{:S(2)}, u32[]{:S(2)}) collective-permute-start(bf16[136,640]{1,0:T(8,128)(2,1)S(1)} %get-tuple-element.39.after), channel_id=1, source_target_pairs={{0,8},{4,12},{8,0},{12,4},{16,24},{20,28},{24,16},{28,20},{1,9},{5... | collective-permute-start | bytes 522248 | tf_op jit(solution)/shard_map/ppermute | solution.py:529
  26.2 10.4 %collective-permute-start.8 = (bf16[136,640]{1,0:T(8,128)(2,1)S(1)}, bf16[136,640]{1,0:T(8,128)(2,1)S(1)}, u32[]{:S(2)}, u32[]{:S(2)}) collective-permute-start(bf16[136,640]{1,0:T(8,128)(2,1)S(1)} %merge.3.after), channel_id=1, source_target_pairs={{0,16},{4,20},{8,24},{12,28},{16,0},{20,4},{24,8},{28,12},{1,17},{... | collective-permute-start | bytes 522248 | tf_op jit(solution)/shard_map/ppermute | solution.py:529
  28.9 17.9 %collective-permute-start.4 = (bf16[136,640]{1,0:T(8,128)(2,1)S(1)}, bf16[136,640]{1,0:T(8,128)(2,1)S(1)}, u32[]{:S(2)}, u32[]{:S(2)}) collective-permute-start(bf16[136,640]{1,0:T(8,128)(2,1)S(1)} %get-tuple-element.31), channel_id=1, source_target_pairs={{0,4},{4,0},{8,12},{12,8},{16,20},{20,16},{24,28},{28,24},{1,5},{5... | collective-permute-start | bytes 522248 | tf_op jit(solution)/shard_map/ppermute | solution.py:529
  30.4 16.4 %collective-permute-start.7 = (bf16[136,640]{1,0:T(8,128)(2,1)S(1)}, bf16[136,640]{1,0:T(8,128)(2,1)S(1)}, u32[]{:S(2)}, u32[]{:S(2)}) collective-permute-start(bf16[136,640]{1,0:T(8,128)(2,1)S(1)} %collective-permute-done.6.received.rest_1_), channel_id=1, source_target_pairs={{0,4},{4,0},{8,12},{12,8},{16,20},{20,16},{24,28},{28,24},{1,5},{5... | collective-permute-start | bytes 522248 | tf_op jit(solution)/shard_map/ppermute | solution.py:529
  36.6 11.4 %collective-permute-start.9 = (bf16[136,640]{1,0:T(8,128)(2,1)S(1)}, bf16[136,640]{1,0:T(8,128)(2,1)S(1)}, u32[]{:S(2)}, u32[]{:S(2)}) collective-permute-start(bf16[136,640]{1,0:T(8,128)(2,1)S(1)} %collective-permute-done.8.rest_2_), channel_id=1, source_target_pairs={{0,4},{4,0},{8,12},{12,8},{16,20},{20,16},{24,28},{28,24},{1,5},{5... | collective-permute-start | bytes 522248 | tf_op jit(solution)/shard_map/ppermute | solution.py:529

commit v8 on v7

--- a/solution.py
+++ b/solution.py
@@ -148,27 +148,6 @@
     rows[layout.skip : layout.skip + 8, :] = (dot(low, own) + dot(middle, own)) + dot(high, own)
 
 
-def scale_kernel(heads, padded, layout, mixer, factors, rows, scaled, to_total):
-    tokens, width = mixer.shape
-    wide = spread(0, padded, heads, width)
-
-    def step(a, carry):
-        at = pl.ds(pl.multiple_of(a * HALF, HALF), HALF)
-        row = rows[pl.ds(layout.after + a, 1), :]
-        value = mixer[at, :].astype(F32) * dot(factors[at, :], wide)
-        scaled[at, :] = value.astype(BF16)
-        to_total[at, :] = (value * row).astype(BF16)
-        return carry
-
-    lax.fori_loop(0, tokens // HALF, step, 0, unroll=4)
-
-
-def exp_rows(total, count):
-    where = iota((count, total.shape[1]), 0)
-    high = total.astype(BF16).astype(F32)
-    return jnp.where(where == 0, high, jnp.where(where == 1, total - high, 0.0)).astype(BF16)
-
-
 def own_columns(width):
     rank = lax.axis_index("seq")
     mine = (rank & 1) * (width // 2)
@@ -177,16 +156,40 @@
     return aligned(mine), aligned(other)
 
 
-def state_kernel(layout, to_total, write_t, rows, first, second, mine, mine_exp, whole):
+def scale_kernel(heads, padded, layout, side, mixer, factors, rows, *rest):
+    scaled, to_total, wide = rest[-3:]
+    tokens, width = mixer.shape
+    columns = own_columns(width)[side]
+    wide[...] = spread(0, padded, heads, width)
+
+    def step(a, carry):
+        at = pl.ds(pl.multiple_of(a * HALF, HALF), HALF)
+        row = rows[pl.ds(layout.after + a, 1), columns]
+        value = mixer[at, columns].astype(F32) * dot(factors[at, :], wide[:, columns])
+        scaled[at, columns] = value.astype(BF16)
+        to_total[at, :] = (value * row).astype(BF16)
+        return carry
+
+    lax.fori_loop(0, tokens // HALF, step, 0, unroll=4)
+
+
+def exp_rows(total, count):
+    where = iota((count, total.shape[1]), 0)
+    high = total.astype(BF16).astype(F32)
+    return jnp.where(where == 0, high, jnp.where(where == 1, total - high, 0.0)).astype(BF16)
+
+
+def state_kernel(layout, side, to_total, write_t, rows, payload, *more):
     state = write_t.shape[0]
-    own, other = own_columns(whole.shape[1])
-    whole[...] = dot(write_t[...], to_total[...])
-    for payload, at in ((first, other), (second, own)):
-        payload[0:state, :] = whole[:, at].astype(BF16)
-        total = rows[layout.total : layout.total + 1, at]
-        payload[state:, :] = exp_rows(total, payload.shape[0] - state)
-    mine[...] = whole[:, own]
-    mine_exp[...] = jnp.broadcast_to(rows[layout.total : layout.total + 1, own], mine_exp.shape)
+    columns = own_columns(rows.shape[1])[side]
+    new = dot(write_t[...], to_total[...])
+    payload[0:state, :] = new.astype(BF16)
+    total = rows[pl.ds(layout.total, 1), columns]
+    payload[state:, :] = exp_rows(total, payload.shape[0] - state)
+    if more:
+        mine, mine_exp = more
+        mine[...] = new
+        mine_exp[...] = jnp.broadcast_to(total, mine_exp.shape)
 
 
 def upper_half(bit, width):
@@ -477,28 +480,40 @@
     read_t = gather_columns(read_map.T, "head", rows)
     state = write_t.shape[0]
 
-    scaled, to_total = pl.pallas_call(
-        functools.partial(scale_kernel, heads, padded, layout),
-        in_specs=[VMEM_SPEC] * 3,
-        out_specs=(VMEM_SPEC,) * 2,
-        out_shape=(sds((tokens, width), BF16),) * 2,
-        compiler_params=grant(4),
-        cost_estimate=cost(3_000_000_000, tokens * width * 6),
-        name="scale",
-    )(mixer_input, factors, rows)
-
     half = width // 2
     carried = (sds((state + 8, half), BF16), sds((state, half), F32), sds((8, half), F32))
-    first_out, second_out, mine, mine_exp = pl.pallas_call(
-        functools.partial(state_kernel, layout),
-        in_specs=[VMEM_SPEC] * 3,
-        out_specs=(VMEM_SPEC,) * 4,
-        out_shape=carried[:1] + carried,
-        scratch_shapes=[pltpu.VMEM((state, width), F32)],
-        compiler_params=grant(4),
-        cost_estimate=cost(2 * tokens * width * state, tokens * width * 2),
-        name="state",
-    )(to_total, write_t, rows)
+
+    def front(side, scaled):
+        operands = [mixer_input, factors, rows]
+        aliases = {}
+        if scaled is not None:
+            aliases = {len(operands): 0}
+            operands.append(scaled)
+        scaled, to_total = pl.pallas_call(
+            functools.partial(scale_kernel, heads, padded, layout, side),
+            in_specs=[VMEM_SPEC] * len(operands),
+            out_specs=(VMEM_SPEC,) * 2,
+            out_shape=(sds((tokens, width), BF16), sds((tokens, half), BF16)),
+            input_output_aliases=aliases,
+            scratch_shapes=[pltpu.VMEM((LANES, width), BF16)],
+            compiler_params=grant(4),
+            cost_estimate=cost(1_500_000_000, tokens * width * 3),
+            name="scale",
+        )(*operands)
+        shapes = carried if side == 0 else carried[:1]
+        results = pl.pallas_call(
+            functools.partial(state_kernel, layout, side),
+            in_specs=[VMEM_SPEC] * 3,
+            out_specs=(VMEM_SPEC,) * len(shapes),
+            out_shape=shapes,
+            compiler_params=grant(4),
+            cost_estimate=cost(tokens * width * state, tokens * width),
+            name="state",
+        )(to_total, write_t, rows)
+        return scaled, results
+
+    scaled, (first_out,) = front(1, None)
+    scaled, (second_out, mine, mine_exp) = front(0, scaled)
 
     def local(first, count, slots, after):
         return pl.pallas_call(

time: 50.2 us -> 50.7 us (level)
  Pallas kernels: 25.3 us -> 26.3 us
  waiting for transfers between devices: 11.5 us -> 10.9 us
    pallas_call x2 -> x4, Pallas kernels: 3.21 us -> 4.07 us  [the longest x2 2.88 us: front(): pl.pallas_call(functools.partial(scale_kernel, heads, padded, layout, sid...]
    ppermute x6, waiting for transfers between devices: 8.15 us -> 7.5 us  [swap(): return lax.ppermute(value, 'seq', [(i, i ^ 1 << bit) for i in range(ranks)])]
  transfers between devices with their start and end apart: 10 -> 10, of which waited for: 4 -> 4; matrix products, arithmetic and copies ran while one was open for 0% -> 0% of each run, Pallas kernels for 46% -> 48%
where the time goes in v8:
time: 50.7 us; the launch traced here: 50.5 us
  Pallas kernels  26.3 us (52%)
  starting transfers between devices  13 us (26%)
  waiting for transfers between devices  10.9 us (21%)
    pallas_call x3, Pallas kernels, local(): pl.pallas_call(functools.partial(local_kernel, heads, padded, local_bits,...  13.2 us
    ppermute x6, starting transfers between devices, swap(): return lax.ppermute(value, 'seq', [(i, i ^ 1 << bit) for i in range(ranks)])  9.81 us
    ppermute x6, waiting for transfers between devices, swap(): return lax.ppermute(value, 'seq', [(i, i ^ 1 << bit) for i in range(ranks)])  7.5 us
    pallas_call x2, Pallas kernels, finish(): pl.pallas_call(functools.partial(final_kernel, starts, local_bits, device...  4.59 us
    ppermute x4, waiting for transfers between devices, gather_columns(): other = lax.ppermute(pieces, axis, [(i, i ^ stride) for i in range(size)])  3.38 us
    ppermute x4, starting transfers between devices, gather_columns(): other = lax.ppermute(pieces, axis, [(i, i ^ stride) for i in range(size)])  3.17 us
    pallas_call x1, Pallas kernels, on_device(): pl.pallas_call(functools.partial(prep_kernel, heads, padded, layout), in_...  3.03 us
    pallas_call x2, Pallas kernels, front(): pl.pallas_call(functools.partial(scale_kernel, heads, padded, layout, sid...  2.88 us
  transfers between devices with their start and end apart: 10, of which 4 were waited for; matrix products, arithmetic and copies ran while one was open for 0% of the time, Pallas kernels for 48%

profile of v8, /device:TPU:0, one launch (start us, length us, event | category | flops | bytes accessed | tf_op | source)
XLA Modules:
  0.0 50.5 jit_solution(4432533820039651659)
XLA Ops:
  0.0 3.0 %collective-permute-start = (bf16[32,2048]{1,0:T(8,128)(2,1)}, bf16[32,2048]{1,0:T(8,128)(2,1)S(1)}, u32[]{:S(2)}, u32[]{:S(2)}) collective-permute-start(bf16[32,2048]{1,0:T(8,128)(2,1)} %bitcast.3), channel_id=1, source_target_pairs={{0,2},{1,3},{2,0},{3,1},{4,6},{5,7},{6,4},{7,5},{8,10},{9,11},{10,... | collective-permute-start | bytes 393224 | tf_op jit(solution)/shard_map/ppermute | solution.py:413
  3.0 0.1 collective-permute-start.2
  3.0 3.0 %prep.1 = (bf16[2048,128]{1,0:T(8,128)(2,1)S(1)}, f32[2048,128]{1,0:T(8,128)S(1)}, f32[32,2048]{1,0:T(8,128)S(1)}, f32[7,2048]{1,0:T(8,128)S(1)}, f32[80,1280]{1,0:T(8,128)S(1)}) custom-call(f32[20,2048]{1,0:T(8,128)} %log_decay_far.1, f32[20,2048]{1,0:T(8,128)} %step_size_far.1, s32[7,2048]{1,0:T(8,128)} %level_index_far.1, f32[7,8]{1,0:T(8,128)} %level_table_far.1, ...), custom_call_target="tpu_custom_call" | custom-call | flops 2000000000 | bytes 4000000 | tf_op jit(solution)/shard_map/prep/pallas_call | solution.py:450
  6.1 1.5 %collective-permute-done.second = bf16[32,2048]{1,0:T(8,128)(2,1)S(1)} collective-permute-done((bf16[32,2048]{1,0:T(8,128)(2,1)}, bf16[32,2048]{1,0:T(8,128)(2,1)S(1)}, u32[]{:S(2)}, u32[]{:S(2)}) %collective-permute-start) | collective-permute-done | bytes 131104 | tf_op jit(solution)/shard_map/ppermute | solution.py:413
  7.6 0.1 collective-permute-start.1
  7.7 1.9 %collective-permute-done.2.second = bf16[32,2048]{1,0:T(8,128)(2,1)S(1)} collective-permute-done((bf16[32,2048]{1,0:T(8,128)(2,1)}, bf16[32,2048]{1,0:T(8,128)(2,1)S(1)}, u32[]{:S(2)}, u32[]{:S(2)}) %collective-permute-start.2) | collective-permute-done | bytes 131104 | tf_op jit(solution)/shard_map/ppermute | solution.py:413
  9.6 0.1 collective-permute-start.3
  9.7 1.4 %scale.2 = (bf16[2048,1280]{1,0:T(8,128)(2,1)S(1)}, bf16[2048,640]{1,0:T(8,128)(2,1)S(1)}) custom-call(bf16[2048,1280]{1,0:T(8,128)(2,1)S(1)} %copy-done, bf16[2048,128]{1,0:T(8,128)(2,1)S(1)} %get-tuple-element.30.factors, f32[80,1280]{1,0:T(8,128)S(1)} %get-tuple-element.28.rest_0_.rows.after), custom_call_target="tpu_custom_call" | custom-call | flops 1500000000 | bytes 7864320 | tf_op jit(solution)/shard_map/scale/pallas_call | solution.py:492
  11.1 1.4 %scale.3 = (bf16[2048,1280]{1,0:T(8,128)(2,1)S(1)}, bf16[2048,640]{1,0:T(8,128)(2,1)S(1)}) custom-call(bf16[2048,1280]{1,0:T(8,128)(2,1)S(1)} %copy-done, bf16[2048,128]{1,0:T(8,128)(2,1)S(1)} %get-tuple-element.30.factors, f32[80,1280]{1,0:T(8,128)S(1)} %get-tuple-element.28.rest_0_.rows.after, ...), custom_call_target="tpu_custom_call", output_to_operand_aliasing={{0}: (3, {})} | custom-call | flops 1500000000 | bytes 7864320 | tf_op jit(solution)/shard_map/scale/pallas_call | solution.py:492
  12.6 0.0 collective-permute-done.3.second
  12.6 0.6 %state.3 = bf16[136,640]{1,0:T(8,128)(2,1)S(1)} custom-call(bf16[2048,640]{1,0:T(8,128)(2,1)S(1)} %get-tuple-element.34.to_total, bf16[128,2048]{1,0:T(8,128)(2,1)S(1)} %join.7.write_t, f32[80,1280]{1,0:T(8,128)S(1)} %get-tuple-element.28.rest_0_.rows.after), custom_call_target="tpu_custom_call" | custom-call | flops 335544320 | bytes 2621440 | tf_op jit(solution)/shard_map/state/pallas_call | solution.py:504
  13.2 1.8 %collective-permute-start.5 = (bf16[136,640]{1,0:T(8,128)(2,1)S(1)}, bf16[136,640]{1,0:T(8,128)(2,1)S(1)}, u32[]{:S(2)}, u32[]{:S(2)}) collective-permute-start(bf16[136,640]{1,0:T(8,128)(2,1)S(1)} %state.3), channel_id=1, source_target_pairs={{0,4},{4,0},{8,12},{12,8},{16,20},{20,16},{24,28},{28,24},{1,5},{5... | collective-permute-start | bytes 522248 | tf_op jit(solution)/shard_map/ppermute | solution.py:544
  15.0 0.6 %state.2 = (bf16[136,640]{1,0:T(8,128)(2,1)S(1)}, f32[128,640]{1,0:T(8,128)S(1)}, f32[8,640]{1,0:T(8,128)S(1)}) custom-call(bf16[2048,640]{1,0:T(8,128)(2,1)S(1)} %get-tuple-element.32.to_total, bf16[128,2048]{1,0:T(8,128)(2,1)S(1)} %join.7.write_t, f32[80,1280]{1,0:T(8,128)S(1)} %get-tuple-element.28.rest_0_.rows.after), custom_call_target="tpu_custom_call" | custom-call | flops 335544320 | bytes 2621440 | tf_op jit(solution)/shard_map/state/pallas_call | solution.py:504
  15.6 0.0 collective-permute-done.1.second
  15.6 2.6 %local.3 = (f32[512,1280]{1,0:T(8,128)S(1)}, f32[512,1280]{1,0:T(8,128)S(1)}, f32[3,128,1280]{2,1,0:T(8,128)S(1)}) custom-call(bf16[2048,1280]{1,0:T(8,128)(2,1)S(1)} %copy-done, bf16[2048,1280]{1,0:T(8,128)(2,1)S(1)} %get-tuple-element.37.scaled, bf16[128,2048]{1,0:T(8,128)(2,1)S(1)} %join.7.write_t, bf16[128,2048]{1,0:T(8,128)(2,1)S(1)} %join.5.read_t, ...), custom_call_target="tpu_custom_call" | custom-call | flops 2621440000 | bytes 5242880 | tf_op jit(solution)/shard_map/local/pallas_call | solution.py:519
  18.3 1.8 %collective-permute-done.5.received.rest_0_ = bf16[136,640]{1,0:T(8,128)(2,1)S(1)} collective-permute-done((bf16[136,640]{1,0:T(8,128)(2,1)S(1)}, bf16[136,640]{1,0:T(8,128)(2,1)S(1)}, u32[]{:S(2)}, u32[]{:S(2)}) %collective-permute-start.5) | collective-permute-done | bytes 174112 | tf_op jit(solution)/shard_map/ppermute | solution.py:544
  20.1 0.1 merge.2
  20.2 1.8 %collective-permute-start.6 = (bf16[136,640]{1,0:T(8,128)(2,1)S(1)}, bf16[136,640]{1,0:T(8,128)(2,1)S(1)}, u32[]{:S(2)}, u32[]{:S(2)}) collective-permute-start(bf16[136,640]{1,0:T(8,128)(2,1)S(1)} %get-tuple-element.41.after), channel_id=1, source_target_pairs={{0,8},{4,12},{8,0},{12,4},{16,24},{20,28},{24,16},{28,20},{1,9},{5... | collective-permute-start | bytes 522248 | tf_op jit(solution)/shard_map/ppermute | solution.py:544
  22.0 4.5 %local.4 = (f32[768,1280]{1,0:T(8,128)S(1)}, f32[768,1280]{1,0:T(8,128)S(1)}, f32[3,128,1280]{2,1,0:T(8,128)S(1)}) custom-call(bf16[2048,1280]{1,0:T(8,128)(2,1)S(1)} %copy-done, bf16[2048,1280]{1,0:T(8,128)(2,1)S(1)} %get-tuple-element.37.scaled, bf16[128,2048]{1,0:T(8,128)(2,1)S(1)} %join.7.write_t, bf16[128,2048]{1,0:T(8,128)(2,1)S(1)} %join.5.read_t, ...), custom_call_target="tpu_custom_call" | custom-call | flops 3932160000 | bytes 7864320 | tf_op jit(solution)/shard_map/local/pallas_call | solution.py:519
  26.5 0.0 collective-permute-done.6.received.rest_1_
  26.5 0.1 merge.3.after
  26.6 2.7 %collective-permute-start.8 = (bf16[136,640]{1,0:T(8,128)(2,1)S(1)}, bf16[136,640]{1,0:T(8,128)(2,1)S(1)}, u32[]{:S(2)}, u32[]{:S(2)}) collective-permute-start(bf16[136,640]{1,0:T(8,128)(2,1)S(1)} %merge.3.after), channel_id=1, source_target_pairs={{0,16},{4,20},{8,24},{12,28},{16,0},{20,4},{24,8},{28,12},{1,17},{... | collective-permute-start | bytes 522248 | tf_op jit(solution)/shard_map/ppermute | solution.py:544
  29.2 1.5 %collective-permute-start.4 = (bf16[136,640]{1,0:T(8,128)(2,1)S(1)}, bf16[136,640]{1,0:T(8,128)(2,1)S(1)}, u32[]{:S(2)}, u32[]{:S(2)}) collective-permute-start(bf16[136,640]{1,0:T(8,128)(2,1)S(1)} %get-tuple-element.33), channel_id=1, source_target_pairs={{0,4},{4,0},{8,12},{12,8},{16,20},{20,16},{24,28},{28,24},{1,5},{5... | collective-permute-start | bytes 522248 | tf_op jit(solution)/shard_map/ppermute | solution.py:544
  30.7 0.5 %collective-permute-start.7 = (bf16[136,640]{1,0:T(8,128)(2,1)S(1)}, bf16[136,640]{1,0:T(8,128)(2,1)S(1)}, u32[]{:S(2)}, u32[]{:S(2)}) collective-permute-start(bf16[136,640]{1,0:T(8,128)(2,1)S(1)} %collective-permute-done.6.received.rest_1_), channel_id=1, source_target_pairs={{0,4},{4,0},{8,12},{12,8},{16,20},{20,16},{24,28},{28,24},{1,5},{5... | collective-permute-start | bytes 522248 | tf_op jit(solution)/shard_map/ppermute | solution.py:544
  31.2 5.7 %collective-permute-done.8.rest_2_ = bf16[136,640]{1,0:T(8,128)(2,1)S(1)} collective-permute-done((bf16[136,640]{1,0:T(8,128)(2,1)S(1)}, bf16[136,640]{1,0:T(8,128)(2,1)S(1)}, u32[]{:S(2)}, u32[]{:S(2)}) %collective-permute-start.8) | collective-permute-done | bytes 174112 | tf_op jit(solution)/shard_map/ppermute | solution.py:544
  36.9 1.5 %collective-permute-start.9 = (bf16[136,640]{1,0:T(8,128)(2,1)S(1)}, bf16[136,640]{1,0:T(8,128)(2,1)S(1)}, u32[]{:S(2)}, u32[]{:S(2)}) collective-permute-start(bf16[136,640]{1,0:T(8,128)(2,1)S(1)} %collective-permute-done.8.rest_2_), channel_id=1, source_target_pairs={{0,4},{4,0},{8,12},{12,8},{16,20},{20,16},{24,28},{28,24},{1,5},{5... | collective-permute-start | bytes 522248 | tf_op jit(solution)/shard_map/ppermute | solution.py:544
  38.5 6.1 %local.5 = (f32[768,1280]{1,0:T(8,128)S(1)}, f32[768,1280]{1,0:T(8,128)S(1)}, f32[3,128,1280]{2,1,0:T(8,128)}) custom-call(bf16[2048,1280]{1,0:T(8,128)(2,1)S(1)} %copy-done, bf16[2048,1280]{1,0:T(8,128)(2,1)S(1)} %get-tuple-element.37.scaled, bf16[128,2048]{1,0:T(8,128)(2,1)S(1)} %join.7.write_t, bf16[128,2048]{1,0:T(8,128)(2,1)S(1)} %join.5.read_t, ...), custom_call_target="tpu_custom_call" | custom-call | flops 3932160000 | bytes 7864320 | tf_op jit(solution)/shard_map/local/pallas_call | solution.py:519
  44.6 2.7 %final.2.rest_7_ = bf16[2048,1280]{1,0:T(8,128)(2,1)} custom-call(bf16[128,2048]{1,0:T(8,128)(2,1)S(1)} %join.5.read_t, f32[7,2048]{1,0:T(8,128)S(1)} %get-tuple-element.29.weight_h, bf16[136,640]{1,0:T(8,128)(2,1)S(1)} %collective-permute-done.5.received.rest_0_, bf16[136,640]{1,0:T(8,128)(2,1)S(1)} %collective-permute-done.6.received.rest_1_, ...), custom_call_target="tpu_custom_call" | custom-call | flops 335544320 | bytes 7864320 | tf_op jit(solution)/shard_map/final/pallas_call | solution.py:593
  47.2 0.0 collective-permute-done.4.rest_0_
  47.2 0.0 collective-permute-done.7.rest_1_
  47.3 1.2 %near.1.rest_3_ = f32[2048,640]{1,0:T(8,128)S(1)} custom-call(bf16[128,2048]{1,0:T(8,128)(2,1)S(1)} %join.5.read_t, f32[7,2048]{1,0:T(8,128)S(1)} %get-tuple-element.29.weight_h, bf16[136,640]{1,0:T(8,128)(2,1)S(1)} %collective-permute-done.4.rest_0_, bf16[136,640]{1,0:T(8,128)(2,1)S(1)} %collective-permute-done.7.rest_1_, ...), custom_call_target="tpu_custom_call" | custom-call | flops 671088640 | bytes 7864320 | tf_op jit(solution)/shard_map/near/pallas_call | solution.py:611
  48.5 1.9 %final.3 = bf16[2048,1280]{1,0:T(8,128)(2,1)} custom-call(bf16[128,2048]{1,0:T(8,128)(2,1)S(1)} %join.5.read_t, f32[7,2048]{1,0:T(8,128)S(1)} %get-tuple-element.29.weight_h, bf16[136,640]{1,0:T(8,128)(2,1)S(1)} %collective-permute-done.4.rest_0_, bf16[136,640]{1,0:T(8,128)(2,1)S(1)} %collective-permute-done.7.rest_1_, ...), custom_call_target="tpu_custom_call", output_to_operand_aliasing={{}: (9, {})} | custom-call | flops 335544320 | bytes 7864320 | tf_op jit(solution)/shard_map/final/pallas_call | solution.py:593
  (12 shorter events, 0.1 us)
Async XLA Ops:
  0.0 7.6 %copy-start.1 = (bf16[2048,32]{0,1:T(8,128)(2,1)S(1)}, bf16[2048,32]{0,1:T(8,128)(2,1)}, u32[]{:S(2)}) copy-start(bf16[2048,32]{0,1:T(8,128)(2,1)} %param.10) | copy-start | bytes 393220
  0.0 7.6 %collective-permute-start = (bf16[32,2048]{1,0:T(8,128)(2,1)}, bf16[32,2048]{1,0:T(8,128)(2,1)S(1)}, u32[]{:S(2)}, u32[]{:S(2)}) collective-permute-start(bf16[32,2048]{1,0:T(8,128)(2,1)} %bitcast.3), channel_id=1, source_target_pairs={{0,2},{1,3},{2,0},{3,1},{4,6},{5,7},{6,4},{7,5},{8,10},{9,11},{10,... | collective-permute-start | bytes 393224 | tf_op jit(solution)/shard_map/ppermute | solution.py:413
  3.0 6.6 %collective-permute-start.2 = (bf16[32,2048]{1,0:T(8,128)(2,1)}, bf16[32,2048]{1,0:T(8,128)(2,1)S(1)}, u32[]{:S(2)}, u32[]{:S(2)}) collective-permute-start(bf16[32,2048]{1,0:T(8,128)(2,1)} %bitcast.5), channel_id=1, source_target_pairs={{0,2},{1,3},{2,0},{3,1},{4,6},{5,7},{6,4},{7,5},{8,10},{9,11},{10,... | collective-permute-start | bytes 393224 | tf_op jit(solution)/shard_map/ppermute | solution.py:413
  3.0 6.5 %copy-start.2 = (bf16[2048,32]{0,1:T(8,128)(2,1)S(1)}, bf16[2048,32]{0,1:T(8,128)(2,1)}, u32[]{:S(2)}) copy-start(bf16[2048,32]{0,1:T(8,128)(2,1)} %param.9) | copy-start | bytes 393220
  3.0 6.6 %copy-start = (bf16[2048,1280]{1,0:T(8,128)(2,1)S(1)}, bf16[2048,1280]{1,0:T(8,128)(2,1)}, u32[]{:S(2)}) copy-start(bf16[2048,1280]{1,0:T(8,128)(2,1)} %mixer.9) | copy-start | bytes 15728644
  7.6 8.0 %collective-permute-start.1 = (bf16[64,2048]{1,0:T(8,128)(2,1)S(1)}, bf16[64,2048]{1,0:T(8,128)(2,1)S(1)}, u32[]{:S(2)}, u32[]{:S(2)}) collective-permute-start(bf16[64,2048]{1,0:T(8,128)(2,1)S(1)} %join.4.first), channel_id=1, source_target_pairs={{0,1},{1,0},{2,3},{3,2},{4,5},{5,4},{6,7},{7,6},{8,9},{9,8},{10,11... | collective-permute-start | bytes 786440 | tf_op jit(solution)/shard_map/ppermute | solution.py:413
  9.6 3.0 %collective-permute-start.3 = (bf16[64,2048]{1,0:T(8,128)(2,1)S(1)}, bf16[64,2048]{1,0:T(8,128)(2,1)S(1)}, u32[]{:S(2)}, u32[]{:S(2)}) collective-permute-start(bf16[64,2048]{1,0:T(8,128)(2,1)S(1)} %join.6.first), channel_id=1, source_target_pairs={{0,1},{1,0},{2,3},{3,2},{4,5},{5,4},{6,7},{7,6},{8,9},{9,8},{10,11... | collective-permute-start | bytes 786440 | tf_op jit(solution)/shard_map/ppermute | solution.py:413
  13.2 6.9 %collective-permute-start.5 = (bf16[136,640]{1,0:T(8,128)(2,1)S(1)}, bf16[136,640]{1,0:T(8,128)(2,1)S(1)}, u32[]{:S(2)}, u32[]{:S(2)}) collective-permute-start(bf16[136,640]{1,0:T(8,128)(2,1)S(1)} %state.3), channel_id=1, source_target_pairs={{0,4},{4,0},{8,12},{12,8},{16,20},{20,16},{24,28},{28,24},{1,5},{5... | collective-permute-start | bytes 522248 | tf_op jit(solution)/shard_map/ppermute | solution.py:544
  20.2 6.3 %collective-permute-start.6 = (bf16[136,640]{1,0:T(8,128)(2,1)S(1)}, bf16[136,640]{1,0:T(8,128)(2,1)S(1)}, u32[]{:S(2)}, u32[]{:S(2)}) collective-permute-start(bf16[136,640]{1,0:T(8,128)(2,1)S(1)} %get-tuple-element.41.after), channel_id=1, source_target_pairs={{0,8},{4,12},{8,0},{12,4},{16,24},{20,28},{24,16},{28,20},{1,9},{5... | collective-permute-start | bytes 522248 | tf_op jit(solution)/shard_map/ppermute | solution.py:544
  26.6 10.4 %collective-permute-start.8 = (bf16[136,640]{1,0:T(8,128)(2,1)S(1)}, bf16[136,640]{1,0:T(8,128)(2,1)S(1)}, u32[]{:S(2)}, u32[]{:S(2)}) collective-permute-start(bf16[136,640]{1,0:T(8,128)(2,1)S(1)} %merge.3.after), channel_id=1, source_target_pairs={{0,16},{4,20},{8,24},{12,28},{16,0},{20,4},{24,8},{28,12},{1,17},{... | collective-permute-start | bytes 522248 | tf_op jit(solution)/shard_map/ppermute | solution.py:544
  29.2 18.0 %collective-permute-start.4 = (bf16[136,640]{1,0:T(8,128)(2,1)S(1)}, bf16[136,640]{1,0:T(8,128)(2,1)S(1)}, u32[]{:S(2)}, u32[]{:S(2)}) collective-permute-start(bf16[136,640]{1,0:T(8,128)(2,1)S(1)} %get-tuple-element.33), channel_id=1, source_target_pairs={{0,4},{4,0},{8,12},{12,8},{16,20},{20,16},{24,28},{28,24},{1,5},{5... | collective-permute-start | bytes 522248 | tf_op jit(solution)/shard_map/ppermute | solution.py:544
  30.7 16.5 %collective-permute-start.7 = (bf16[136,640]{1,0:T(8,128)(2,1)S(1)}, bf16[136,640]{1,0:T(8,128)(2,1)S(1)}, u32[]{:S(2)}, u32[]{:S(2)}) collective-permute-start(bf16[136,640]{1,0:T(8,128)(2,1)S(1)} %collective-permute-done.6.received.rest_1_), channel_id=1, source_target_pairs={{0,4},{4,0},{8,12},{12,8},{16,20},{20,16},{24,28},{28,24},{1,5},{5... | collective-permute-start | bytes 522248 | tf_op jit(solution)/shard_map/ppermute | solution.py:544
  36.9 11.5 %collective-permute-start.9 = (bf16[136,640]{1,0:T(8,128)(2,1)S(1)}, bf16[136,640]{1,0:T(8,128)(2,1)S(1)}, u32[]{:S(2)}, u32[]{:S(2)}) collective-permute-start(bf16[136,640]{1,0:T(8,128)(2,1)S(1)} %collective-permute-done.8.rest_2_), channel_id=1, source_target_pairs={{0,4},{4,0},{8,12},{12,8},{16,20},{20,16},{24,28},{28,24},{1,5},{5... | collective-permute-start | bytes 522248 | tf_op jit(solution)/shard_map/ppermute | solution.py:544

commit v9 on v8

--- a/solution.py
+++ b/solution.py
@@ -347,9 +347,15 @@
     return jnp.concatenate(queries, 0) if len(queries) > 1 else queries[0]
 
 
+def views(received):
+    first = received[0]
+    count = first.shape[0] // 2
+    return [first.at[pl.ds(0, count), :], first.at[pl.ds(count, count), :]] + list(received[1:])
+
+
 def near_kernel(starts, local_bits, bits, read_t, weight_h, *rest):
     pieces = len(starts) - 1
-    received, rest = rest[:bits], rest[bits:]
+    received, rest = views(rest[: bits - 1]), rest[bits - 1 :]
     bases, reaches, rest = rest[:pieces], rest[pieces : 2 * pieces], rest[2 * pieces :]
     out, buckets = rest
     columns = own_columns(bases[0].shape[1])[1]
@@ -369,12 +375,12 @@
 
 def final_kernel(starts, local_bits, bits, wanted, side, read_t, weight_h, *rest):
     pieces = len(starts) - 1
-    received, rest = rest[:bits], rest[bits:]
     near = None
     if side:
-        near, rest = rest[0], rest[1:]
+        received, near, rest = views(rest[: bits - 1]), rest[bits - 1], rest[bits:]
         reaches = rest[:pieces]
     else:
+        received, rest = rest[:bits], rest[bits:]
         bases, reaches = rest[:pieces], rest[pieces : 2 * pieces]
     out, buckets, ready, sems = rest[-4:]
     columns = own_columns(out.shape[1])[side]
@@ -552,7 +558,7 @@
     slots = jnp.zeros((local_bits, 8, LANES), F32)
     bases, reaches = [], []
     own_parts = [swap(first_out, 0)]
-    other_parts = [swap(second_out, 0)]
+    other_parts = []
     after = rows
     payload = None
     for bit in range(device_bits):
@@ -576,7 +582,18 @@
                 mine, mine_exp = more
             after = payload
             own_parts.append(swap(payload, bit + 1))
-            if bit > 0:
+            if bit == 1:
+                both = pl.pallas_call(
+                    join_kernel,
+                    in_specs=[VMEM_SPEC] * 2,
+                    out_specs=VMEM_SPEC,
+                    out_shape=sds((2 * payload.shape[0], half), BF16),
+                    compiler_params=grant(2),
+                    cost_estimate=cost(0, 8 * payload.size),
+                    name="both",
+                )(second_out, own_parts[1])
+                other_parts.append(swap(both, 0))
+            elif bit > 1:
                 other_parts.append(swap(own_parts[bit], 0))
     starts = sorted(set(starts))
 
@@ -610,7 +627,7 @@
     near_bits = device_bits - 1
     near = pl.pallas_call(
         functools.partial(near_kernel, starts, local_bits, near_bits),
-        in_specs=[VMEM_SPEC] * (2 + near_bits + 2 * len(bases)),
+        in_specs=[VMEM_SPEC] * (2 + near_bits - 1 + 2 * len(bases)),
         out_specs=VMEM_SPEC,
         out_shape=sds((tokens, half), F32),
         scratch_shapes=[pltpu.VMEM((near_bits * state, half), BF16)],

time: 50.7 us -> 50.8 us (level)
    ppermute x6 -> x5, starting transfers between devices: 9.81 us -> 9.38 us  [swap(): return lax.ppermute(value, 'seq', [(i, i ^ 1 << bit) for i in range(ranks)])]
    ppermute x6 -> x5, waiting for transfers between devices: 7.5 us -> 7.91 us  [swap(): return lax.ppermute(value, 'seq', [(i, i ^ 1 << bit) for i in range(ranks)])]
  transfers between devices with their start and end apart: 10 -> 9, of which waited for: 4 -> 4; matrix products, arithmetic and copies ran while one was open for 0% -> 0% of each run, Pallas kernels for 48% -> 48%
where the time goes in v9:
time: 50.8 us; the launch traced here: 50.6 us
  Pallas kernels  26.5 us (52%)
  starting transfers between devices  12.5 us (25%)
  waiting for transfers between devices  11.3 us (22%)
    pallas_call x3, Pallas kernels, local(): pl.pallas_call(functools.partial(local_kernel, heads, padded, local_bits,...  13.2 us
    ppermute x5, starting transfers between devices, swap(): return lax.ppermute(value, 'seq', [(i, i ^ 1 << bit) for i in range(ranks)])  9.38 us
    ppermute x5, waiting for transfers between devices, swap(): return lax.ppermute(value, 'seq', [(i, i ^ 1 << bit) for i in range(ranks)])  7.91 us
    pallas_call x2, Pallas kernels, finish(): pl.pallas_call(functools.partial(final_kernel, starts, local_bits, device...  4.61 us
    ppermute x4, waiting for transfers between devices, gather_columns(): other = lax.ppermute(pieces, axis, [(i, i ^ stride) for i in range(size)])  3.38 us
    ppermute x4, starting transfers between devices, gather_columns(): other = lax.ppermute(pieces, axis, [(i, i ^ stride) for i in range(size)])  3.17 us
    pallas_call x1, Pallas kernels, on_device(): pl.pallas_call(functools.partial(prep_kernel, heads, padded, layout), in_...  3.03 us
    pallas_call x2, Pallas kernels, front(): pl.pallas_call(functools.partial(scale_kernel, heads, padded, layout, sid...  2.88 us
  transfers between devices with their start and end apart: 9, of which 4 were waited for; matrix products, arithmetic and copies ran while one was open for 0% of the time, Pallas kernels for 48%

profile of v9, /device:TPU:0, one launch (start us, length us, event | category | flops | bytes accessed | tf_op | source)
XLA Modules:
  0.0 50.6 jit_solution(3736048556238844385)
XLA Ops:
  0.0 3.0 %collective-permute-start = (bf16[32,2048]{1,0:T(8,128)(2,1)}, bf16[32,2048]{1,0:T(8,128)(2,1)S(1)}, u32[]{:S(2)}, u32[]{:S(2)}) collective-permute-start(bf16[32,2048]{1,0:T(8,128)(2,1)} %bitcast.3), channel_id=1, source_target_pairs={{0,2},{1,3},{2,0},{3,1},{4,6},{5,7},{6,4},{7,5},{8,10},{9,11},{10,... | collective-permute-start | bytes 393224 | tf_op jit(solution)/shard_map/ppermute | solution.py:419
  3.0 0.1 collective-permute-start.2
  3.0 3.0 %prep.1 = (bf16[2048,128]{1,0:T(8,128)(2,1)S(1)}, f32[2048,128]{1,0:T(8,128)S(1)}, f32[32,2048]{1,0:T(8,128)S(1)}, f32[7,2048]{1,0:T(8,128)S(1)}, f32[80,1280]{1,0:T(8,128)S(1)}) custom-call(f32[20,2048]{1,0:T(8,128)} %log_decay_far.1, f32[20,2048]{1,0:T(8,128)} %step_size_far.1, s32[7,2048]{1,0:T(8,128)} %level_index_far.1, f32[7,8]{1,0:T(8,128)} %level_table_far.1, ...), custom_call_target="tpu_custom_call" | custom-call | flops 2000000000 | bytes 4000000 | tf_op jit(solution)/shard_map/prep/pallas_call | solution.py:456
  6.1 1.5 %collective-permute-done.second = bf16[32,2048]{1,0:T(8,128)(2,1)S(1)} collective-permute-done((bf16[32,2048]{1,0:T(8,128)(2,1)}, bf16[32,2048]{1,0:T(8,128)(2,1)S(1)}, u32[]{:S(2)}, u32[]{:S(2)}) %collective-permute-start) | collective-permute-done | bytes 131104 | tf_op jit(solution)/shard_map/ppermute | solution.py:419
  7.6 0.0 copy-done.1
  7.6 0.1 collective-permute-start.1
  7.7 1.9 %collective-permute-done.2.second = bf16[32,2048]{1,0:T(8,128)(2,1)S(1)} collective-permute-done((bf16[32,2048]{1,0:T(8,128)(2,1)}, bf16[32,2048]{1,0:T(8,128)(2,1)S(1)}, u32[]{:S(2)}, u32[]{:S(2)}) %collective-permute-start.2) | collective-permute-done | bytes 131104 | tf_op jit(solution)/shard_map/ppermute | solution.py:419
  9.6 0.1 collective-permute-start.3
  9.7 1.4 %scale.2 = (bf16[2048,1280]{1,0:T(8,128)(2,1)S(1)}, bf16[2048,640]{1,0:T(8,128)(2,1)S(1)}) custom-call(bf16[2048,1280]{1,0:T(8,128)(2,1)S(1)} %copy-done, bf16[2048,128]{1,0:T(8,128)(2,1)S(1)} %get-tuple-element.30.factors, f32[80,1280]{1,0:T(8,128)S(1)} %get-tuple-element.28.rest_0_.rows.after), custom_call_target="tpu_custom_call" | custom-call | flops 1500000000 | bytes 7864320 | tf_op jit(solution)/shard_map/scale/pallas_call | solution.py:498
  11.1 1.4 %scale.3 = (bf16[2048,1280]{1,0:T(8,128)(2,1)S(1)}, bf16[2048,640]{1,0:T(8,128)(2,1)S(1)}) custom-call(bf16[2048,1280]{1,0:T(8,128)(2,1)S(1)} %copy-done, bf16[2048,128]{1,0:T(8,128)(2,1)S(1)} %get-tuple-element.30.factors, f32[80,1280]{1,0:T(8,128)S(1)} %get-tuple-element.28.rest_0_.rows.after, ...), custom_call_target="tpu_custom_call", output_to_operand_aliasing={{0}: (3, {})} | custom-call | flops 1500000000 | bytes 7864320 | tf_op jit(solution)/shard_map/scale/pallas_call | solution.py:498
  12.6 0.0 collective-permute-done.3.second
  12.6 0.6 %state.3 = bf16[136,640]{1,0:T(8,128)(2,1)S(1)} custom-call(bf16[2048,640]{1,0:T(8,128)(2,1)S(1)} %get-tuple-element.34.to_total, bf16[128,2048]{1,0:T(8,128)(2,1)S(1)} %join.7.write_t, f32[80,1280]{1,0:T(8,128)S(1)} %get-tuple-element.28.rest_0_.rows.after), custom_call_target="tpu_custom_call" | custom-call | flops 335544320 | bytes 2621440 | tf_op jit(solution)/shard_map/state/pallas_call | solution.py:510
  13.2 1.8 %collective-permute-start.4 = (bf16[136,640]{1,0:T(8,128)(2,1)S(1)}, bf16[136,640]{1,0:T(8,128)(2,1)S(1)}, u32[]{:S(2)}, u32[]{:S(2)}) collective-permute-start(bf16[136,640]{1,0:T(8,128)(2,1)S(1)} %state.3), channel_id=1, source_target_pairs={{0,4},{4,0},{8,12},{12,8},{16,20},{20,16},{24,28},{28,24},{1,5},{5... | collective-permute-start | bytes 522248 | tf_op jit(solution)/shard_map/ppermute | solution.py:550
  15.0 0.6 %state.2 = (bf16[136,640]{1,0:T(8,128)(2,1)S(1)}, f32[128,640]{1,0:T(8,128)S(1)}, f32[8,640]{1,0:T(8,128)S(1)}) custom-call(bf16[2048,640]{1,0:T(8,128)(2,1)S(1)} %get-tuple-element.32.to_total, bf16[128,2048]{1,0:T(8,128)(2,1)S(1)} %join.7.write_t, f32[80,1280]{1,0:T(8,128)S(1)} %get-tuple-element.28.rest_0_.rows.after), custom_call_target="tpu_custom_call" | custom-call | flops 335544320 | bytes 2621440 | tf_op jit(solution)/shard_map/state/pallas_call | solution.py:510
  15.6 0.0 collective-permute-done.1.second
  15.6 2.6 %local.3 = (f32[512,1280]{1,0:T(8,128)S(1)}, f32[512,1280]{1,0:T(8,128)S(1)}, f32[3,128,1280]{2,1,0:T(8,128)S(1)}) custom-call(bf16[2048,1280]{1,0:T(8,128)(2,1)S(1)} %copy-done, bf16[2048,1280]{1,0:T(8,128)(2,1)S(1)} %get-tuple-element.37.scaled, bf16[128,2048]{1,0:T(8,128)(2,1)S(1)} %join.7.write_t, bf16[128,2048]{1,0:T(8,128)(2,1)S(1)} %join.5.read_t, ...), custom_call_target="tpu_custom_call" | custom-call | flops 2621440000 | bytes 5242880 | tf_op jit(solution)/shard_map/local/pallas_call | solution.py:525
  18.3 1.8 %collective-permute-done.4.received.rest_0_ = bf16[136,640]{1,0:T(8,128)(2,1)S(1)} collective-permute-done((bf16[136,640]{1,0:T(8,128)(2,1)S(1)}, bf16[136,640]{1,0:T(8,128)(2,1)S(1)}, u32[]{:S(2)}, u32[]{:S(2)}) %collective-permute-start.4) | collective-permute-done | bytes 174112 | tf_op jit(solution)/shard_map/ppermute | solution.py:550
  20.1 0.1 merge.2
  20.2 1.8 %collective-permute-start.5 = (bf16[136,640]{1,0:T(8,128)(2,1)S(1)}, bf16[136,640]{1,0:T(8,128)(2,1)S(1)}, u32[]{:S(2)}, u32[]{:S(2)}) collective-permute-start(bf16[136,640]{1,0:T(8,128)(2,1)S(1)} %get-tuple-element.41.after), channel_id=1, source_target_pairs={{0,8},{4,12},{8,0},{12,4},{16,24},{20,28},{24,16},{28,20},{1,9},{5... | collective-permute-start | bytes 522248 | tf_op jit(solution)/shard_map/ppermute | solution.py:550
  22.0 4.5 %local.4 = (f32[768,1280]{1,0:T(8,128)S(1)}, f32[768,1280]{1,0:T(8,128)S(1)}, f32[3,128,1280]{2,1,0:T(8,128)S(1)}) custom-call(bf16[2048,1280]{1,0:T(8,128)(2,1)S(1)} %copy-done, bf16[2048,1280]{1,0:T(8,128)(2,1)S(1)} %get-tuple-element.37.scaled, bf16[128,2048]{1,0:T(8,128)(2,1)S(1)} %join.7.write_t, bf16[128,2048]{1,0:T(8,128)(2,1)S(1)} %join.5.read_t, ...), custom_call_target="tpu_custom_call" | custom-call | flops 3932160000 | bytes 7864320 | tf_op jit(solution)/shard_map/local/pallas_call | solution.py:525
  26.5 0.0 collective-permute-done.5.second.received.rest_1_
  26.5 0.1 merge.3.after
  26.6 2.7 %collective-permute-start.7 = (bf16[136,640]{1,0:T(8,128)(2,1)S(1)}, bf16[136,640]{1,0:T(8,128)(2,1)S(1)}, u32[]{:S(2)}, u32[]{:S(2)}) collective-permute-start(bf16[136,640]{1,0:T(8,128)(2,1)S(1)} %merge.3.after), channel_id=1, source_target_pairs={{0,16},{4,20},{8,24},{12,28},{16,0},{20,4},{24,8},{28,12},{1,17},{... | collective-permute-start | bytes 522248 | tf_op jit(solution)/shard_map/ppermute | solution.py:550
  29.3 1.6 %collective-permute-start.6 = (bf16[272,640]{1,0:T(8,128)(2,1)S(1)}, bf16[272,640]{1,0:T(8,128)(2,1)S(1)}, u32[]{:S(2)}, u32[]{:S(2)}) collective-permute-start(bf16[272,640]{1,0:T(8,128)(2,1)S(1)} %both.1), channel_id=1, source_target_pairs={{0,4},{4,0},{8,12},{12,8},{16,20},{20,16},{24,28},{28,24},{1,5},{5... | collective-permute-start | bytes 1044488 | tf_op jit(solution)/shard_map/ppermute | solution.py:550
  30.9 6.1 %collective-permute-done.7.rest_2_ = bf16[136,640]{1,0:T(8,128)(2,1)S(1)} collective-permute-done((bf16[136,640]{1,0:T(8,128)(2,1)S(1)}, bf16[136,640]{1,0:T(8,128)(2,1)S(1)}, u32[]{:S(2)}, u32[]{:S(2)}) %collective-permute-start.7) | collective-permute-done | bytes 174112 | tf_op jit(solution)/shard_map/ppermute | solution.py:550
  37.0 1.6 %collective-permute-start.8 = (bf16[136,640]{1,0:T(8,128)(2,1)S(1)}, bf16[136,640]{1,0:T(8,128)(2,1)S(1)}, u32[]{:S(2)}, u32[]{:S(2)}) collective-permute-start(bf16[136,640]{1,0:T(8,128)(2,1)S(1)} %collective-permute-done.7.rest_2_), channel_id=1, source_target_pairs={{0,4},{4,0},{8,12},{12,8},{16,20},{20,16},{24,28},{28,24},{1,5},{5... | collective-permute-start | bytes 522248 | tf_op jit(solution)/shard_map/ppermute | solution.py:550
  38.5 6.1 %local.5 = (f32[768,1280]{1,0:T(8,128)S(1)}, f32[768,1280]{1,0:T(8,128)S(1)}, f32[3,128,1280]{2,1,0:T(8,128)}) custom-call(bf16[2048,1280]{1,0:T(8,128)(2,1)S(1)} %copy-done, bf16[2048,1280]{1,0:T(8,128)(2,1)S(1)} %get-tuple-element.37.scaled, bf16[128,2048]{1,0:T(8,128)(2,1)S(1)} %join.7.write_t, bf16[128,2048]{1,0:T(8,128)(2,1)S(1)} %join.5.read_t, ...), custom_call_target="tpu_custom_call" | custom-call | flops 3932160000 | bytes 7864320 | tf_op jit(solution)/shard_map/local/pallas_call | solution.py:525
  44.6 2.7 %final.2.rest_6_ = bf16[2048,1280]{1,0:T(8,128)(2,1)} custom-call(bf16[128,2048]{1,0:T(8,128)(2,1)S(1)} %join.5.read_t, f32[7,2048]{1,0:T(8,128)S(1)} %get-tuple-element.29.weight_h, bf16[136,640]{1,0:T(8,128)(2,1)S(1)} %collective-permute-done.4.received.rest_0_, bf16[136,640]{1,0:T(8,128)(2,1)S(1)} %collective-permute-done.5.second.received.rest_1_, ...), custom_call_target="tpu_custom_call" | custom-call | flops 335544320 | bytes 7864320 | tf_op jit(solution)/shard_map/final/pallas_call | solution.py:610
  47.3 0.0 collective-permute-done.6.rest_0_
  47.3 1.2 %near.1.rest_2_ = f32[2048,640]{1,0:T(8,128)S(1)} custom-call(bf16[128,2048]{1,0:T(8,128)(2,1)S(1)} %join.5.read_t, f32[7,2048]{1,0:T(8,128)S(1)} %get-tuple-element.29.weight_h, bf16[272,640]{1,0:T(8,128)(2,1)S(1)} %collective-permute-done.6.rest_0_, f32[512,1280]{1,0:T(8,128)S(1)} %get-tuple-element.45.rest_1_.rest_3_, ...), custom_call_target="tpu_custom_call" | custom-call | flops 671088640 | bytes 7864320 | tf_op jit(solution)/shard_map/near/pallas_call | solution.py:628
  48.6 0.0 collective-permute-done.8.rest_1_
  48.6 1.9 %final.3 = bf16[2048,1280]{1,0:T(8,128)(2,1)} custom-call(bf16[128,2048]{1,0:T(8,128)(2,1)S(1)} %join.5.read_t, f32[7,2048]{1,0:T(8,128)S(1)} %get-tuple-element.29.weight_h, bf16[272,640]{1,0:T(8,128)(2,1)S(1)} %collective-permute-done.6.rest_0_, bf16[136,640]{1,0:T(8,128)(2,1)S(1)} %collective-permute-done.8.rest_1_, ...), custom_call_target="tpu_custom_call", output_to_operand_aliasing={{}: (8, {})} | custom-call | flops 335544320 | bytes 7864320 | tf_op jit(solution)/shard_map/final/pallas_call | solution.py:610
  (11 shorter events, 0.1 us)
Async XLA Ops:
  0.0 7.6 %copy-start.1 = (bf16[2048,32]{0,1:T(8,128)(2,1)S(1)}, bf16[2048,32]{0,1:T(8,128)(2,1)}, u32[]{:S(2)}) copy-start(bf16[2048,32]{0,1:T(8,128)(2,1)} %param.10) | copy-start | bytes 393220
  0.0 7.6 %collective-permute-start = (bf16[32,2048]{1,0:T(8,128)(2,1)}, bf16[32,2048]{1,0:T(8,128)(2,1)S(1)}, u32[]{:S(2)}, u32[]{:S(2)}) collective-permute-start(bf16[32,2048]{1,0:T(8,128)(2,1)} %bitcast.3), channel_id=1, source_target_pairs={{0,2},{1,3},{2,0},{3,1},{4,6},{5,7},{6,4},{7,5},{8,10},{9,11},{10,... | collective-permute-start | bytes 393224 | tf_op jit(solution)/shard_map/ppermute | solution.py:419
  3.0 6.6 %collective-permute-start.2 = (bf16[32,2048]{1,0:T(8,128)(2,1)}, bf16[32,2048]{1,0:T(8,128)(2,1)S(1)}, u32[]{:S(2)}, u32[]{:S(2)}) collective-permute-start(bf16[32,2048]{1,0:T(8,128)(2,1)} %bitcast.5), channel_id=1, source_target_pairs={{0,2},{1,3},{2,0},{3,1},{4,6},{5,7},{6,4},{7,5},{8,10},{9,11},{10,... | collective-permute-start | bytes 393224 | tf_op jit(solution)/shard_map/ppermute | solution.py:419
  3.0 6.5 %copy-start.2 = (bf16[2048,32]{0,1:T(8,128)(2,1)S(1)}, bf16[2048,32]{0,1:T(8,128)(2,1)}, u32[]{:S(2)}) copy-start(bf16[2048,32]{0,1:T(8,128)(2,1)} %param.9) | copy-start | bytes 393220
  3.0 6.6 %copy-start = (bf16[2048,1280]{1,0:T(8,128)(2,1)S(1)}, bf16[2048,1280]{1,0:T(8,128)(2,1)}, u32[]{:S(2)}) copy-start(bf16[2048,1280]{1,0:T(8,128)(2,1)} %mixer.9) | copy-start | bytes 15728644
  7.6 8.0 %collective-permute-start.1 = (bf16[64,2048]{1,0:T(8,128)(2,1)S(1)}, bf16[64,2048]{1,0:T(8,128)(2,1)S(1)}, u32[]{:S(2)}, u32[]{:S(2)}) collective-permute-start(bf16[64,2048]{1,0:T(8,128)(2,1)S(1)} %join.4.first), channel_id=1, source_target_pairs={{0,1},{1,0},{2,3},{3,2},{4,5},{5,4},{6,7},{7,6},{8,9},{9,8},{10,11... | collective-permute-start | bytes 786440 | tf_op jit(solution)/shard_map/ppermute | solution.py:419
  9.6 3.0 %collective-permute-start.3 = (bf16[64,2048]{1,0:T(8,128)(2,1)S(1)}, bf16[64,2048]{1,0:T(8,128)(2,1)S(1)}, u32[]{:S(2)}, u32[]{:S(2)}) collective-permute-start(bf16[64,2048]{1,0:T(8,128)(2,1)S(1)} %join.6.first), channel_id=1, source_target_pairs={{0,1},{1,0},{2,3},{3,2},{4,5},{5,4},{6,7},{7,6},{8,9},{9,8},{10,11... | collective-permute-start | bytes 786440 | tf_op jit(solution)/shard_map/ppermute | solution.py:419
  13.2 6.9 %collective-permute-start.4 = (bf16[136,640]{1,0:T(8,128)(2,1)S(1)}, bf16[136,640]{1,0:T(8,128)(2,1)S(1)}, u32[]{:S(2)}, u32[]{:S(2)}) collective-permute-start(bf16[136,640]{1,0:T(8,128)(2,1)S(1)} %state.3), channel_id=1, source_target_pairs={{0,4},{4,0},{8,12},{12,8},{16,20},{20,16},{24,28},{28,24},{1,5},{5... | collective-permute-start | bytes 522248 | tf_op jit(solution)/shard_map/ppermute | solution.py:550
  20.2 6.3 %collective-permute-start.5 = (bf16[136,640]{1,0:T(8,128)(2,1)S(1)}, bf16[136,640]{1,0:T(8,128)(2,1)S(1)}, u32[]{:S(2)}, u32[]{:S(2)}) collective-permute-start(bf16[136,640]{1,0:T(8,128)(2,1)S(1)} %get-tuple-element.41.after), channel_id=1, source_target_pairs={{0,8},{4,12},{8,0},{12,4},{16,24},{20,28},{24,16},{28,20},{1,9},{5... | collective-permute-start | bytes 522248 | tf_op jit(solution)/shard_map/ppermute | solution.py:550
  26.6 10.4 %collective-permute-start.7 = (bf16[136,640]{1,0:T(8,128)(2,1)S(1)}, bf16[136,640]{1,0:T(8,128)(2,1)S(1)}, u32[]{:S(2)}, u32[]{:S(2)}) collective-permute-start(bf16[136,640]{1,0:T(8,128)(2,1)S(1)} %merge.3.after), channel_id=1, source_target_pairs={{0,16},{4,20},{8,24},{12,28},{16,0},{20,4},{24,8},{28,12},{1,17},{... | collective-permute-start | bytes 522248 | tf_op jit(solution)/shard_map/ppermute | solution.py:550
  29.3 18.0 %collective-permute-start.6 = (bf16[272,640]{1,0:T(8,128)(2,1)S(1)}, bf16[272,640]{1,0:T(8,128)(2,1)S(1)}, u32[]{:S(2)}, u32[]{:S(2)}) collective-permute-start(bf16[272,640]{1,0:T(8,128)(2,1)S(1)} %both.1), channel_id=1, source_target_pairs={{0,4},{4,0},{8,12},{12,8},{16,20},{20,16},{24,28},{28,24},{1,5},{5... | collective-permute-start | bytes 1044488 | tf_op jit(solution)/shard_map/ppermute | solution.py:550
  37.0 11.6 %collective-permute-start.8 = (bf16[136,640]{1,0:T(8,128)(2,1)S(1)}, bf16[136,640]{1,0:T(8,128)(2,1)S(1)}, u32[]{:S(2)}, u32[]{:S(2)}) collective-permute-start(bf16[136,640]{1,0:T(8,128)(2,1)S(1)} %collective-permute-done.7.rest_2_), channel_id=1, source_target_pairs={{0,4},{4,0},{8,12},{12,8},{16,20},{20,16},{24,28},{28,24},{1,5},{5... | collective-permute-start | bytes 522248 | tf_op jit(solution)/shard_map/ppermute | solution.py:550

commit v10 on v9

--- a/solution.py
+++ b/solution.py
@@ -47,10 +47,10 @@
     return mask.astype(F32).astype(BF16)
 
 
-def spread(first_row, padded, heads, width):
-    per_head = width // heads
+def spread(first_row, padded, heads, width, per_head=None, offset=0):
+    per_head = per_head or width // heads
     row = iota((4 * padded, width), 0) - first_row
-    lane = iota((4 * padded, width), 1)
+    lane = iota((4 * padded, width), 1) + offset
     inside = (row >= 0) & (row < 2 * padded)
     row = jnp.where(row >= padded, row - padded, row)
     own = (row * per_head <= lane) & (lane < (row + 1) * per_head) & (row < heads)
@@ -157,20 +157,22 @@
 
 
 def scale_kernel(heads, padded, layout, side, mixer, factors, rows, *rest):
-    scaled, to_total, wide = rest[-3:]
+    scaled, to_total = rest[-2:]
     tokens, width = mixer.shape
     columns = own_columns(width)[side]
-    wide[...] = spread(0, padded, heads, width)
+    rank = lax.axis_index("seq")
+    first = ((rank + side) & 1) * (width // 2)
+    wide = spread(0, padded, heads, width // 2, width // heads, first)
 
     def step(a, carry):
         at = pl.ds(pl.multiple_of(a * HALF, HALF), HALF)
         row = rows[pl.ds(layout.after + a, 1), columns]
-        value = mixer[at, columns].astype(F32) * dot(factors[at, :], wide[:, columns])
+        value = mixer[at, columns].astype(F32) * dot(factors[at, :], wide)
         scaled[at, columns] = value.astype(BF16)
         to_total[at, :] = (value * row).astype(BF16)
         return carry
 
-    lax.fori_loop(0, tokens // HALF, step, 0, unroll=4)
+    lax.fori_loop(0, tokens // HALF, step, 0, unroll=8)
 
 
 def exp_rows(total, count):
@@ -501,7 +503,6 @@
             out_specs=(VMEM_SPEC,) * 2,
             out_shape=(sds((tokens, width), BF16), sds((tokens, half), BF16)),
             input_output_aliases=aliases,
-            scratch_shapes=[pltpu.VMEM((LANES, width), BF16)],
             compiler_params=grant(4),
             cost_estimate=cost(1_500_000_000, tokens * width * 3),
             name="scale",

time: 50.8 us -> 50.2 us (0.988)
  Pallas kernels: 26.5 us -> 25.9 us
    pallas_call x2, Pallas kernels: 2.88 us -> 2.3 us  [front(): pl.pallas_call(functools.partial(scale_kernel, heads, padded, layout, sid...]
where the time goes in v10:
time: 50.2 us; the launch traced here: 50 us
  Pallas kernels  25.9 us (52%)
  starting transfers between devices  12.5 us (25%)
  waiting for transfers between devices  11.3 us (23%)
    pallas_call x3, Pallas kernels, local(): pl.pallas_call(functools.partial(local_kernel, heads, padded, local_bits,...  13.2 us
    ppermute x5, starting transfers between devices, swap(): return lax.ppermute(value, 'seq', [(i, i ^ 1 << bit) for i in range(ranks)])  9.34 us
    ppermute x5, waiting for transfers between devices, swap(): return lax.ppermute(value, 'seq', [(i, i ^ 1 << bit) for i in range(ranks)])  7.92 us
    pallas_call x2, Pallas kernels, finish(): pl.pallas_call(functools.partial(final_kernel, starts, local_bits, device...  4.61 us
    ppermute x4, waiting for transfers between devices, gather_columns(): other = lax.ppermute(pieces, axis, [(i, i ^ stride) for i in range(size)])  3.38 us
    ppermute x4, starting transfers between devices, gather_columns(): other = lax.ppermute(pieces, axis, [(i, i ^ stride) for i in range(size)])  3.17 us
    pallas_call x1, Pallas kernels, on_device(): pl.pallas_call(functools.partial(prep_kernel, heads, padded, layout), in_...  3.03 us
    pallas_call x2, Pallas kernels, front(): pl.pallas_call(functools.partial(scale_kernel, heads, padded, layout, sid...  2.3 us
  transfers between devices with their start and end apart: 9, of which 4 were waited for; matrix products, arithmetic and copies ran while one was open for 0% of the time, Pallas kernels for 48%

profile of v10, /device:TPU:0, one launch (start us, length us, event | category | flops | bytes accessed | tf_op | source)
XLA Modules:
  0.0 50.0 jit_solution(5950058851642455894)
XLA Ops:
  0.0 3.0 %collective-permute-start = (bf16[32,2048]{1,0:T(8,128)(2,1)}, bf16[32,2048]{1,0:T(8,128)(2,1)S(1)}, u32[]{:S(2)}, u32[]{:S(2)}) collective-permute-start(bf16[32,2048]{1,0:T(8,128)(2,1)} %bitcast.3), channel_id=1, source_target_pairs={{0,2},{1,3},{2,0},{3,1},{4,6},{5,7},{6,4},{7,5},{8,10},{9,11},{10,... | collective-permute-start | bytes 393224 | tf_op jit(solution)/shard_map/ppermute | solution.py:421
  3.0 0.1 collective-permute-start.2
  3.0 3.0 %prep.1 = (bf16[2048,128]{1,0:T(8,128)(2,1)S(1)}, f32[2048,128]{1,0:T(8,128)S(1)}, f32[32,2048]{1,0:T(8,128)S(1)}, f32[7,2048]{1,0:T(8,128)S(1)}, f32[80,1280]{1,0:T(8,128)S(1)}) custom-call(f32[20,2048]{1,0:T(8,128)} %log_decay_far.1, f32[20,2048]{1,0:T(8,128)} %step_size_far.1, s32[7,2048]{1,0:T(8,128)} %level_index_far.1, f32[7,8]{1,0:T(8,128)} %level_table_far.1, ...), custom_call_target="tpu_custom_call" | custom-call | flops 2000000000 | bytes 4000000 | tf_op jit(solution)/shard_map/prep/pallas_call | solution.py:458
  6.1 1.5 %collective-permute-done.second = bf16[32,2048]{1,0:T(8,128)(2,1)S(1)} collective-permute-done((bf16[32,2048]{1,0:T(8,128)(2,1)}, bf16[32,2048]{1,0:T(8,128)(2,1)S(1)}, u32[]{:S(2)}, u32[]{:S(2)}) %collective-permute-start) | collective-permute-done | bytes 131104 | tf_op jit(solution)/shard_map/ppermute | solution.py:421
  7.6 0.0 copy-done.1
  7.6 0.1 collective-permute-start.1
  7.7 1.9 %collective-permute-done.2.second = bf16[32,2048]{1,0:T(8,128)(2,1)S(1)} collective-permute-done((bf16[32,2048]{1,0:T(8,128)(2,1)}, bf16[32,2048]{1,0:T(8,128)(2,1)S(1)}, u32[]{:S(2)}, u32[]{:S(2)}) %collective-permute-start.2) | collective-permute-done | bytes 131104 | tf_op jit(solution)/shard_map/ppermute | solution.py:421
  9.6 0.1 collective-permute-start.3
  9.7 1.2 %scale.2 = (bf16[2048,1280]{1,0:T(8,128)(2,1)S(1)}, bf16[2048,640]{1,0:T(8,128)(2,1)S(1)}) custom-call(bf16[2048,1280]{1,0:T(8,128)(2,1)S(1)} %copy-done, bf16[2048,128]{1,0:T(8,128)(2,1)S(1)} %get-tuple-element.30.factors, f32[80,1280]{1,0:T(8,128)S(1)} %get-tuple-element.28.rest_0_.rows.after), custom_call_target="tpu_custom_call" | custom-call | flops 1500000000 | bytes 7864320 | tf_op jit(solution)/shard_map/scale/pallas_call | solution.py:500
  10.8 1.1 %scale.3 = (bf16[2048,1280]{1,0:T(8,128)(2,1)S(1)}, bf16[2048,640]{1,0:T(8,128)(2,1)S(1)}) custom-call(bf16[2048,1280]{1,0:T(8,128)(2,1)S(1)} %copy-done, bf16[2048,128]{1,0:T(8,128)(2,1)S(1)} %get-tuple-element.30.factors, f32[80,1280]{1,0:T(8,128)S(1)} %get-tuple-element.28.rest_0_.rows.after, ...), custom_call_target="tpu_custom_call", output_to_operand_aliasing={{0}: (3, {})} | custom-call | flops 1500000000 | bytes 7864320 | tf_op jit(solution)/shard_map/scale/pallas_call | solution.py:500
  12.0 0.0 collective-permute-done.3.second
  12.0 0.6 %state.3 = bf16[136,640]{1,0:T(8,128)(2,1)S(1)} custom-call(bf16[2048,640]{1,0:T(8,128)(2,1)S(1)} %get-tuple-element.34.to_total, bf16[128,2048]{1,0:T(8,128)(2,1)S(1)} %join.7.write_t, f32[80,1280]{1,0:T(8,128)S(1)} %get-tuple-element.28.rest_0_.rows.after), custom_call_target="tpu_custom_call" | custom-call | flops 335544320 | bytes 2621440 | tf_op jit(solution)/shard_map/state/pallas_call | solution.py:511
  12.6 1.8 %collective-permute-start.4 = (bf16[136,640]{1,0:T(8,128)(2,1)S(1)}, bf16[136,640]{1,0:T(8,128)(2,1)S(1)}, u32[]{:S(2)}, u32[]{:S(2)}) collective-permute-start(bf16[136,640]{1,0:T(8,128)(2,1)S(1)} %state.3), channel_id=1, source_target_pairs={{0,4},{4,0},{8,12},{12,8},{16,20},{20,16},{24,28},{28,24},{1,5},{5... | collective-permute-start | bytes 522248 | tf_op jit(solution)/shard_map/ppermute | solution.py:551
  14.4 0.6 %state.2 = (bf16[136,640]{1,0:T(8,128)(2,1)S(1)}, f32[128,640]{1,0:T(8,128)S(1)}, f32[8,640]{1,0:T(8,128)S(1)}) custom-call(bf16[2048,640]{1,0:T(8,128)(2,1)S(1)} %get-tuple-element.32.to_total, bf16[128,2048]{1,0:T(8,128)(2,1)S(1)} %join.7.write_t, f32[80,1280]{1,0:T(8,128)S(1)} %get-tuple-element.28.rest_0_.rows.after), custom_call_target="tpu_custom_call" | custom-call | flops 335544320 | bytes 2621440 | tf_op jit(solution)/shard_map/state/pallas_call | solution.py:511
  15.0 0.0 collective-permute-done.1.second
  15.1 2.6 %local.3 = (f32[512,1280]{1,0:T(8,128)S(1)}, f32[512,1280]{1,0:T(8,128)S(1)}, f32[3,128,1280]{2,1,0:T(8,128)S(1)}) custom-call(bf16[2048,1280]{1,0:T(8,128)(2,1)S(1)} %copy-done, bf16[2048,1280]{1,0:T(8,128)(2,1)S(1)} %get-tuple-element.37.scaled, bf16[128,2048]{1,0:T(8,128)(2,1)S(1)} %join.7.write_t, bf16[128,2048]{1,0:T(8,128)(2,1)S(1)} %join.5.read_t, ...), custom_call_target="tpu_custom_call" | custom-call | flops 2621440000 | bytes 5242880 | tf_op jit(solution)/shard_map/local/pallas_call | solution.py:526
  17.7 1.8 %collective-permute-done.4.received.rest_0_ = bf16[136,640]{1,0:T(8,128)(2,1)S(1)} collective-permute-done((bf16[136,640]{1,0:T(8,128)(2,1)S(1)}, bf16[136,640]{1,0:T(8,128)(2,1)S(1)}, u32[]{:S(2)}, u32[]{:S(2)}) %collective-permute-start.4) | collective-permute-done | bytes 174112 | tf_op jit(solution)/shard_map/ppermute | solution.py:551
  19.5 0.1 merge.2
  19.6 1.8 %collective-permute-start.5 = (bf16[136,640]{1,0:T(8,128)(2,1)S(1)}, bf16[136,640]{1,0:T(8,128)(2,1)S(1)}, u32[]{:S(2)}, u32[]{:S(2)}) collective-permute-start(bf16[136,640]{1,0:T(8,128)(2,1)S(1)} %get-tuple-element.41.after), channel_id=1, source_target_pairs={{0,8},{4,12},{8,0},{12,4},{16,24},{20,28},{24,16},{28,20},{1,9},{5... | collective-permute-start | bytes 522248 | tf_op jit(solution)/shard_map/ppermute | solution.py:551
  21.4 4.5 %local.4 = (f32[768,1280]{1,0:T(8,128)S(1)}, f32[768,1280]{1,0:T(8,128)S(1)}, f32[3,128,1280]{2,1,0:T(8,128)S(1)}) custom-call(bf16[2048,1280]{1,0:T(8,128)(2,1)S(1)} %copy-done, bf16[2048,1280]{1,0:T(8,128)(2,1)S(1)} %get-tuple-element.37.scaled, bf16[128,2048]{1,0:T(8,128)(2,1)S(1)} %join.7.write_t, bf16[128,2048]{1,0:T(8,128)(2,1)S(1)} %join.5.read_t, ...), custom_call_target="tpu_custom_call" | custom-call | flops 3932160000 | bytes 7864320 | tf_op jit(solution)/shard_map/local/pallas_call | solution.py:526
  25.9 0.0 collective-permute-done.5.second.received.rest_1_
  25.9 0.1 merge.3.after
  26.0 2.6 %collective-permute-start.7 = (bf16[136,640]{1,0:T(8,128)(2,1)S(1)}, bf16[136,640]{1,0:T(8,128)(2,1)S(1)}, u32[]{:S(2)}, u32[]{:S(2)}) collective-permute-start(bf16[136,640]{1,0:T(8,128)(2,1)S(1)} %merge.3.after), channel_id=1, source_target_pairs={{0,16},{4,20},{8,24},{12,28},{16,0},{20,4},{24,8},{28,12},{1,17},{... | collective-permute-start | bytes 522248 | tf_op jit(solution)/shard_map/ppermute | solution.py:551
  28.7 1.6 %collective-permute-start.6 = (bf16[272,640]{1,0:T(8,128)(2,1)S(1)}, bf16[272,640]{1,0:T(8,128)(2,1)S(1)}, u32[]{:S(2)}, u32[]{:S(2)}) collective-permute-start(bf16[272,640]{1,0:T(8,128)(2,1)S(1)} %both.1), channel_id=1, source_target_pairs={{0,4},{4,0},{8,12},{12,8},{16,20},{20,16},{24,28},{28,24},{1,5},{5... | collective-permute-start | bytes 1044488 | tf_op jit(solution)/shard_map/ppermute | solution.py:551
  30.3 6.1 %collective-permute-done.7.rest_2_ = bf16[136,640]{1,0:T(8,128)(2,1)S(1)} collective-permute-done((bf16[136,640]{1,0:T(8,128)(2,1)S(1)}, bf16[136,640]{1,0:T(8,128)(2,1)S(1)}, u32[]{:S(2)}, u32[]{:S(2)}) %collective-permute-start.7) | collective-permute-done | bytes 174112 | tf_op jit(solution)/shard_map/ppermute | solution.py:551
  36.4 1.5 %collective-permute-start.8 = (bf16[136,640]{1,0:T(8,128)(2,1)S(1)}, bf16[136,640]{1,0:T(8,128)(2,1)S(1)}, u32[]{:S(2)}, u32[]{:S(2)}) collective-permute-start(bf16[136,640]{1,0:T(8,128)(2,1)S(1)} %collective-permute-done.7.rest_2_), channel_id=1, source_target_pairs={{0,4},{4,0},{8,12},{12,8},{16,20},{20,16},{24,28},{28,24},{1,5},{5... | collective-permute-start | bytes 522248 | tf_op jit(solution)/shard_map/ppermute | solution.py:551
  37.9 6.1 %local.5 = (f32[768,1280]{1,0:T(8,128)S(1)}, f32[768,1280]{1,0:T(8,128)S(1)}, f32[3,128,1280]{2,1,0:T(8,128)}) custom-call(bf16[2048,1280]{1,0:T(8,128)(2,1)S(1)} %copy-done, bf16[2048,1280]{1,0:T(8,128)(2,1)S(1)} %get-tuple-element.37.scaled, bf16[128,2048]{1,0:T(8,128)(2,1)S(1)} %join.7.write_t, bf16[128,2048]{1,0:T(8,128)(2,1)S(1)} %join.5.read_t, ...), custom_call_target="tpu_custom_call" | custom-call | flops 3932160000 | bytes 7864320 | tf_op jit(solution)/shard_map/local/pallas_call | solution.py:526
  44.0 2.7 %final.2.rest_6_ = bf16[2048,1280]{1,0:T(8,128)(2,1)} custom-call(bf16[128,2048]{1,0:T(8,128)(2,1)S(1)} %join.5.read_t, f32[7,2048]{1,0:T(8,128)S(1)} %get-tuple-element.29.weight_h, bf16[136,640]{1,0:T(8,128)(2,1)S(1)} %collective-permute-done.4.received.rest_0_, bf16[136,640]{1,0:T(8,128)(2,1)S(1)} %collective-permute-done.5.second.received.rest_1_, ...), custom_call_target="tpu_custom_call" | custom-call | flops 335544320 | bytes 7864320 | tf_op jit(solution)/shard_map/final/pallas_call | solution.py:611
  46.7 0.0 collective-permute-done.6.rest_0_
  46.7 1.2 %near.1.rest_2_ = f32[2048,640]{1,0:T(8,128)S(1)} custom-call(bf16[128,2048]{1,0:T(8,128)(2,1)S(1)} %join.5.read_t, f32[7,2048]{1,0:T(8,128)S(1)} %get-tuple-element.29.weight_h, bf16[272,640]{1,0:T(8,128)(2,1)S(1)} %collective-permute-done.6.rest_0_, f32[512,1280]{1,0:T(8,128)S(1)} %get-tuple-element.45.rest_1_.rest_3_, ...), custom_call_target="tpu_custom_call" | custom-call | flops 671088640 | bytes 7864320 | tf_op jit(solution)/shard_map/near/pallas_call | solution.py:629
  47.9 0.0 collective-permute-done.8.rest_1_
  47.9 1.9 %final.3 = bf16[2048,1280]{1,0:T(8,128)(2,1)} custom-call(bf16[128,2048]{1,0:T(8,128)(2,1)S(1)} %join.5.read_t, f32[7,2048]{1,0:T(8,128)S(1)} %get-tuple-element.29.weight_h, bf16[272,640]{1,0:T(8,128)(2,1)S(1)} %collective-permute-done.6.rest_0_, bf16[136,640]{1,0:T(8,128)(2,1)S(1)} %collective-permute-done.8.rest_1_, ...), custom_call_target="tpu_custom_call", output_to_operand_aliasing={{}: (8, {})} | custom-call | flops 335544320 | bytes 7864320 | tf_op jit(solution)/shard_map/final/pallas_call | solution.py:611
  (11 shorter events, 0.1 us)
Async XLA Ops:
  0.0 7.6 %copy-start.1 = (bf16[2048,32]{0,1:T(8,128)(2,1)S(1)}, bf16[2048,32]{0,1:T(8,128)(2,1)}, u32[]{:S(2)}) copy-start(bf16[2048,32]{0,1:T(8,128)(2,1)} %param.10) | copy-start | bytes 393220
  0.0 7.6 %collective-permute-start = (bf16[32,2048]{1,0:T(8,128)(2,1)}, bf16[32,2048]{1,0:T(8,128)(2,1)S(1)}, u32[]{:S(2)}, u32[]{:S(2)}) collective-permute-start(bf16[32,2048]{1,0:T(8,128)(2,1)} %bitcast.3), channel_id=1, source_target_pairs={{0,2},{1,3},{2,0},{3,1},{4,6},{5,7},{6,4},{7,5},{8,10},{9,11},{10,... | collective-permute-start | bytes 393224 | tf_op jit(solution)/shard_map/ppermute | solution.py:421
  3.0 6.6 %collective-permute-start.2 = (bf16[32,2048]{1,0:T(8,128)(2,1)}, bf16[32,2048]{1,0:T(8,128)(2,1)S(1)}, u32[]{:S(2)}, u32[]{:S(2)}) collective-permute-start(bf16[32,2048]{1,0:T(8,128)(2,1)} %bitcast.5), channel_id=1, source_target_pairs={{0,2},{1,3},{2,0},{3,1},{4,6},{5,7},{6,4},{7,5},{8,10},{9,11},{10,... | collective-permute-start | bytes 393224 | tf_op jit(solution)/shard_map/ppermute | solution.py:421
  3.0 6.5 %copy-start.2 = (bf16[2048,32]{0,1:T(8,128)(2,1)S(1)}, bf16[2048,32]{0,1:T(8,128)(2,1)}, u32[]{:S(2)}) copy-start(bf16[2048,32]{0,1:T(8,128)(2,1)} %param.9) | copy-start | bytes 393220
  3.0 6.6 %copy-start = (bf16[2048,1280]{1,0:T(8,128)(2,1)S(1)}, bf16[2048,1280]{1,0:T(8,128)(2,1)}, u32[]{:S(2)}) copy-start(bf16[2048,1280]{1,0:T(8,128)(2,1)} %mixer.9) | copy-start | bytes 15728644
  7.6 7.4 %collective-permute-start.1 = (bf16[64,2048]{1,0:T(8,128)(2,1)S(1)}, bf16[64,2048]{1,0:T(8,128)(2,1)S(1)}, u32[]{:S(2)}, u32[]{:S(2)}) collective-permute-start(bf16[64,2048]{1,0:T(8,128)(2,1)S(1)} %join.4.first), channel_id=1, source_target_pairs={{0,1},{1,0},{2,3},{3,2},{4,5},{5,4},{6,7},{7,6},{8,9},{9,8},{10,11... | collective-permute-start | bytes 786440 | tf_op jit(solution)/shard_map/ppermute | solution.py:421
  9.6 2.4 %collective-permute-start.3 = (bf16[64,2048]{1,0:T(8,128)(2,1)S(1)}, bf16[64,2048]{1,0:T(8,128)(2,1)S(1)}, u32[]{:S(2)}, u32[]{:S(2)}) collective-permute-start(bf16[64,2048]{1,0:T(8,128)(2,1)S(1)} %join.6.first), channel_id=1, source_target_pairs={{0,1},{1,0},{2,3},{3,2},{4,5},{5,4},{6,7},{7,6},{8,9},{9,8},{10,11... | collective-permute-start | bytes 786440 | tf_op jit(solution)/shard_map/ppermute | solution.py:421
  12.6 6.9 %collective-permute-start.4 = (bf16[136,640]{1,0:T(8,128)(2,1)S(1)}, bf16[136,640]{1,0:T(8,128)(2,1)S(1)}, u32[]{:S(2)}, u32[]{:S(2)}) collective-permute-start(bf16[136,640]{1,0:T(8,128)(2,1)S(1)} %state.3), channel_id=1, source_target_pairs={{0,4},{4,0},{8,12},{12,8},{16,20},{20,16},{24,28},{28,24},{1,5},{5... | collective-permute-start | bytes 522248 | tf_op jit(solution)/shard_map/ppermute | solution.py:551
  19.6 6.3 %collective-permute-start.5 = (bf16[136,640]{1,0:T(8,128)(2,1)S(1)}, bf16[136,640]{1,0:T(8,128)(2,1)S(1)}, u32[]{:S(2)}, u32[]{:S(2)}) collective-permute-start(bf16[136,640]{1,0:T(8,128)(2,1)S(1)} %get-tuple-element.41.after), channel_id=1, source_target_pairs={{0,8},{4,12},{8,0},{12,4},{16,24},{20,28},{24,16},{28,20},{1,9},{5... | collective-permute-start | bytes 522248 | tf_op jit(solution)/shard_map/ppermute | solution.py:551
  26.0 10.4 %collective-permute-start.7 = (bf16[136,640]{1,0:T(8,128)(2,1)S(1)}, bf16[136,640]{1,0:T(8,128)(2,1)S(1)}, u32[]{:S(2)}, u32[]{:S(2)}) collective-permute-start(bf16[136,640]{1,0:T(8,128)(2,1)S(1)} %merge.3.after), channel_id=1, source_target_pairs={{0,16},{4,20},{8,24},{12,28},{16,0},{20,4},{24,8},{28,12},{1,17},{... | collective-permute-start | bytes 522248 | tf_op jit(solution)/shard_map/ppermute | solution.py:551
  28.7 18.0 %collective-permute-start.6 = (bf16[272,640]{1,0:T(8,128)(2,1)S(1)}, bf16[272,640]{1,0:T(8,128)(2,1)S(1)}, u32[]{:S(2)}, u32[]{:S(2)}) collective-permute-start(bf16[272,640]{1,0:T(8,128)(2,1)S(1)} %both.1), channel_id=1, source_target_pairs={{0,4},{4,0},{8,12},{12,8},{16,20},{20,16},{24,28},{28,24},{1,5},{5... | collective-permute-start | bytes 1044488 | tf_op jit(solution)/shard_map/ppermute | solution.py:551
  36.4 11.5 %collective-permute-start.8 = (bf16[136,640]{1,0:T(8,128)(2,1)S(1)}, bf16[136,640]{1,0:T(8,128)(2,1)S(1)}, u32[]{:S(2)}, u32[]{:S(2)}) collective-permute-start(bf16[136,640]{1,0:T(8,128)(2,1)S(1)} %collective-permute-done.7.rest_2_), channel_id=1, source_target_pairs={{0,4},{4,0},{8,12},{12,8},{16,20},{20,16},{24,28},{28,24},{1,5},{5... | collective-permute-start | bytes 522248 | tf_op jit(solution)/shard_map/ppermute | solution.py:551
